TPU v7x, 32 devices: a whole 2x2x4 slice. The times are simulated.
32 devices in a mesh: batch: 4 (over y, x), vocab: 8 (over z, core).
Axes of the slice: x: 2, y: 2, z: 4, core: 2. Of those that a mesh axis runs over, the one named last changes fastest.
Arguments:
- tokens: int32 [32768], P('batch'), may hold values from 0 to 51199
- targets: int32 [4096], P('batch'), may hold values from 0 to 51199
- segments: int32 [32768], P(('batch', 'vocab')), may hold values from 0 to 2, as said below
- counted: int32 [4096], P(('batch', 'vocab')), may hold values from 0 to 1023, as said below
- vocab_mask: int32 [51200], P('vocab'), may hold values 0 or 1
- step_count: int32 [1], replicated, may hold values from 2 to 20
- table: float32 [51200, 768], P('vocab', 'batch'), may hold values from -0.4375 to 0.4375
- table_moment: float32 [51200, 768], P('vocab', 'batch'), may hold values from -2.3841858e-06 to 2.3841858e-06
- table_square: float32 [51200, 768], P('vocab', 'batch'), may hold values from 2.1549823e-15 to 8.619929e-15
- attend: float32 [1, 768, 2304], P(None, 'batch'), may hold values from -0.21875 to 0.21875
- attend_moment: float32 [1, 768, 2304], P(None, 'batch'), may hold values from -4.7683716e-06 to 4.7683716e-06
- attend_square: float32 [1, 768, 2304], P(None, 'batch'), may hold values from 8.619929e-15 to 3.4479716e-14
- project: float32 [1, 768, 768], P(None, 'batch'), may hold values from -0.875 to 0.875
- project_moment: float32 [1, 768, 768], P(None, 'batch'), may hold values from -4.7683716e-06 to 4.7683716e-06
- project_square: float32 [1, 768, 768], P(None, 'batch'), may hold values from 8.619929e-15 to 3.4479716e-14
- expand: float32 [1, 768, 3072], P(None, 'batch'), may hold values from -0.21875 to 0.21875
- expand_moment: float32 [1, 768, 3072], P(None, 'batch'), may hold values from -4.7683716e-06 to 4.7683716e-06
- expand_square: float32 [1, 768, 3072], P(None, 'batch'), may hold values from 8.619929e-15 to 3.4479716e-14
- contract: float32 [1, 3072, 768], P(None, 'batch'), may hold values from -0.109375 to 0.109375
- contract_moment: float32 [1, 3072, 768], P(None, 'batch'), may hold values from -4.7683716e-06 to 4.7683716e-06
- contract_square: float32 [1, 3072, 768], P(None, 'batch'), may hold values from 8.619929e-15 to 3.4479716e-14
- gain: float32 [3, 768], P(None, 'batch'), may hold values from 0.5 to 1.5
- gain_moment: float32 [3, 768], P(None, 'batch'), may hold values from -2.2888184e-05 to 2.2888184e-05
- gain_square: float32 [3, 768], P(None, 'batch'), may hold values from 2.1549822e-13 to 8.619929e-13
- shift: float32 [3, 768], P(None, 'batch'), may hold values from -1 to 1
- shift_moment: float32 [3, 768], P(None, 'batch'), may hold values from -2.2888184e-05 to 2.2888184e-05
- shift_square: float32 [3, 768], P(None, 'batch'), may hold values from 2.1549822e-13 to 8.619929e-13
Outputs:
- loss: float32 [], replicated
- gradient_norm: float32 [], replicated
- table_after: float32 [51200, 768], P('vocab', 'batch')
- table_first: float32 [51200, 768], P('vocab', 'batch')
- table_second: float32 [51200, 768], P('vocab', 'batch')
- attend_after: float32 [1, 768, 2304], P(None, 'batch')
- attend_first: float32 [1, 768, 2304], P(None, 'batch')
- attend_second: float32 [1, 768, 2304], P(None, 'batch')
- project_after: float32 [1, 768, 768], P(None, 'batch')
- project_first: float32 [1, 768, 768], P(None, 'batch')
- project_second: float32 [1, 768, 768], P(None, 'batch')
- expand_after: float32 [1, 768, 3072], P(None, 'batch')
- expand_first: float32 [1, 768, 3072], P(None, 'batch')
- expand_second: float32 [1, 768, 3072], P(None, 'batch')
- contract_after: float32 [1, 3072, 768], P(None, 'batch')
- contract_first: float32 [1, 3072, 768], P(None, 'batch')
- contract_second: float32 [1, 3072, 768], P(None, 'batch')
- gain_after: float32 [3, 768], P(None, 'batch')
- gain_first: float32 [3, 768], P(None, 'batch')
- gain_second: float32 [3, 768], P(None, 'batch')
- shift_after: float32 [3, 768], P(None, 'batch')
- shift_first: float32 [3, 768], P(None, 'batch')
- shift_second: float32 [3, 768], P(None, 'batch')
Inputs may be any that keep to these rules, and one draw needn't show every extreme that they name: Each sequence of 1024 tokens is cut into three segments, numbered 0, 1, 2 in order: one of 512 tokens and two of 256 tokens, in any order. Each sequence has 128 counted positions, the k-th among positions 8 k to 8 k + 7; the first is 0 and the last 1023.
All inputs are finite; a program needn't handle non-finite values. No bound on the sum of `vocab_mask` on one device may be relied on, other than what follows from the above.
Results may differ from a plain program's by a relative error of at most 0.022.
Values may be sent and summed in bfloat16 or wider, within the bound.
A program may use at most 448 MiB of HBM per device.

v0:
```python
import jax
import jax.numpy as jnp
from jax import lax
from jax.sharding import PartitionSpec as P

D = 768
H = 12
HD = 64
NB = 256
SEG_BLOCKS = 4
LAYERS = 1
SEQ_LEN = 1024


NORM_EPS = 1e-05
MAX_NORM = 0.02
LEARN_RATE = 0.04
NORM_RATE = 0.5
BETA_ONE = 0.9
BETA_TWO = 0.999
ADAM_EPS = 1e-08
DECAY = 0.1
NEG_BIG = -1e30
BF = jnp.bfloat16
FL = jnp.float32


def layer_norm(value, gain, shift):
    centre = value - jnp.mean(value, axis=-1, keepdims=True)
    spread = jnp.mean(centre * centre, axis=-1, keepdims=True)
    return centre * lax.rsqrt(spread + NORM_EPS) * gain + shift


def norm_back(value, gain, shift, upstream):
    unused, pullback = jax.vjp(layer_norm, value, gain, shift)
    return pullback(upstream)


def gelu_tanh(value):
    return jax.nn.gelu(value, approximate=True)


def memory_weights(segments):
    length = segments.shape[0]
    slots = SEG_BLOCKS - 2
    places = jnp.arange(length, dtype=jnp.int32)
    slot_ids = jnp.arange(slots, dtype=jnp.int32)
    inside = segments[None, :] == slot_ids[:, None]
    starts = jnp.sum((segments[None, :] < slot_ids[:, None]).astype(jnp.int32), axis=1)
    counts = jnp.sum(inside.astype(jnp.int32), axis=1)
    times = ((places[None, :] - starts[:, None]).astype(FL) + 0.5) / jnp.maximum(counts, 1)[
        :, None
    ].astype(FL)
    centres = (jnp.arange(NB, dtype=FL) + 0.5) / NB
    offset = (times[:, None, :] - centres[None, :, None]) * NB
    basis = jnp.exp(-0.5 * offset * offset) * inside[:, None, :].astype(FL)
    total = jnp.sum(basis, axis=2, keepdims=True) + (counts == 0).astype(FL)[:, None, None]
    return (basis / total).reshape(slots * NB, length)


def key_layout(segments):
    slots = SEG_BLOCKS - 2
    memory_seg = jnp.repeat(jnp.arange(slots, dtype=jnp.int32) + 1, NB)
    key_seg = jnp.concatenate(
        [jnp.broadcast_to(memory_seg, (segments.shape[0], slots * NB)), segments], axis=1
    )
    key_pos = jnp.concatenate(
        [jnp.full((slots * NB,), -1, jnp.int32), jnp.arange(segments.shape[1], dtype=jnp.int32)]
    )
    return (key_seg, key_pos)


def split_heads(projected, memory_kv):
    batch, length = (projected.shape[0], projected.shape[1])
    queries = projected[..., :D].reshape(batch, length, H, HD)
    keys = jnp.concatenate([memory_kv[..., :D], projected[..., D : 2 * D]], axis=1).reshape(
        batch, -1, H, HD
    )
    values = jnp.concatenate([memory_kv[..., D:], projected[..., 2 * D :]], axis=1).reshape(
        batch, -1, H, HD
    )
    return (queries, keys, values)


def block_scores(query_block, keys, start, context):
    segments, key_seg, key_pos = context
    rows = query_block.shape[1]
    scores = jnp.einsum("bqhd,bkhd->bhqk", query_block, keys, preferred_element_type=FL) * HD ** (
        -0.5
    )
    query_seg = lax.dynamic_slice_in_dim(segments, start, rows, 1)
    query_pos = start + jnp.arange(rows, dtype=jnp.int32)
    visible = (key_seg[:, None, :] == query_seg[:, :, None]) & (
        key_pos[None, None, :] <= query_pos[None, :, None]
    )
    return jnp.where(visible[:, None], scores, NEG_BIG)


def attend_forward(queries, keys, values, context):
    batch, length = (queries.shape[0], queries.shape[1])
    rows = min(512, length)

    def one_block(index):
        start = index * rows
        query_block = lax.dynamic_slice_in_dim(queries, start, rows, 1)
        scores = block_scores(query_block, keys, start, context)
        peak = jnp.max(scores, axis=-1, keepdims=True)
        expo = jnp.exp(scores - peak)
        total = jnp.sum(expo, axis=-1, keepdims=True)
        probs = (expo / total).astype(BF)
        mixed = jnp.einsum("bhqk,bkhd->bqhd", probs, values, preferred_element_type=FL).astype(BF)
        return (mixed, (peak + jnp.log(total))[..., 0])

    mixed, log_norm = lax.map(one_block, jnp.arange(length // rows))
    mixed = jnp.moveaxis(mixed, 0, 1).reshape(batch, length, D)
    log_norm = jnp.moveaxis(log_norm, 0, 2).reshape(batch, H, length)
    return (mixed, log_norm)


def attend_backward(queries, keys, values, log_norm, grad_mixed, context):
    batch, length = (queries.shape[0], queries.shape[1])
    rows = min(512, length)
    scale = HD ** (-0.5)

    def one_block(carry, index):
        grad_keys, grad_values = carry
        start = index * rows
        query_block = lax.dynamic_slice_in_dim(queries, start, rows, 1)
        grad_block = lax.dynamic_slice_in_dim(grad_mixed, start, rows, 1)
        norm_block = lax.dynamic_slice_in_dim(log_norm, start, rows, 2)
        scores = block_scores(query_block, keys, start, context)
        probs = jnp.exp(scores - norm_block[..., None])
        grad_probs = jnp.einsum("bqhd,bkhd->bhqk", grad_block, values, preferred_element_type=FL)
        inner = jnp.sum(probs * grad_probs, axis=-1, keepdims=True)
        grad_scores = (probs * (grad_probs - inner)).astype(BF)
        grad_query = (
            jnp.einsum("bhqk,bkhd->bqhd", grad_scores, keys, preferred_element_type=FL) * scale
        )
        grad_keys = (
            grad_keys
            + jnp.einsum("bhqk,bqhd->bkhd", grad_scores, query_block, preferred_element_type=FL)
            * scale
        )
        grad_values = grad_values + jnp.einsum(
            "bhqk,bqhd->bkhd", probs.astype(BF), grad_block, preferred_element_type=FL
        )
        return ((grad_keys, grad_values), grad_query)

    empty = jnp.zeros(keys.shape, FL)
    (grad_keys, grad_values), grad_query = lax.scan(
        one_block, (empty, empty), jnp.arange(length // rows)
    )
    grad_query = jnp.moveaxis(grad_query, 0, 1).reshape(batch, length, D)
    return (grad_query, grad_keys, grad_values)


def layer_forward(state, layer, weights, mixing, context):
    attend_all, project_all, expand_all, contract_all, gain_all, shift_all = weights
    normed = layer_norm(state, gain_all[2 * layer], shift_all[2 * layer]).astype(BF)
    projected = jnp.einsum(
        "bsd,de->bse", normed, attend_all[layer], preferred_element_type=FL
    ).astype(BF)
    memory = jnp.einsum("bms,bsd->bmd", mixing, normed, preferred_element_type=FL).astype(BF)
    memory_kv = jnp.einsum(
        "bmd,de->bme", memory, attend_all[layer][:, D:], preferred_element_type=FL
    ).astype(BF)
    queries, keys, values = split_heads(projected, memory_kv)
    mixed, log_norm = attend_forward(queries, keys, values, context)
    state_one = state + jnp.einsum(
        "bsd,de->bse", mixed, project_all[layer], preferred_element_type=FL
    )
    normed_two = layer_norm(state_one, gain_all[2 * layer + 1], shift_all[2 * layer + 1]).astype(BF)
    inner = jnp.einsum("bsd,df->bsf", normed_two, expand_all[layer], preferred_element_type=FL)
    active = gelu_tanh(inner).astype(BF)
    state_two = state_one + jnp.einsum(
        "bsf,fd->bsd", active, contract_all[layer], preferred_element_type=FL
    )
    kept = (
        state,
        normed,
        projected,
        memory,
        memory_kv,
        mixed,
        log_norm,
        state_one,
        normed_two,
        inner,
        active,
    )
    return (state_two, kept)


def layer_backward(grad_out, kept, layer, weights, mixing, context):
    attend_all, project_all, expand_all, contract_all, gain_all, shift_all = weights
    (
        state,
        normed,
        projected,
        memory,
        memory_kv,
        mixed,
        log_norm,
        state_one,
        normed_two,
        inner,
        active,
    ) = kept
    batch, length = (state.shape[0], state.shape[1])
    grad_low = grad_out.astype(BF)
    grad_contract = jnp.einsum("bsf,bsd->fd", active, grad_low, preferred_element_type=FL)
    grad_active = jnp.einsum(
        "bsd,fd->bsf", grad_low, contract_all[layer], preferred_element_type=FL
    )
    unused, gelu_pull = jax.vjp(gelu_tanh, inner)
    grad_inner = gelu_pull(grad_active)[0].astype(BF)
    grad_expand = jnp.einsum("bsd,bsf->df", normed_two, grad_inner, preferred_element_type=FL)
    grad_normed_two = jnp.einsum(
        "bsf,df->bsd", grad_inner, expand_all[layer], preferred_element_type=FL
    )
    grad_one, gain_two, shift_two = norm_back(
        state_one, gain_all[2 * layer + 1], shift_all[2 * layer + 1], grad_normed_two
    )
    grad_one = grad_one + grad_out
    grad_branch = grad_one.astype(BF)
    grad_project = jnp.einsum("bsd,bse->de", mixed, grad_branch, preferred_element_type=FL)
    grad_mixed = jnp.einsum(
        "bse,de->bsd", grad_branch, project_all[layer], preferred_element_type=FL
    ).astype(BF)
    queries, keys, values = split_heads(projected, memory_kv)
    grad_query, grad_keys, grad_values = attend_backward(
        queries, keys, values, log_norm, grad_mixed.reshape(batch, length, H, HD), context
    )
    slots = memory_kv.shape[1]
    grad_projected = jnp.concatenate(
        [
            grad_query,
            grad_keys[:, slots:].reshape(batch, length, D),
            grad_values[:, slots:].reshape(batch, length, D),
        ],
        axis=-1,
    ).astype(BF)
    grad_memory_kv = jnp.concatenate(
        [
            grad_keys[:, :slots].reshape(batch, slots, D),
            grad_values[:, :slots].reshape(batch, slots, D),
        ],
        axis=-1,
    ).astype(BF)
    grad_attend = jnp.einsum("bsd,bse->de", normed, grad_projected, preferred_element_type=FL)
    grad_attend = grad_attend.at[:, D:].add(
        jnp.einsum("bmd,bme->de", memory, grad_memory_kv, preferred_element_type=FL)
    )
    grad_memory = jnp.einsum(
        "bme,de->bmd", grad_memory_kv, attend_all[layer][:, D:], preferred_element_type=FL
    ).astype(BF)
    grad_normed = jnp.einsum(
        "bse,de->bsd", grad_projected, attend_all[layer], preferred_element_type=FL
    )
    grad_normed = grad_normed + jnp.einsum(
        "bms,bmd->bsd", mixing, grad_memory, preferred_element_type=FL
    )
    grad_state, gain_one, shift_one = norm_back(
        state, gain_all[2 * layer], shift_all[2 * layer], grad_normed
    )
    return (
        grad_state + grad_one,
        (grad_attend, grad_project, grad_expand, grad_contract),
        (gain_one, gain_two),
        (shift_one, shift_two),
    )


def adamw(weight, moment, square, gradient, clip, count, decay, rate):
    gradient = gradient * clip
    moment = BETA_ONE * moment + (1 - BETA_ONE) * gradient
    square = BETA_TWO * square + (1 - BETA_TWO) * gradient * gradient
    fixed_moment = moment / (1 - BETA_ONE**count)
    fixed_square = square / (1 - BETA_TWO**count)
    weight = weight - rate * (fixed_moment / (jnp.sqrt(fixed_square) + ADAM_EPS) + decay * weight)
    return (weight, moment, square)


def shards(
    tokens,
    targets,
    segments,
    counted,
    vocab_mask,
    step_count,
    table,
    table_moment,
    table_square,
    attend,
    attend_moment,
    attend_square,
    project,
    project_moment,
    project_square,
    expand,
    expand_moment,
    expand_square,
    contract,
    contract_moment,
    contract_square,
    gain,
    gain_moment,
    gain_square,
    shift,
    shift_moment,
    shift_square,
):
    gathered = (
        lax.all_gather(table.astype(BF), "batch", axis=1, tiled=True),
        lax.all_gather(attend.astype(BF), "batch", axis=1, tiled=True),
        lax.all_gather(project.astype(BF), "batch", axis=1, tiled=True),
        lax.all_gather(expand.astype(BF), "batch", axis=1, tiled=True),
        lax.all_gather(contract.astype(BF), "batch", axis=1, tiled=True),
        lax.all_gather(gain.astype(BF), "batch", axis=1, tiled=True),
        lax.all_gather(shift.astype(BF), "batch", axis=1, tiled=True),
    )
    words = gathered[0]
    weights = (
        gathered[1],
        gathered[2],
        gathered[3],
        gathered[4],
        gathered[5].astype(FL),
        gathered[6].astype(FL),
    )
    gain_all, shift_all = (weights[4], weights[5])
    rows_local = words.shape[0]
    base = lax.axis_index("vocab") * rows_local
    vocab_ids = base + jnp.arange(rows_local, dtype=jnp.int32)
    live = vocab_mask > 0
    own_count = segments.shape[0]
    local_seqs = own_count // SEQ_LEN
    local_ids = tokens - base
    mine = (local_ids >= 0) & (local_ids < rows_local)
    found = jnp.take(words, jnp.clip(local_ids, 0, rows_local - 1), axis=0)
    embedded = lax.psum_scatter(
        jnp.where(mine[:, None], found.astype(FL), 0.0).astype(jnp.bfloat16),
        "vocab",
        scatter_dimension=0,
        tiled=True,
    ).astype(jnp.float32)
    seq_segments = segments.reshape(local_seqs, SEQ_LEN)
    mixing = jax.vmap(memory_weights)(seq_segments).astype(BF)
    key_seg, key_pos = key_layout(seq_segments)
    context = (seq_segments, key_seg, key_pos)
    state = embedded.reshape(local_seqs, SEQ_LEN, D)
    layer = 0
    state, kept = layer_forward(state, layer, weights, mixing, context)
    kept_all = [kept]
    final_state = state.reshape(-1, D)
    picks = counted.reshape(local_seqs, -1)
    flat_picks = (jnp.arange(local_seqs, dtype=jnp.int32)[:, None] * SEQ_LEN + picks).reshape(-1)
    chosen = jnp.take(final_state, flat_picks, axis=0)
    own_input = layer_norm(chosen, gain_all[2 * LAYERS], shift_all[2 * LAYERS]).astype(BF)
    head_input = lax.all_gather(own_input, "vocab", axis=0, tiled=True)
    logits = jnp.einsum("td,vd->tv", head_input, words, preferred_element_type=FL)
    hot_target = targets[:, None] == vocab_ids[None, :]
    masked = jnp.where(live[None, :], logits, NEG_BIG)
    picked = jnp.sum(jnp.where(hot_target, logits, 0.0), axis=1)
    valid = jnp.sum((hot_target & live[None, :]).astype(FL), axis=1)
    peak = lax.pmax(jnp.max(masked, axis=1), "vocab")
    local_total = jnp.sum(jnp.where(live[None, :], jnp.exp(masked - peak[:, None]), 0.0), axis=1)
    total, picked, valid = (
        lax.psum(local_total.astype(jnp.bfloat16), "vocab").astype(jnp.float32),
        lax.psum(picked.astype(jnp.bfloat16), "vocab").astype(jnp.float32),
        lax.psum(valid.astype(jnp.bfloat16), "vocab").astype(jnp.float32),
    )
    normal = peak + jnp.log(total)
    count_valid = jnp.sum(valid)
    factor = valid / (jnp.maximum(count_valid, 1.0) * lax.axis_size("batch"))
    loss_part = jnp.sum(factor * (normal - picked))
    probs = jnp.where(live[None, :], jnp.exp(logits - normal[:, None]), 0.0)
    grad_logits = (factor[:, None] * (probs - hot_target.astype(FL))).astype(BF)
    grad_head = lax.psum_scatter(
        jnp.dot(grad_logits, words, preferred_element_type=FL),
        "vocab",
        scatter_dimension=0,
        tiled=True,
    )
    grad_table = jnp.einsum("tv,td->vd", grad_logits, head_input, preferred_element_type=FL)
    grad_chosen, gain_last, shift_last = norm_back(
        chosen, gain_all[2 * LAYERS], shift_all[2 * LAYERS], grad_head
    )
    grad_final = jnp.zeros_like(final_state).at[flat_picks].add(grad_chosen)
    grad_state = grad_final.reshape(local_seqs, SEQ_LEN, D)
    layer_grads = [None] * LAYERS
    gain_rows = [None] * (2 * LAYERS)
    shift_rows = [None] * (2 * LAYERS)
    for layer in reversed(range(LAYERS)):
        grad_state, matrices, gain_pair, shift_pair = layer_backward(
            grad_state, kept_all[layer], layer, weights, mixing, context
        )
        layer_grads[layer] = matrices
        gain_rows[2 * layer] = gain_pair[0]
        gain_rows[2 * layer + 1] = gain_pair[1]
        shift_rows[2 * layer] = shift_pair[0]
        shift_rows[2 * layer + 1] = shift_pair[1]
    grad_embedded = grad_state.reshape(-1, D).astype(BF)
    local_ids = tokens - base
    mine = (local_ids >= 0) & (local_ids < rows_local)
    places = jnp.where(mine, local_ids, rows_local)
    grad_table = grad_table.at[places].add(
        lax.all_gather(grad_embedded, "vocab", axis=0, tiled=True).astype(FL), mode="drop"
    )
    grad_gain = jnp.stack(gain_rows + [gain_last])
    grad_shift = jnp.stack(shift_rows + [shift_last])
    stacked = [jnp.stack([entry[index] for entry in layer_grads]) for index in range(4)]
    summed = (
        lax.psum_scatter(
            grad_table.astype(jnp.bfloat16), "batch", scatter_dimension=1, tiled=True
        ).astype(jnp.float32),
        lax.psum_scatter(
            stacked[0].astype(jnp.bfloat16), "batch", scatter_dimension=1, tiled=True
        ).astype(jnp.float32),
        lax.psum_scatter(
            stacked[1].astype(jnp.bfloat16), "batch", scatter_dimension=1, tiled=True
        ).astype(jnp.float32),
        lax.psum_scatter(
            stacked[2].astype(jnp.bfloat16), "batch", scatter_dimension=1, tiled=True
        ).astype(jnp.float32),
        lax.psum_scatter(
            stacked[3].astype(jnp.bfloat16), "batch", scatter_dimension=1, tiled=True
        ).astype(jnp.float32),
        lax.psum_scatter(
            grad_gain.astype(jnp.bfloat16), "batch", scatter_dimension=1, tiled=True
        ).astype(jnp.float32),
        lax.psum_scatter(
            grad_shift.astype(jnp.bfloat16), "batch", scatter_dimension=1, tiled=True
        ).astype(jnp.float32),
    )
    grad_table = summed[0]
    dense = (
        lax.psum(summed[1].astype(jnp.bfloat16), "vocab").astype(jnp.float32),
        lax.psum(summed[2].astype(jnp.bfloat16), "vocab").astype(jnp.float32),
        lax.psum(summed[3].astype(jnp.bfloat16), "vocab").astype(jnp.float32),
        lax.psum(summed[4].astype(jnp.bfloat16), "vocab").astype(jnp.float32),
        lax.psum(summed[5].astype(jnp.bfloat16), "vocab").astype(jnp.float32),
        lax.psum(summed[6].astype(jnp.bfloat16), "vocab").astype(jnp.float32),
    )
    stacked = [dense[0], dense[1], dense[2], dense[3]]
    grad_gain, grad_shift = (dense[4], dense[5])
    at_root = (lax.axis_index("vocab") == 0).astype(FL)
    owned = (
        jnp.sum(stacked[0] * stacked[0])
        + jnp.sum(stacked[1] * stacked[1])
        + jnp.sum(stacked[2] * stacked[2])
        + jnp.sum(stacked[3] * stacked[3])
        + jnp.sum(grad_gain * grad_gain)
        + jnp.sum(grad_shift * grad_shift)
    )
    squares, loss = lax.psum(
        (jnp.sum(grad_table * grad_table) + at_root * owned, at_root * loss_part),
        ("batch", "vocab"),
    )
    gradient_norm = jnp.sqrt(squares)
    clip = jnp.minimum(1.0, MAX_NORM / (gradient_norm + 1e-06))
    count = step_count[0].astype(FL)
    table_out = adamw(table, table_moment, table_square, grad_table, clip, count, DECAY, LEARN_RATE)
    attend_out = adamw(
        attend, attend_moment, attend_square, stacked[0], clip, count, DECAY, LEARN_RATE
    )
    project_out = adamw(
        project, project_moment, project_square, stacked[1], clip, count, DECAY, LEARN_RATE
    )
    expand_out = adamw(
        expand, expand_moment, expand_square, stacked[2], clip, count, DECAY, LEARN_RATE
    )
    contract_out = adamw(
        contract, contract_moment, contract_square, stacked[3], clip, count, DECAY, LEARN_RATE
    )
    gain_out = adamw(gain, gain_moment, gain_square, grad_gain, clip, count, 0.0, NORM_RATE)
    shift_out = adamw(shift, shift_moment, shift_square, grad_shift, clip, count, 0.0, NORM_RATE)
    return (
        loss,
        gradient_norm,
        table_out[0],
        table_out[1],
        table_out[2],
        attend_out[0],
        attend_out[1],
        attend_out[2],
        project_out[0],
        project_out[1],
        project_out[2],
        expand_out[0],
        expand_out[1],
        expand_out[2],
        contract_out[0],
        contract_out[1],
        contract_out[2],
        gain_out[0],
        gain_out[1],
        gain_out[2],
        shift_out[0],
        shift_out[1],
        shift_out[2],
    )


def solution(mesh):
    placed = (
        P("batch"),
        P("batch"),
        P(("batch", "vocab")),
        P(("batch", "vocab")),
        P("vocab"),
        P(),
        P("vocab", "batch"),
        P("vocab", "batch"),
        P("vocab", "batch"),
        P(None, "batch", None),
        P(None, "batch", None),
        P(None, "batch", None),
        P(None, "batch", None),
        P(None, "batch", None),
        P(None, "batch", None),
        P(None, "batch", None),
        P(None, "batch", None),
        P(None, "batch", None),
        P(None, "batch", None),
        P(None, "batch", None),
        P(None, "batch", None),
        P(None, "batch"),
        P(None, "batch"),
        P(None, "batch"),
        P(None, "batch"),
        P(None, "batch"),
        P(None, "batch"),
    )
    return jax.shard_map(
        shards,
        mesh=mesh,
        in_specs=placed,
        out_specs=(
            P(),
            P(),
            P("vocab", "batch"),
            P("vocab", "batch"),
            P("vocab", "batch"),
            P(None, "batch", None),
            P(None, "batch", None),
            P(None, "batch", None),
            P(None, "batch", None),
            P(None, "batch", None),
            P(None, "batch", None),
            P(None, "batch", None),
            P(None, "batch", None),
            P(None, "batch", None),
            P(None, "batch", None),
            P(None, "batch", None),
            P(None, "batch", None),
            P(None, "batch"),
            P(None, "batch"),
            P(None, "batch"),
            P(None, "batch"),
            P(None, "batch"),
            P(None, "batch"),
        ),
        check_vma=False,
    )
```

profile of v0, /device:TPU:0, one launch (start us, length us, event | category | flops | bytes accessed | tf_op | source)
XLA Modules:
  0.0 1683.7 jit_solution(11998423210561078031)
XLA Ops:
  12.1 101.7 %all-gather.10.cloned.1.call-done = bf16[6400,768]{0,1:T(8,128)(2,1)} async-done(((bf16[6400,192]{0,1:T(8,128)(2,1)}), bf16[6400,768]{0,1:T(8,128)(2,1)}) %all-gather.10.cloned.1.call-update) | async-done | bytes 9830416 | tf_op jit(solution)/shard_map/all_gather | solution.py:314
  113.8 13.8 copy.152
  127.6 42.2 %gather_fusion = bf16[8192,768]{1,0:T(8,128)(2,1)} fusion(bf16[6400,768]{1,0:T(8,128)(2,1)} %copy.152, s32[8192]{0:T(1024)S(1)} %get-tuple-element.556), kind=kCustom, calls=%fused_computation | custom fusion | bytes 25198592 | tf_op jit(solution)/shard_map/jit(_take)/gather | solution.py:340
  169.7 16.6 copy.153
  224.9 102.3 %reduce-scatter.16.cloned.1.call-done = bf16[1024,768]{0,1:T(8,128)(2,1)} async-done(((bf16[8192,768]{0,1:T(8,128)(2,1)}), bf16[1024,768]{0,1:T(8,128)(2,1)}) %reduce-scatter.16.cloned.1.call-update) | async-done | bytes 1572880 | tf_op jit(solution)/shard_map/reduce_scatter | solution.py:341
  332.6 42.7 %all-gather.12.cloned.1.call-done = bf16[1,768,2304]{2,1,0:T(8,128)(2,1)} async-done(((bf16[1,192,2304]{2,1,0:T(8,128)(2,1)}), bf16[1,768,2304]{2,1,0:T(8,128)(2,1)}) %all-gather.12.cloned.1.call-update) | async-done | bytes 3538960 | tf_op jit(solution)/shard_map/all_gather | solution.py:315
  397.2 109.6 %while.30 = (s32[]{:T(128)}, bf16[2,1,512,12,64]{2,4,3,1,0:T(8,128)(2,1)}, f32[2,1,12,512]{3,2,1,0:T(8,128)S(1)}, s32[1,1536]{1,0:T(1,128)S(1)}, s32[2]{0:T(128)...) while((s32[]{:T(128)}, ...), condition=%wide.region_12.13_spmd, body=%wide.region_9.12_spmd.sunk | while | flops 2531912192 | bytes 132377320 | solution.py:114
  399.2 17.8 %fusion.221 = (f32[12,512]{1,0:T(8,128)S(1)}, f32[12,512,1536]{2,1,0:T(8,128)}) fusion(pred[512,1536]{1,0:T(8,128)(4,1)S(1)} %compare_and_fusion.8, bf16[1,1536,12,64]{1,3,2,0:T(8,128)(2,1)S(1)} %get-tuple-element.739, bf16[1,1024,12,64]{1,3,2,0:T(8,128)(2,1)} %get-tuple-element.738, s32[]{:T(128)S(6)} %select_n.153), kind=kOutput, calls=%fused_computation.7.clone.1 | convolution fusion | flops 1236264960 | bytes 41705476 | tf_op jit(solution)/shard_map/while/body/eval_jaxpr/bqhd,bkhd->bhqk/dot_general | solution.py:88
  417.0 17.4 %fusion.222 = f32[12,512]{1,0:T(8,128)S(1)} fusion(f32[12,512,1536]{2,1,0:T(8,128)} %get-tuple-element.688, f32[12,512]{1,0:T(8,128)S(1)} %get-tuple-element.689, pred[512,1536]{1,0:T(8,128)(4,1)S(1)} %compare_and_fusion.8), kind=kLoop, calls=%fused_computation.8.clone.1 | loop fusion | flops 37742592 | bytes 38584320 | tf_op jit(solution)/shard_map/while/body/eval_jaxpr/reduce_sum | solution.py:109
  434.4 17.7 %fusion.223 = bf16[2,1,512,12,64]{2,4,3,1,0:T(8,128)(2,1)} fusion(bf16[2,1,512,12,64]{2,4,3,1,0:T(8,128)(2,1)} %get-tuple-element.719, s32[]{:T(128)} %get-tuple-element.718, bf16[1,1536,12,64]{1,3,2,0:T(8,128)(2,1)S(1)} %copy-done.2, f32[12,512,1536]{2,1,0:T(8,128)} %get-tuple-element.688, f32[12,512]{1,0:T(8,128)S(1)} %fusion.222, ...), kind=kOutput, calls=%fused_computation.16.clone.1 | convolution fusion | flops 1255538688 | bytes 41730560 | tf_op jit(solution)/shard_map/while/body/eval_jaxpr/bhqk,bkhd->bqhd/dot_general | solution.py:111
  454.1 16.9 %fusion.221 = (f32[12,512]{1,0:T(8,128)S(1)}, f32[12,512,1536]{2,1,0:T(8,128)}) fusion(pred[512,1536]{1,0:T(8,128)(4,1)S(1)} %compare_and_fusion.8, bf16[1,1536,12,64]{1,3,2,0:T(8,128)(2,1)S(1)} %get-tuple-element.739, bf16[1,1024,12,64]{1,3,2,0:T(8,128)(2,1)} %get-tuple-element.738, s32[]{:T(128)S(6)} %select_n.153), kind=kOutput, calls=%fused_computation.7.clone.1 | convolution fusion | flops 1236264960 | bytes 41705476 | tf_op jit(solution)/shard_map/while/body/eval_jaxpr/bqhd,bkhd->bhqk/dot_general | solution.py:88
  471.0 18.1 %fusion.222 = f32[12,512]{1,0:T(8,128)S(1)} fusion(f32[12,512,1536]{2,1,0:T(8,128)} %get-tuple-element.688, f32[12,512]{1,0:T(8,128)S(1)} %get-tuple-element.689, pred[512,1536]{1,0:T(8,128)(4,1)S(1)} %compare_and_fusion.8), kind=kLoop, calls=%fused_computation.8.clone.1 | loop fusion | flops 37742592 | bytes 38584320 | tf_op jit(solution)/shard_map/while/body/eval_jaxpr/reduce_sum | solution.py:109
  489.1 17.5 %fusion.223 = bf16[2,1,512,12,64]{2,4,3,1,0:T(8,128)(2,1)} fusion(bf16[2,1,512,12,64]{2,4,3,1,0:T(8,128)(2,1)} %get-tuple-element.719, s32[]{:T(128)} %get-tuple-element.718, bf16[1,1536,12,64]{1,3,2,0:T(8,128)(2,1)S(1)} %copy-done.2, f32[12,512,1536]{2,1,0:T(8,128)} %get-tuple-element.688, f32[12,512]{1,0:T(8,128)S(1)} %fusion.222, ...), kind=kOutput, calls=%fused_computation.16.clone.1 | convolution fusion | flops 1255538688 | bytes 41730560 | tf_op jit(solution)/shard_map/while/body/eval_jaxpr/bhqk,bkhd->bqhd/dot_general | solution.py:111
  527.7 11.5 fusion.118
  552.1 23.1 %all-gather.20.cloned.1.call-done = bf16[1024,768]{1,0:T(8,128)(2,1)} async-done(((bf16[128,768]{1,0:T(8,128)(2,1)}), bf16[1024,768]{1,0:T(8,128)(2,1)}) %all-gather.20.cloned.1.call-update) | async-done | bytes 1572880 | tf_op jit(solution)/shard_map/all_gather | solution.py:360
  575.2 20.2 %select_reduce_fusion.1 = (f32[1024]{0:T(1024)}, f32[1024,6400]{1,0:T(8,128)}) fusion(pred[6400]{0:T(1024)(128)(4,1)} %broadcast_compare_fusion, bf16[1024,768]{1,0:T(8,128)(2,1)} %all-gather.20.cloned.1.call-done, bf16[6400,768]{0,1:T(8,128)(2,1)} %all-gather.10.cloned.1.call-done), kind=kOutput, calls=%fused_computation.68 | convolution fusion | flops 10079435776 | bytes 37628160 | tf_op jit(solution)/shard_map/td,vd->tv/dot_general | solution.py:361
  595.4 16.1 pmax.7
  611.5 18.8 %fusion.48 = (bf16[1024]{0:T(1024)(128)(2,1)}, bf16[1024]{0:T(1024)(128)(2,1)}, bf16[1024]{0:T(1024)(128)(2,1)}) fusion(f32[1024,6400]{1,0:T(8,128)} %get-tuple-element.562, s32[6400]{0:T(1024)} %iota_add_fusion.2, s32[1024]{0:T(1024)} %param.34, f32[1024]{0:T(1024)} %pmax.7, pred[6400]{0:T(1024)(128)(4,1)} %broadcast_compare_fusion), kind=kLoop, calls=%fused_computation.61 | loop fusion | flops 65532928 | bytes 26260736 | tf_op jit(solution)/shard_map/reduce_sum | solution.py:364
  630.3 14.3 all-reduce.2
  648.5 18.1 %fusion.51 = bf16[1024,6400]{1,0:T(8,128)(2,1)} fusion(f32[1024,6400]{1,0:T(8,128)} %get-tuple-element.562, f32[1024]{0:T(1024)S(1)} %log_add_fusion, f32[1024]{0:T(1024)S(1)} %convert_divide_fusion, s32[6400]{0:T(1024)} %iota_add_fusion.2, s32[1024]{0:T(1024)} %param.34, pred[6400]{0:T(1024)(128)(4,1)} %broadcast_compare_fusion), kind=kLoop, calls=%fused_computation.64 | loop fusion | flops 45875200 | bytes 39365888 | tf_op jit(solution)/shard_map/convert_element_type | solution.py:378
  666.6 17.0 %fusion.188 = f32[1024,768]{1,0:T(8,128)} fusion(bf16[1024,6400]{1,0:T(8,128)(2,1)} %fusion.51, bf16[6400,768]{0,1:T(8,128)(2,1)} %all-gather.10.cloned.1.call-done), kind=kOutput, calls=%fused_computation.293 | convolution fusion | flops 10066329600 | bytes 26083328 | tf_op jit(solution)/shard_map/dot_general | solution.py:380
  686.7 35.6 %reduce-scatter.18.cloned.1.call-done = f32[128,768]{1,0:T(8,128)} async-done(((f32[1024,768]{1,0:T(8,128)}), f32[128,768]{1,0:T(8,128)}) %reduce-scatter.18.cloned.1.call-update) | async-done | bytes 393232 | tf_op jit(solution)/shard_map/reduce_scatter | solution.py:379
  734.5 15.9 fusion.58
  750.4 11.9 fusion.186
  780.7 242.5 %while.31 = (s32[]{:T(128)}, f32[1,1536,12,64]{1,3,2,0:T(8,128)}, f32[1,1536,12,64]{1,3,2,0:T(8,128)}, bf16[2,1,512,12,64]{2,4,3,1,0:T(8,128)(2,1)}, s32[2]{0:T(...) while((s32[]{:T(128)}, f32[1,1536,12,64]{1,3,2,0:T(8,128)}, ...), condition=%wide.region_33.34_spmd.clone, body=%wide.region_31.33_spmd.clone.sunk | while | flops 6190000640 | bytes 332876576 | solution.py:150
  782.7 16.4 fusion.232
  799.2 27.7 %multiply_reduce_fusion.9 = (f32[12,512]{1,0:T(8,128)S(1)}, f32[12,512,1536]{2,1,0:T(8,128)}) fusion(f32[12,512,1536]{2,1,0:T(8,128)} %fusion.232, f32[12,512]{1,0:T(8,128)S(1)} %dynamic-slice_bitcast_fusion.2, pred[512,1536]{1,0:T(8,128)(4,1)S(1)} %compare_and_fusion.9, bf16[1,1536,12,64]{1,3,2,0:T(8,128)(2,1)S(1)} %copy-done.3, ...), kind=kOutput, calls=%fused_computation.26.clone.1 | convolution fusion | flops 1255139328 | bytes 79486976 | tf_op jit(solution)/shard_map/while/body/eval_jaxpr/bqhd,bkhd->bhqk/dot_general | solution.py:133
  826.9 31.6 %multiply_convert_fusion.5 = bf16[12,512,1536]{2,1,0:T(8,128)(2,1)} fusion(f32[12,512,1536]{2,1,0:T(8,128)} %get-tuple-element.702, f32[12,512,1536]{2,1,0:T(8,128)} %fusion.232, f32[12,512]{1,0:T(8,128)S(1)} %get-tuple-element.703, f32[12,512]{1,0:T(8,128)S(1)} %dynamic-slice_bitcast_fusion.2, pred[512,1536]{1,0:T(8,128)(4,1)S(1)} %compare_and_fusion.9), kind=kLoop, calls=%fused_computation.25.clone.1 | loop fusion | flops 56623104 | bytes 95207424 | tf_op jit(solution)/shard_map/while/body/eval_jaxpr/convert_element_type | solution.py:135
  858.5 12.1 bitcast_add_fusion.4
  881.1 19.4 %bitcast_add_fusion.5 = f32[1,1536,12,64]{1,3,2,0:T(8,128)} fusion(f32[1,1536,12,64]{1,3,2,0:T(8,128)} %get-tuple-element.765, f32[12,512,1536]{2,1,0:T(8,128)} %fusion.232, f32[12,512]{1,0:T(8,128)S(1)} %dynamic-slice_bitcast_fusion.2, pred[512,1536]{1,0:T(8,128)(4,1)S(1)} %compare_and_fusion.9, pred[]{:T(512)S(6)} %compare.8, ...), kind=kOutput, calls=%fused_computation.31.clone.1 | convolution fusion | flops 1248067584 | bytes 48783364 | tf_op jit(solution)/shard_map/while/body/eval_jaxpr/bhqk,bqhd->bkhd/dot_general | solution.py:144
  902.6 16.1 fusion.232
  918.7 27.6 %multiply_reduce_fusion.9 = (f32[12,512]{1,0:T(8,128)S(1)}, f32[12,512,1536]{2,1,0:T(8,128)}) fusion(f32[12,512,1536]{2,1,0:T(8,128)} %fusion.232, f32[12,512]{1,0:T(8,128)S(1)} %dynamic-slice_bitcast_fusion.2, pred[512,1536]{1,0:T(8,128)(4,1)S(1)} %compare_and_fusion.9, bf16[1,1536,12,64]{1,3,2,0:T(8,128)(2,1)S(1)} %copy-done.3, ...), kind=kOutput, calls=%fused_computation.26.clone.1 | convolution fusion | flops 1255139328 | bytes 79486976 | tf_op jit(solution)/shard_map/while/body/eval_jaxpr/bqhd,bkhd->bhqk/dot_general | solution.py:133
  946.4 31.6 %multiply_convert_fusion.5 = bf16[12,512,1536]{2,1,0:T(8,128)(2,1)} fusion(f32[12,512,1536]{2,1,0:T(8,128)} %get-tuple-element.702, f32[12,512,1536]{2,1,0:T(8,128)} %fusion.232, f32[12,512]{1,0:T(8,128)S(1)} %get-tuple-element.703, f32[12,512]{1,0:T(8,128)S(1)} %dynamic-slice_bitcast_fusion.2, pred[512,1536]{1,0:T(8,128)(4,1)S(1)} %compare_and_fusion.9), kind=kLoop, calls=%fused_computation.25.clone.1 | loop fusion | flops 56623104 | bytes 95207424 | tf_op jit(solution)/shard_map/while/body/eval_jaxpr/convert_element_type | solution.py:135
  978.0 13.5 bitcast_add_fusion.4
  1002.0 20.8 %bitcast_add_fusion.5 = f32[1,1536,12,64]{1,3,2,0:T(8,128)} fusion(f32[1,1536,12,64]{1,3,2,0:T(8,128)} %get-tuple-element.765, f32[12,512,1536]{2,1,0:T(8,128)} %fusion.232, f32[12,512]{1,0:T(8,128)S(1)} %dynamic-slice_bitcast_fusion.2, pred[512,1536]{1,0:T(8,128)(4,1)S(1)} %compare_and_fusion.9, pred[]{:T(512)S(6)} %compare.8, ...), kind=kOutput, calls=%fused_computation.31.clone.1 | convolution fusion | flops 1248067584 | bytes 48783364 | tf_op jit(solution)/shard_map/while/body/eval_jaxpr/bhqk,bqhd->bkhd/dot_general | solution.py:144
  1054.3 12.0 fusion.79
  1089.7 58.3 %reduce-scatter.24.cloned.1.call-done = bf16[1,192,3072]{2,1,0:T(8,128)(2,1)} async-done(((bf16[1,768,3072]{2,1,0:T(8,128)(2,1)}), bf16[1,192,3072]{2,1,0:T(8,128)(2,1)}) %reduce-scatter.24.cloned.1.call-update) | async-done | bytes 1179664 | tf_op jit(solution)/shard_map/reduce_scatter | solution.py:423
  1147.9 60.6 %reduce-scatter.26.cloned.1.call-done = bf16[1,768,768]{2,1,0:T(8,128)(2,1)} async-done(((bf16[1,3072,768]{2,1,0:T(8,128)(2,1)}), bf16[1,768,768]{2,1,0:T(8,128)(2,1)}) %reduce-scatter.26.cloned.1.call-update) | async-done | bytes 1179664 | tf_op jit(solution)/shard_map/reduce_scatter | solution.py:426
  1209.0 17.4 %fusion.187 = f32[6400,768]{1,0:T(8,128)} fusion(bf16[1024,6400]{1,0:T(8,128)(2,1)} %fusion.51, bf16[1024,768]{1,0:T(8,128)(2,1)S(1)} %copy-done.96), kind=kOutput, calls=%fused_computation.292 | convolution fusion | flops 10066329600 | bytes 34340864 | tf_op jit(solution)/shard_map/tv,td->vd/dot_general | solution.py:385
  1226.3 101.1 %all-gather.22.cloned.1.call-done = bf16[8192,768]{0,1:T(8,128)(2,1)} async-done(((bf16[1024,768]{0,1:T(8,128)(2,1)}), bf16[8192,768]{0,1:T(8,128)(2,1)}) %all-gather.22.cloned.1.call-update) | async-done | bytes 12582928 | tf_op jit(solution)/shard_map/all_gather | solution.py:408
  1327.4 17.6 %copy.169 = f32[8192,768]{1,0:T(8,128)} copy(bf16[8192,768]{0,1:T(8,128)(2,1)} %all-gather.22.cloned.1.call-done) | data formatting | bytes 37748736 | tf_op jit(solution)/shard_map/convert_element_type | solution.py:408
  1345.0 66.9 %scatter_fusion = f32[6400,768]{1,0:T(8,128)} fusion(f32[6400,768]{1,0:T(8,128)} %fusion.187, s32[8192]{0:T(1024)S(1)} %copy-done.62, f32[8192,768]{1,0:T(8,128)} %copy.169), kind=kCustom, calls=%fused_computation.3 | custom fusion | flops 6291456 | bytes 75530240 | tf_op jit(solution)/shard_map/scatter-add | solution.py:407
  1412.0 11.6 convert_element_type.338
  1423.6 13.1 copy.181
  1452.1 14.8 all-reduce.1
  1481.0 89.1 %reduce-scatter.28.cloned.1.call-done = bf16[192,6400]{1,0:T(8,128)(2,1)} async-done(((bf16[768,6400]{1,0:T(8,128)(2,1)}), bf16[192,6400]{1,0:T(8,128)(2,1)}) %reduce-scatter.28.cloned.1.call-update) | async-done | bytes 2457616
  1583.1 39.5 %all-reduce = (f32[]{:T(128)}, f32[]{:T(128)}) all-reduce(f32[]{:T(128)S(6)} %mul.770, f32[]{:T(128)S(6)} %add.459), channel_id=1, replica_groups=mesh['batch'=4,'vocab'=8] {'batch','vocab'}, use_global_device_ids=true, to_apply=%region_24.25 | all-reduce | flops 2 | bytes 16 | tf_op jit(solution)/shard_map/psum | solution.py:456
  1623.3 14.1 multiply_subtract_fusion
  (421 shorter events, 296.5 us)
Async XLA Ops:
  7.2 106.6 %all-gather.10.cloned.1.call-start = ((), (), s32[]{:S(2)}) async-start(), calls=%async_computation.9 | async-start | bytes 12288000 | tf_op jit(solution)/shard_map/all_gather | solution.py:314
  11.4 315.8 %reduce-scatter.16.cloned.1.call-start = ((), (), s32[]{:S(2)}) async-start(), calls=%async_computation.10 | async-start | bytes 14155776 | tf_op jit(solution)/shard_map/reduce_scatter | solution.py:341
  197.8 177.4 %all-gather.12.cloned.1.call-start = ((), (), s32[]{:S(2)}) async-start(), calls=%async_computation.11 | async-start | bytes 4423680 | tf_op jit(solution)/shard_map/all_gather | solution.py:315
  200.3 312.0 %all-gather.14.cloned.1.call-start = ((), (), s32[]{:S(2)}) async-start(), calls=%async_computation.12 | async-start | bytes 1474560 | tf_op jit(solution)/shard_map/all_gather | solution.py:316
  201.1 315.4 %all-gather.16.cloned.1.call-start = ((), (), s32[]{:S(2)}) async-start(), calls=%async_computation.13 | async-start | bytes 5898240 | tf_op jit(solution)/shard_map/all_gather | solution.py:317
  204.0 11.7 copy-start.80
  204.1 323.7 %all-gather.18.cloned.1.call-start = ((), (), s32[]{:S(2)}) async-start(), calls=%async_computation.14 | async-start | bytes 5898240 | tf_op jit(solution)/shard_map/all_gather | solution.py:318
  205.3 369.9 %all-gather.20.cloned.1.call-start = ((), (), s32[]{:S(2)}) async-start(), calls=%async_computation.15 | async-start | bytes 1769472 | tf_op jit(solution)/shard_map/all_gather | solution.py:360
  205.6 18.6 %copy-start.94 = (s32[128]{0:T(128)}, s32[128]{0:T(128)S(1)}, u32[]{:S(2)}) copy-start(s32[128]{0:T(128)S(1)} %compare_select_fusion.3) | copy-start | bytes 1540
  215.7 162.9 %copy-start.71 = (f32[768]{0:T(1024)}, f32[768]{0:T(1024)S(1)}, u32[]{:S(2)}) copy-start(f32[768]{0:T(1024)S(1)} %get-tuple-element.462) | copy-start | bytes 9220
  223.5 155.0 %copy-start.90 = (f32[768]{0:T(1024)}, f32[768]{0:T(1024)S(1)}, u32[]{:S(2)}) copy-start(f32[768]{0:T(1024)S(1)} %get-tuple-element.465) | copy-start | bytes 9220
  224.9 107.7 %copy-start.43 = (bf16[512,1024]{1,0:T(8,128)(2,1)}, bf16[512,1024]{1,0:T(8,128)(2,1)S(1)}, u32[]{:S(2)}) copy-start(bf16[512,1024]{1,0:T(8,128)(2,1)S(1)} %fusion.104) | copy-start | bytes 3145732
  329.0 49.6 %copy-start.63 = (f32[1024]{0:T(1024)}, f32[1024]{0:T(1024)S(1)}, u32[]{:S(2)}) copy-start(f32[1024]{0:T(1024)S(1)} %broadcast_multiply_fusion.1) | copy-start | bytes 12292
  330.9 47.7 %copy-start.69 = (f32[1024]{0:T(1024)}, f32[1024]{0:T(1024)S(1)}, u32[]{:S(2)}) copy-start(f32[1024]{0:T(1024)S(1)} %fusion.153) | copy-start | bytes 12292
  332.6 45.9 %copy-start.33 = (bf16[512,768]{1,0:T(8,128)(2,1)}, bf16[512,768]{1,0:T(8,128)(2,1)S(1)}, u32[]{:S(2)}) copy-start(bf16[512,768]{1,0:T(8,128)(2,1)S(1)} %convolution_convert_fusion.6) | copy-start | bytes 2359300
  417.0 17.4 %copy-start.2 = (bf16[1,1536,12,64]{1,3,2,0:T(8,128)(2,1)S(1)}, bf16[1,1536,12,64]{1,3,2,0:T(8,128)(2,1)}, u32[]{:S(2)}) copy-start(bf16[1,1536,12,64]{1,3,2,0:T(8,128)(2,1)} %get-tuple-element.740) | copy-start | bytes 7077892 | tf_op jit(solution)/shard_map/while
  471.0 18.1 %copy-start.2 = (bf16[1,1536,12,64]{1,3,2,0:T(8,128)(2,1)S(1)}, bf16[1,1536,12,64]{1,3,2,0:T(8,128)(2,1)}, u32[]{:S(2)}) copy-start(bf16[1,1536,12,64]{1,3,2,0:T(8,128)(2,1)} %get-tuple-element.740) | copy-start | bytes 7077892 | tf_op jit(solution)/shard_map/while
  516.1 253.5 %copy-start.4 = (f32[1024,768]{0,1:T(8,128)}, f32[1024,768]{0,1:T(8,128)S(1)}, u32[]{:S(2)}) copy-start(f32[1024,768]{0,1:T(8,128)S(1)} %get-tuple-element.560) | copy-start | bytes 9437188
  516.1 253.5 %copy-start.51 = (f32[1024]{0:T(1024)}, f32[1024]{0:T(1024)S(1)}, u32[]{:S(2)}) copy-start(f32[1024]{0:T(1024)S(1)} %broadcast_multiply_fusion) | copy-start | bytes 12292
  516.5 11.2 copy-start.75
  516.5 253.1 %copy-start.55 = (f32[1024]{0:T(1024)}, f32[1024]{0:T(1024)S(1)}, u32[]{:S(2)}) copy-start(f32[1024]{0:T(1024)S(1)} %fusion.154) | copy-start | bytes 12292
  550.1 172.1 %reduce-scatter.18.cloned.1.call-start = ((), (), s32[]{:S(2)}) async-start(), calls=%async_computation.16 | async-start | bytes 3538944 | tf_op jit(solution)/shard_map/reduce_scatter | solution.py:379
  683.6 406.0 %reduce-scatter.22.cloned.1.call-start = ((), (), s32[]{:S(2)}) async-start(), calls=%async_computation.19 | async-start | bytes 1474560 | tf_op jit(solution)/shard_map/reduce_scatter | solution.py:420
  750.4 11.9 copy-start.98
  776.2 313.5 %reduce-scatter.20.cloned.1.call-start = ((), (), s32[]{:S(2)}) async-start(), calls=%async_computation.18 | async-start | bytes 4423680 | tf_op jit(solution)/shard_map/reduce_scatter | solution.py:417
  782.7 16.5 copy-start.3
  782.7 16.5 copy-start.15
  902.6 16.1 copy-start.3
  902.6 16.1 copy-start.15
  1026.3 10.2 copy-start.25
  1027.5 9.0 copy-start.27
  1040.8 107.1 %reduce-scatter.24.cloned.1.call-start = ((), (), s32[]{:S(2)}) async-start(), calls=%async_computation.20 | async-start | bytes 5898240 | tf_op jit(solution)/shard_map/reduce_scatter | solution.py:423
  1052.5 156.0 %reduce-scatter.26.cloned.1.call-start = ((), (), s32[]{:S(2)}) async-start(), calls=%async_computation.21 | async-start | bytes 5898240 | tf_op jit(solution)/shard_map/reduce_scatter | solution.py:426
  1066.4 261.1 %all-gather.22.cloned.1.call-start = ((), (), s32[]{:S(2)}) async-start(), calls=%async_computation.17 | async-start | bytes 14155776 | tf_op jit(solution)/shard_map/all_gather | solution.py:408
  1074.5 8.6 copy-start.74
  1074.5 9.9 copy-start.9
  1087.6 121.4 %copy-start.96 = (bf16[1024,768]{1,0:T(8,128)(2,1)S(1)}, bf16[1024,768]{1,0:T(8,128)(2,1)}, u32[]{:S(2)}) copy-start(bf16[1024,768]{1,0:T(8,128)(2,1)} %all-gather.20.cloned.1.call-done) | copy-start | bytes 4718596
  1087.6 362.7 %reduce-scatter.32.cloned.1.call-start = ((), (), s32[]{:S(2)}) async-start(), calls=%async_computation.24 | async-start | bytes 245760
  1088.6 362.5 %reduce-scatter.30.cloned.1.call-start = ((), (), s32[]{:S(2)}) async-start(), calls=%async_computation.23 | async-start | bytes 245760
  1089.6 379.7 %all-reduce.6.cloned.1.call-start = ((), (), s32[]{:S(2)}) async-start(), calls=%async_computation.25 | async-start | bytes 7077888 | tf_op jit(solution)/shard_map/psum | solution.py:438
  1208.5 361.5 %reduce-scatter.28.cloned.1.call-start = ((), (), s32[]{:S(2)}) async-start(), calls=%async_computation.22 | async-start | bytes 12288000
  1226.3 118.7 %copy-start.62 = (s32[8192]{0:T(1024)S(1)}, s32[8192]{0:T(1024)}, u32[]{:S(2)}) copy-start(s32[8192]{0:T(1024)} %get-tuple-element.555) | copy-start | bytes 98308
  1443.8 8.2 copy-start.84
  1443.9 23.0 %copy-start.78 = (f32[1024]{0:T(1024)S(1)}, f32[1024]{0:T(1024)}, u32[]{:S(2)}) copy-start(f32[1024]{0:T(1024)} %copy-done.77) | copy-start | bytes 12292
  1443.9 23.0 %copy-start.79 = (bf16[1024]{0:T(1024)(128)(2,1)S(1)}, bf16[1024]{0:T(1024)(128)(2,1)}, u32[]{:S(2)}) copy-start(bf16[1024]{0:T(1024)(128)(2,1)} %get-tuple-element.516) | copy-start | bytes 6148
  1469.3 8.5 copy-start.22
  1650.0 9.1 copy-start.17
  1650.0 9.1 copy-start.23
  (73 other events, 255.8 us)
Sparse Core Ops, SparseCore 0:
  11.5 102.2 all-gather.9
  197.9 129.1 reduce-scatter.15
  329.6 45.6 all-gather.11
  377.5 27.7 all-gather.13
  407.5 57.0 all-gather.15
  466.9 57.0 all-gather.17
  550.2 24.9 all-gather.19
  683.8 38.4 reduce-scatter.17
  776.2 27.6 reduce-scatter.21
  1040.9 46.2 reduce-scatter.19
  1090.8 57.0 reduce-scatter.23
  1151.4 57.0 reduce-scatter.25
  1210.7 116.7 all-gather.21
  1330.6 22.1 reduce-scatter.31
  1356.0 23.9 reduce-scatter.29
  1382.5 85.8 all-reduce.5
  1471.7 98.2 reduce-scatter.27
where the time goes:
time: 1690 us; the launch traced here: 1680 us
  waiting for transfers between devices  615 us (36%)
  matrix products  412 us (24%)
  other arithmetic  323 us (19%)
  local copies, waits for them, and re-layouts  205 us (12%)
  blocking collectives  99.7 us (6%)
  between operations  24.1 us (1%)
    reduce_scatter x1, waiting for transfers between devices, shards(): lax.psum_scatter(jnp.where(mine[:, None], found.astype(FL), 0.0).astype(j...  102 us
    all_gather x1, waiting for transfers between devices, shards(): lax.all_gather(table.astype(BF), 'batch', axis=1, tiled=True)  102 us
    all_gather x1, waiting for transfers between devices, shards(): lax.all_gather(grad_embedded, 'vocab', axis=0, tiled=True).astype(FL)  101 us
    unnamed x20, waiting for transfers between devices  89.3 us
    unnamed x216, local copies, waits for them, and re-layouts  75.3 us
    dot_general x4, matrix products, block_scores(): jnp.einsum('bqhd,bkhd->bhqk', query_block, keys, preferred_element_type=FL)  67.3 us
    scatter-add x1, other arithmetic, shards(): grad_table.at[places]  66.9 us
    convert_element_type x2, other arithmetic, one_block(): grad_scores = (probs * (grad_probs - inner)).astype(BF)  63.2 us
  transfers between devices with their start and end apart: 17, of which 9 were waited for; matrix products, arithmetic and copies ran while one was open for 37% of the time, Pallas kernels for 0%

commit v1 on v0

v1 whole, which is shorter than its diff:
```python
import functools
import math

import jax
import jax.numpy as jnp
from jax import lax
from jax.experimental import pallas as pl
from jax.experimental.pallas import tpu as pltpu
from jax.sharding import PartitionSpec as P

D = 768
H = 12
HD = 64
FF = 3072
NB = 256
SEG_BLOCKS = 4
SLOTS = SEG_BLOCKS - 2
SEQ_LEN = 1024
PICKS = 128
KEYS = SLOTS * NB + SEQ_LEN
BLK = 256
PAIR = 2 * HD
NPAIR = H // 2
EXTRA = 128

NORM_EPS = 1e-05
MAX_NORM = 0.02
LEARN_RATE = 0.04
NORM_RATE = 0.5
BETA_ONE = 0.9
BETA_TWO = 0.999
ADAM_EPS = 1e-08
DECAY = 0.1
NEG_BIG = -1e30
BF = jnp.bfloat16
FL = jnp.float32
I32 = jnp.int32
MESH = pl.DeviceIdType.MESH
SD = jax.ShapeDtypeStruct
VM = pl.BlockSpec(memory_space=pltpu.VMEM)
SM = pl.BlockSpec(memory_space=pltpu.SMEM)
HB = pl.BlockSpec(memory_space=pl.ANY)
LIMIT = 62 * 2**20


def nn(a, b):
    return lax.dot_general(a, b, (((1,), (0,)), ((), ())), preferred_element_type=FL)


def nt(a, b):
    return lax.dot_general(a, b, (((1,), (1,)), ((), ())), preferred_element_type=FL)


def iota(shape, axis):
    return lax.broadcasted_iota(I32, shape, axis)


def lanes(start, size):
    return pl.ds(pl.multiple_of(start, 128), size)


def chunk_of(rows, want):
    return want if rows % want == 0 else rows


def run(kernel, outs, scratch, ins, name, collective=None, flops=0, moved=0, out_specs=None, in_specs=None):
    return pl.pallas_call(
        kernel,
        out_shape=outs,
        in_specs=in_specs if in_specs is not None else [VM] * len(ins),
        out_specs=out_specs if out_specs is not None else [VM] * len(outs),
        scratch_shapes=scratch,
        compiler_params=pltpu.CompilerParams(
            vmem_limit_bytes=LIMIT,
            collective_id=collective,
            has_side_effects=collective is not None,
        ),
        cost_estimate=pl.CostEstimate(flops=flops, bytes_accessed=moved, transcendentals=0),
        name=name,
    )(*ins)


def send(source, target, out_sem, in_sem, device):
    return pltpu.make_async_remote_copy(
        src_ref=source, dst_ref=target, send_sem=out_sem, recv_sem=in_sem, device_id=device, device_id_type=MESH
    )


def meet(axes):
    barrier = pltpu.get_barrier_semaphore()
    count = 0
    for axis, size in axes:
        me = lax.axis_index(axis)

        def greet(step, carry, axis=axis, size=size, me=me):
            pl.semaphore_signal(barrier, inc=1, device_id={axis: lax.rem(me + step, size)}, device_id_type=MESH)
            return carry

        lax.fori_loop(1, size, greet, 0)
        count += size - 1
    pl.semaphore_wait(barrier, count)


def each(start, stop, body):
    def step(index, carry):
        body(index)
        return carry

    lax.fori_loop(start, stop, step, 0)


def embed_kernel(
    nb, nv, cap, part, round_ref, tok_ref, table_ref, x_ref, ids_ref, place_ref, most_ref, tok_ref_all,
    words, before, ranks, work, sent, got, spread, mixed, turned,
    tok_out, tok_in, row_out, row_in, mix_out, mix_in,
):
    b, v = lax.axis_index("batch"), lax.axis_index("vocab")
    width, rows = table_ref.shape
    shift = round_ref[0] * cap
    meet((("batch", nb), ("vocab", nv)))

    def tok_copy(step):
        return send(
            tok_ref, tok_ref_all.at[b], tok_out.at[step], tok_in.at[step], {"batch": lax.rem(b + step, nb)}
        )

    for step in range(1, nb):
        tok_copy(step).start()
    tok_ref_all[b] = tok_ref[...]
    words[...] = table_ref[...].astype(BF)
    before[...] = (iota((SEQ_LEN, SEQ_LEN), 0) < iota((SEQ_LEN, SEQ_LEN), 1)).astype(FL).astype(BF)
    for step in range(1, nb):
        tok_copy(step).wait()

    base = v * rows
    most = jnp.zeros((nv, 1), FL)
    for p in range(nb):
        ids = tok_ref_all[p]
        mine = (ids >= base) & (ids < base + rows)
        rank = nn(mine.astype(FL).astype(BF), before[...])
        ranks[p] = jnp.where(mine, rank.astype(I32) - shift, -1)
        for owner in range(nv):
            theirs = (ids >= owner * rows) & (ids < (owner + 1) * rows)
            most = jnp.maximum(most, jnp.sum(theirs.astype(FL), axis=1, keepdims=True))
    most_ref[...] = jnp.broadcast_to(jnp.max(most, axis=0, keepdims=True), most_ref.shape)

    def row_copy(step):
        return send(
            sent.at[step], got.at[v], row_out.at[step], row_in.at[step], {"vocab": lax.rem(v + step, nv)}
        )

    def build(turn):
        step = lax.rem(turn, nv)
        dest = lax.rem(v + step, nv)
        found = []
        for p in range(nb):
            pick = (iota((cap, SEQ_LEN), 0) == ranks[p, pl.ds(dest, 1), :]).astype(FL).astype(BF)
            local = tok_ref_all[p, pl.ds(dest, 1), :] - base
            line = iota((8, SEQ_LEN), 0)
            high, low = lax.shift_right_arithmetic(local, 7), lax.bitwise_and(local, 127)
            digits = jnp.where(line == 0, high, jnp.where(line == 1, low, 0)).astype(FL).astype(BF)
            both = nt(pick, digits)
            found.append((both[:, 0:1] * 128.0 + both[:, 1:2]).astype(I32))
        index = jnp.concatenate(found, axis=0)
        ids_ref[dest] = index
        work[...] = jnp.zeros_like(work)

        def piece(j):
            hot = (index - j * part == iota((nb * cap, part), 1)).astype(FL).astype(BF)
            work[...] += nt(hot, words[:, lanes(j * part, part)])

        each(0, rows // part, piece)
        block = work[...].T.astype(BF)

        @pl.when(step > 0)
        def _():
            sent[step] = block
            row_copy(step).start()

        @pl.when(step == 0)
        def _():
            got[v] = block

    each(1, nv + 1, build)

    keys = []
    for p in range(nb):
        ids = tok_ref_all[p, pl.ds(v, 1), :]
        owner = iota((nv, SEQ_LEN), 0)
        theirs = (ids >= owner * rows) & (ids < (owner + 1) * rows)
        rank = nn(theirs.astype(FL).astype(BF), before[...])
        place = jnp.sum(jnp.where(theirs, rank, 0.0), axis=0, keepdims=True).astype(I32) - shift
        holder = jnp.sum(jnp.where(theirs, owner.astype(FL), 0.0), axis=0, keepdims=True).astype(I32)
        line = iota((8, SEQ_LEN), 0)
        place_ref[p] = jnp.where(line == 0, holder, jnp.where(line == 1, place, 0))
        keys.append((holder, place))
        spread[p] = jnp.zeros((width, SEQ_LEN), FL)

    def take(turn):
        step = lax.rem(turn, nv)
        source = lax.rem(v - step + nv, nv)

        @pl.when(step > 0)
        def _():
            row_copy(step).wait()

        block = got[source]
        for p in range(nb):
            holder, place = keys[p]
            key = jnp.where(holder == source, place, -1)
            hot = (iota((cap, SEQ_LEN), 0) == key).astype(FL).astype(BF)
            spread[p] += nn(block[:, p * cap : (p + 1) * cap], hot)

    each(1, nv + 1, take)

    def mix_copy(step):
        return send(
            mixed.at[step], turned.at[b], mix_out.at[step], mix_in.at[step], {"batch": lax.rem(b + step, nb)}
        )

    for step in range(1, nb):
        mixed[step] = spread[lax.rem(b + step, nb)].astype(BF)
        mix_copy(step).start()
    turned[b] = spread[b].astype(BF)
    for step in range(1, nb):
        mix_copy(step).wait()
    x_ref[...] = turned[...].reshape(nb * width, SEQ_LEN).T


def embed(nb, nv, cap, turn, tok, table):
    width, rows = table.shape
    part = chunk_of(rows, 640)
    count = nb * cap
    outs = [
        SD((SEQ_LEN, D), BF),
        SD((nv, count, 1), I32),
        SD((nb, 8, SEQ_LEN), I32),
        SD((8, 128), FL),
        SD((nb, nv, SEQ_LEN), I32),
    ]
    dma = pltpu.SemaphoreType.DMA
    scratch = [
        pltpu.VMEM((width, rows), BF),
        pltpu.VMEM((SEQ_LEN, SEQ_LEN), BF),
        pltpu.VMEM((nb, nv, SEQ_LEN), I32),
        pltpu.VMEM((count, width), FL),
        pltpu.VMEM((nv, width, count), BF),
        pltpu.VMEM((nv, width, count), BF),
        pltpu.VMEM((nb, width, SEQ_LEN), FL),
        pltpu.VMEM((nb, width, SEQ_LEN), BF),
        pltpu.VMEM((nb, width, SEQ_LEN), BF),
        dma((nb,)), dma((nb,)), dma((nv,)), dma((nv,)), dma((nb,)), dma((nb,)),
    ]
    return run(
        functools.partial(embed_kernel, nb, nv, cap, part), outs, scratch, [turn, tok, table], "embed", 0,
        in_specs=[SM, VM, VM],
    )


def unembed_kernel(
    nb, nv, cap, part, x_ref, ids_ref, place_ref, out_ref,
    turned, parts, sent, got, mix_out, mix_in, row_out, row_in,
):
    b, v = lax.axis_index("batch"), lax.axis_index("vocab")
    width, rows = out_ref.shape
    meet((("batch", nb), ("vocab", nv)))
    turned[...] = x_ref[...].T.reshape(nb, width, SEQ_LEN)

    def mix_copy(step):
        other = lax.rem(b + step, nb)
        return send(turned.at[other], parts.at[b], mix_out.at[step], mix_in.at[step], {"batch": other})

    for step in range(1, nb):
        mix_copy(step).start()
    parts[b] = turned[b]
    for step in range(1, nb):
        mix_copy(step).wait()

    def row_copy(step):
        return send(
            sent.at[step], got.at[v], row_out.at[step], row_in.at[step], {"vocab": lax.rem(v + step, nv)}
        )

    def build(turn):
        step = lax.rem(turn, nv)
        owner = lax.rem(v + step, nv)
        blocks = []
        for p in range(nb):
            key = jnp.where(place_ref[p, 0:1, :] == owner, place_ref[p, 1:2, :], -1)
            hot = (iota((cap, SEQ_LEN), 0) == key).astype(FL).astype(BF)
            blocks.append(nt(parts[p], hot).astype(BF))
        block = jnp.concatenate(blocks, axis=1)

        @pl.when(step > 0)
        def _():
            sent[step] = block
            row_copy(step).start()

        @pl.when(step == 0)
        def _():
            got[v] = block

    each(1, nv + 1, build)
    out_ref[...] = jnp.zeros_like(out_ref)

    def take(step):
        source = lax.rem(v - step + nv, nv)

        @pl.when(step > 0)
        def _():
            row_copy(step).wait()

        block, index = got[source], ids_ref[source]

        def piece(j):
            hot = (index - j * part == iota((nb * cap, part), 1)).astype(FL).astype(BF)
            out_ref[:, lanes(j * part, part)] += nn(block, hot)

        each(0, rows // part, piece)

    each(0, nv, take)


def unembed(nb, nv, cap, width, rows, grad, ids, place):
    part = chunk_of(rows, 640)
    count = nb * cap
    dma = pltpu.SemaphoreType.DMA
    scratch = [
        pltpu.VMEM((nb, width, SEQ_LEN), BF),
        pltpu.VMEM((nb, width, SEQ_LEN), BF),
        pltpu.VMEM((nv, width, count), BF),
        pltpu.VMEM((nv, width, count), BF),
        dma((nb,)), dma((nb,)), dma((nv,)), dma((nv,)),
    ]
    return run(
        functools.partial(unembed_kernel, nb, nv, cap, part), [SD((width, rows), FL)], scratch,
        [grad, ids, place], "unembed", 2,
    )[0]


def later_slots(nv, cap, rows, every, turn):
    nb = every.shape[0]
    v = lax.axis_index("vocab")
    local = every - v * rows
    mine = (local >= 0) & (local < rows)
    rank = jnp.cumsum(mine.astype(I32), axis=-1) - 1 - turn * cap
    hot = (rank[:, :, None, :] == jnp.arange(cap)[None, None, :, None]) & mine[:, :, None, :]
    ids = jnp.sum(jnp.where(hot, local[:, :, None, :], 0), axis=-1)
    return jnp.transpose(ids, (1, 0, 2)).reshape(nv, nb * cap, 1)


def standard(value):
    centre = value - jnp.mean(value, axis=-1, keepdims=True)
    spread = jnp.mean(centre * centre, axis=-1, keepdims=True)
    scale = lax.rsqrt(spread + NORM_EPS)
    return centre * scale, scale


def norm_back(unit, scale, gain, upstream):
    inner = upstream * gain
    first = jnp.mean(inner, axis=-1, keepdims=True)
    second = jnp.mean(inner * unit, axis=-1, keepdims=True)
    grad = scale * (inner - first - unit * second)
    return grad, jnp.sum(upstream * unit, axis=0, keepdims=True), jnp.sum(upstream, axis=0, keepdims=True)


def head_lanes(value, head):
    lane = iota(value.shape, 1)
    keep = (lane < HD) if head == 0 else (lane >= HD)
    return jnp.where(keep, value, jnp.zeros_like(value))


def visible_keys(key_ref, query_ref):
    return (key_ref[:, 0:1] == query_ref[0:1, :]) & (key_ref[:, 1:2] <= query_ref[1:2, :])


def attend_kernel(
    x_ref, a_ref, mix_ref, pick_ref, key_ref, query_ref,
    hall_ref, kv_ref, q_ref, hq_ref, xq_ref, o_ref, lse_ref, norm_ref,
):
    norm_ref[...] = a_ref[:, 3 * D :].astype(FL).T[:8, :]
    gain, bias = norm_ref[0:1, :], norm_ref[3:4, :]

    def normalize(i):
        unit, _ = standard(x_ref[pl.ds(i * BLK, BLK), :].astype(FL))
        hall_ref[pl.ds(SLOTS * NB + i * BLK, BLK), :] = (unit * gain + bias).astype(BF)

    each(0, SEQ_LEN // BLK, normalize)
    normed = hall_ref[SLOTS * NB :, :]
    hall_ref[: SLOTS * NB, :] = nn(mix_ref[...], normed).astype(BF)

    def project(i):
        kv_ref[pl.ds(i * BLK, BLK), :] = nn(hall_ref[pl.ds(i * BLK, BLK), :], a_ref[:, D : 3 * D]).astype(BF)

    each(0, KEYS // BLK, project)
    pick = (pick_ref[...] == iota((PICKS, SEQ_LEN), 1)).astype(FL).astype(BF)
    hq_ref[...] = nn(pick, normed).astype(BF)
    xq_ref[...] = nn(pick, x_ref[...])
    q_ref[...] = nn(hq_ref[...], a_ref[:, :D]).astype(BF)
    visible = visible_keys(key_ref, query_ref)

    def attend(p):
        keys = kv_ref[:, lanes(p * PAIR, PAIR)]
        values = kv_ref[:, lanes(D + p * PAIR, PAIR)].T
        queries = q_ref[:, lanes(p * PAIR, PAIR)] * HD ** (-0.5)
        outs = []
        for head in range(2):
            scores = jnp.where(visible, nt(keys, head_lanes(queries, head)), NEG_BIG)
            peak = jnp.max(scores, axis=0, keepdims=True)
            expo = jnp.exp(scores - peak)
            total = jnp.sum(expo, axis=0, keepdims=True)
            probs = (expo * (1.0 / total)).astype(BF)
            outs.append(nn(values[head * HD : (head + 1) * HD, :], probs))
            lse_ref[p, head : head + 1, :] = peak + jnp.log(total)
        o_ref[:, lanes(p * PAIR, PAIR)] = jnp.concatenate(outs, axis=0).T.astype(BF)

    each(0, NPAIR, attend)


def feed_kernel(xq_ref, o_ref, p_ref, u_ref, c_ref, norm_ref, x1_ref, h2_ref, z_ref, act_ref, x2_ref, f_ref):
    x1 = xq_ref[...] + nn(o_ref[...], p_ref[...])
    x1_ref[...] = x1
    unit, _ = standard(x1)
    h2 = (unit * norm_ref[1:2, :] + norm_ref[4:5, :]).astype(BF)
    h2_ref[...] = h2
    x2_ref[...] = x1

    def piece(j):
        cut = lanes(j * D, D)
        z = nn(h2, u_ref[:, cut])
        z_ref[:, cut] = z
        act = jax.nn.gelu(z, approximate=True).astype(BF)
        act_ref[:, cut] = act
        x2_ref[...] += nn(act, c_ref[pl.ds(j * D, D), :])

    each(0, FF // D, piece)
    unit, _ = standard(x2_ref[...])
    f_ref[...] = (unit * norm_ref[2:3, :] + norm_ref[5:6, :]).astype(BF)


def feed_back_kernel(
    df_ref, x2_ref, x1_ref, h2_ref, z_ref, act_ref, o_ref, p_ref, u_ref, c_ref, norm_ref,
    dc_ref, du_ref, dp_ref, dx1_ref, do_ref, dnorm_ref, dh2,
):
    unit, scale = standard(x2_ref[...])
    dx2, gain_last, bias_last = norm_back(unit, scale, norm_ref[2:3, :], df_ref[...])
    dy = dx2.astype(BF)
    dh2[...] = jnp.zeros_like(dh2)
    h2t = h2_ref[...].T

    def piece(j):
        cut = lanes(j * D, D)
        dc_ref[pl.ds(j * D, D), :] = nn(act_ref[:, cut].T, dy).astype(BF)
        dact = nt(dy, c_ref[pl.ds(j * D, D), :])
        z = z_ref[:, cut]
        k = math.sqrt(2.0 / math.pi)
        t = jnp.tanh(k * (z + 0.044715 * z * z * z))
        slope = 0.5 * (1.0 + t) + 0.5 * z * (1.0 - t * t) * (k * (1.0 + 3 * 0.044715 * z * z))
        dz = (dact * slope).astype(BF)
        du_ref[:, cut] = nn(h2t, dz).astype(BF)
        dh2[...] += nt(dz, u_ref[:, cut])

    each(0, FF // D, piece)
    unit, scale = standard(x1_ref[...])
    dx1, gain_two, bias_two = norm_back(unit, scale, norm_ref[1:2, :], dh2[...])
    dx1 = dx1 + dx2
    dx1_ref[...] = dx1
    da = dx1.astype(BF)
    dp_ref[...] = nn(o_ref[...].T, da).astype(BF)
    do_ref[...] = nt(da, p_ref[...]).astype(BF)
    zero = jnp.zeros_like(gain_last)
    dnorm_ref[...] = jnp.concatenate([zero, gain_two, gain_last, zero, bias_two, bias_last, zero, zero], axis=0)


def attend_back_kernel(
    pos_ref, do_ref, q_ref, kv_ref, lse_ref, hall_ref, hq_ref, a_ref, x_ref, dx1_ref, mixt_ref, key_ref, query_ref,
    norm_ref, dnorm_ref, da_ref, dx_ref, dkv, dq, hallt, dh, dxin, dmem,
):
    visible = visible_keys(key_ref, query_ref)

    def attend(p):
        cut = lanes(p * PAIR, PAIR)
        keys = kv_ref[:, cut]
        values = kv_ref[:, lanes(D + p * PAIR, PAIR)]
        turned = keys.T
        queries = q_ref[:, cut] * HD ** (-0.5)
        grads = do_ref[:, cut]
        outs = []
        dk = dv = None
        for head in range(2):
            own, grad = head_lanes(queries, head), head_lanes(grads, head)
            scores = jnp.where(visible, nt(keys, own), NEG_BIG)
            probs = jnp.exp(scores - lse_ref[p, head : head + 1, :])
            dprobs = nt(values, grad)
            inner = jnp.sum(probs * dprobs, axis=0, keepdims=True)
            dscores = (probs * (dprobs - inner)).astype(BF)
            outs.append(nn(turned[head * HD : (head + 1) * HD, :], dscores))
            one, two = nn(dscores, own), nn(probs.astype(BF), grad)
            dk = one if head == 0 else dk + one
            dv = two if head == 0 else dv + two
        dq[:, cut] = (jnp.concatenate(outs, axis=0).T * HD ** (-0.5)).astype(BF)
        dkv[:, cut] = dk.astype(BF)
        dkv[:, lanes(D + p * PAIR, PAIR)] = dv.astype(BF)

    each(0, NPAIR, attend)
    da_ref[:, :D] = nn(hq_ref[...].T, dq[...]).astype(BF)

    def turn(i):
        hallt[:, lanes(i * BLK, BLK)] = hall_ref[pl.ds(i * BLK, BLK), :].T

    each(0, KEYS // BLK, turn)

    def weights(j):
        cut = lanes(j * BLK, BLK)
        da_ref[:, lanes(D + j * BLK, BLK)] = nn(hallt[...], dkv[:, cut]).astype(BF)

    each(0, 2 * D // BLK, weights)

    def memory(i):
        cut = pl.ds(i * BLK, BLK)
        dmem[cut, :] = nt(dkv[cut, :], a_ref[:, D : 3 * D]).astype(BF)

    each(0, SLOTS, memory)

    def local(i):
        cut = pl.ds(i * BLK, BLK)
        dh[cut, :] = nt(dkv[pl.ds(SLOTS * NB + i * BLK, BLK), :], a_ref[:, D : 3 * D]) + nn(mixt_ref[cut, :], dmem[...])

    each(0, SEQ_LEN // BLK, local)
    dxin[:PICKS, :] = nt(dq[...], a_ref[:, :D])

    def scatter_query(k):
        row = pl.ds(pos_ref[k], 1)
        dh[row, :] += dxin[pl.ds(k, 1), :]

    each(0, PICKS, scatter_query)
    gain = norm_ref[0:1, :]
    da_rows = [jnp.zeros((1, D), FL), jnp.zeros((1, D), FL)]

    def finish(i, carry):
        cut = pl.ds(i * BLK, BLK)
        unit, scale = standard(x_ref[cut, :].astype(FL))
        grad, dgain, dbias = norm_back(unit, scale, gain, dh[cut, :])
        dxin[cut, :] = grad
        return carry[0] + dgain, carry[1] + dbias

    dgain, dbias = lax.fori_loop(0, SEQ_LEN // BLK, finish, tuple(da_rows))

    def scatter_rest(k):
        row = pl.ds(pos_ref[k], 1)
        dxin[row, :] += dx1_ref[pl.ds(k, 1), :]

    each(0, PICKS, scatter_rest)
    dx_ref[...] = dxin[...].astype(BF)
    line = iota((8, D), 0)
    norms = dnorm_ref[...] + jnp.where(line == 0, dgain, jnp.where(line == 3, dbias, 0.0))
    tall = jnp.concatenate([norms, jnp.zeros((EXTRA - 8, D), FL)], axis=0)
    da_ref[:, 3 * D :] = tall.T.astype(BF)


def head_kernel(
    nb, nv, part, f_ref, w_ref, live_ref, target_ref, df_ref, dw_ref, loss_ref,
    fall, expo, block, mine, stats, ft, grad_sum, coef, df, half, far_got, out,
    near_out, near_in, far_out, far_in, stat_out, stat_in, pair_out, pair_in, sum_out, sum_in, dw_sem,
):
    v = lax.axis_index("vocab")
    rows = w_ref.shape[1]
    total_rows = nv * PICKS
    core, chip, chips = lax.rem(v, 2), v // 2, nv // 2
    sibling = {"vocab": v + 1 - 2 * core}
    base = v * rows
    pieces = rows // part
    depth = min(2, pieces)
    meet((("vocab", nv),))

    def peer(step):
        return {"vocab": lax.rem(chip + step, chips) * 2 + core}

    def far_copy(step):
        return send(f_ref, fall.at[v], far_out.at[step], far_in.at[step], peer(step))

    def near_copy(step):
        slot = lax.rem(chip - step + chips, chips) * 2 + core
        return send(fall.at[slot], fall.at[slot], near_out.at[step], near_in.at[step], sibling)

    fall[v] = f_ref[...]
    near_copy(0).start()
    each(1, chips, lambda step: far_copy(step).start())

    def logits(step):
        @pl.when(step > 0)
        def _():
            far_copy(step).wait_recv()
            near_copy(step).start()

        near_copy(step).wait_recv()
        source = lax.rem(chip - step + chips, chips)
        start = pl.multiple_of(source * 2 * PICKS, 2 * PICKS)
        features = fall[pl.ds(source * 2, 2)].reshape(2 * PICKS, D)
        target = target_ref[pl.ds(start, 2 * PICKS), :] - base

        def score(j, peak):
            cut = lanes(j * part, part)
            value = nn(features, w_ref[:, cut])
            block[:, cut] = value
            return jnp.maximum(
                peak, jnp.max(jnp.where(live_ref[0:1, cut] > 0, value, NEG_BIG), axis=1, keepdims=True)
            )

        peak = lax.fori_loop(0, pieces, score, jnp.full((2 * PICKS, 1), NEG_BIG, FL))

        def count(j, carry):
            total, picked, valid = carry
            cut = lanes(j * part, part)
            value = block[:, cut]
            live = live_ref[0:1, cut] > 0
            hot = target - j * part == iota((2 * PICKS, part), 1)
            e = jnp.where(live, jnp.exp(value - peak), 0.0)
            expo[pl.ds(start, 2 * PICKS), cut] = e.astype(BF)
            total = total + jnp.sum(e, axis=1, keepdims=True)
            picked = picked + jnp.sum(jnp.where(hot, value, 0.0), axis=1, keepdims=True)
            valid = valid + jnp.sum(jnp.where(hot & live, 1.0, 0.0), axis=1, keepdims=True)
            return total, picked, valid

        zero = jnp.zeros((2 * PICKS, 1), FL)
        total, picked, valid = lax.fori_loop(0, pieces, count, (zero, zero, zero))
        lane = iota((2 * PICKS, 128), 1)
        wide = jnp.where(lane == 0, peak, jnp.where(lane == 1, total, jnp.where(lane == 2, picked, valid)))
        mine[:, pl.ds(start, 2 * PICKS)] = wide.T[:8, :]

    each(0, chips, logits)

    def stat_copy(step):
        return send(mine, stats.at[v], stat_out.at[step], stat_in.at[step], {"vocab": lax.rem(v + step, nv)})

    each(1, nv, lambda step: stat_copy(step).start())
    stats[v] = mine[...]
    for i in range(total_rows // 256 if pieces > 1 else 0):
        ft[:, i * 256 : (i + 1) * 256] = fall[2 * i : 2 * i + 2].reshape(256, D).T
    each(1, nv, lambda step: stat_copy(step).wait())
    start = jnp.full((1, total_rows), NEG_BIG, FL)
    peak = lax.fori_loop(0, nv, lambda u, top: jnp.maximum(top, stats[u, 0:1, :]), start)

    def combine(u, carry):
        scale = jnp.exp(stats[u, 0:1, :] - peak)
        return (
            carry[0] + stats[u, 1:2, :] * scale, carry[1] + stats[u, 2:3, :], carry[2] + stats[u, 3:4, :],
        )

    zero = jnp.zeros((1, total_rows), FL)
    total, picked, valid = lax.fori_loop(0, nv, combine, (zero, zero, zero))
    lse = peak + jnp.log(jnp.maximum(total, 1e-37))
    weight = valid / (jnp.maximum(jnp.sum(valid, axis=1, keepdims=True), 1.0) * nb)
    loss = jnp.sum(weight * (lse - picked), axis=1, keepdims=True)
    loss_ref[...] = jnp.broadcast_to(loss, loss_ref.shape)
    alpha = weight * jnp.exp(mine[0:1, :] - lse)
    line = iota((128, 256), 0)
    for i in range(total_rows // 256):
        cut = slice(i * 256, (i + 1) * 256)
        coef[cut, :] = jnp.where(line == 0, alpha[:, cut], weight[:, cut]).T

    tall = min(total_rows, 1024 if pieces > 1 else 256)
    shards_tall = tall // PICKS
    df[...] = jnp.zeros_like(df)

    def out_copy(j):
        return pltpu.make_async_copy(
            out.at[lax.rem(j, depth)], dw_ref.at[:, lanes(j * part, part)], dw_sem.at[lax.rem(j, depth)]
        )

    def gradients(j):
        cut = lanes(j * part, part)
        words = w_ref[:, cut]

        @pl.when(j >= depth)
        def _():
            out_copy(j - depth).wait()

        def strip(t):
            start = t * tall if total_rows == tall else pl.multiple_of(t * tall, tall)
            here = pl.ds(start, tall)
            hot = target_ref[here, :] - base - j * part == iota((tall, part), 1)
            two = coef[here, :]
            value = two[:, 0:1] * expo[here, cut].astype(FL) - jnp.where(hot, two[:, 1:2], 0.0)
            dlogits = value.astype(BF)
            df[here, :] += nt(dlogits, words)
            if pieces > 1:
                turned = ft[:, pl.ds(start, tall)]
            else:
                turned = fall[pl.ds(t * shards_tall, shards_tall)].reshape(tall, D).T
            for r in range(0, D, D // 3):
                more = nn(turned[r : r + D // 3, :], dlogits)
                if total_rows == tall:
                    out[lax.rem(j, depth), r : r + D // 3, :] = more.astype(BF)
                else:
                    grad_sum[r : r + D // 3, :] += more

        if total_rows == tall:
            strip(0)
        else:
            grad_sum[...] = jnp.zeros_like(grad_sum)
            each(0, total_rows // tall, strip)
            for r in range(0, D, D // 3):
                out[lax.rem(j, depth), r : r + D // 3, :] = grad_sum[r : r + D // 3, :].astype(BF)
        out_copy(j).start()

    each(0, pieces, gradients)

    def shard(index):
        return pl.ds(pl.multiple_of(index * PICKS, PICKS), PICKS)

    def pair_copy(k):
        source = df.at[shard(2 * k + 1 - core), :] if pieces > 1 else fall.at[k]
        return send(source, half.at[k], pair_out.at[k], pair_in.at[k], sibling)

    near_copy(0).wait_send()

    def drain(step):
        far_copy(step).wait_send()
        near_copy(step).wait_send()

    each(1, chips, drain)

    def swap(k):
        if pieces == 1:
            fall[k] = df[shard(2 * k + 1 - core), :].astype(BF)
        pair_copy(k).start()

    each(0, chips, swap)

    def sum_copy(step):
        return send(fall.at[chips + step], far_got.at[step], sum_out.at[step], sum_in.at[step], peer(step))

    def pass_on(turn):
        step = lax.rem(turn, chips)
        k = lax.rem(chip + step, chips)
        pair_copy(k).wait()
        value = df[shard(2 * k + core), :] + half[k].astype(FL)

        @pl.when(step > 0)
        def _():
            fall[chips + step] = value.astype(BF)
            sum_copy(step).start()

        @pl.when(step == 0)
        def _():
            df_ref[...] = value

    each(1, chips + 1, pass_on)

    def collect(step):
        sum_copy(step).wait()
        df_ref[...] += far_got[step].astype(FL)

    each(1, chips, collect)
    for j in range(pieces - depth, pieces):
        out_copy(j).wait()


def head(nb, nv, features, words, live, targets):
    rows = words.shape[1]
    part = chunk_of(rows, 640)
    total_rows = nv * PICKS
    chips = nv // 2
    dma = pltpu.SemaphoreType.DMA
    scratch = [
        pltpu.VMEM((nv, PICKS, D), BF),
        pltpu.VMEM((total_rows, rows), BF),
        pltpu.VMEM((2 * PICKS, rows), FL),
        pltpu.VMEM((8, total_rows), FL),
        pltpu.VMEM((nv, 8, total_rows), FL),
        pltpu.VMEM((D, total_rows) if rows > part else (8, 128), BF),
        pltpu.VMEM((8, 128) if rows > part else (D, part), FL),
        pltpu.VMEM((total_rows, 128), FL),
        pltpu.VMEM((total_rows, D), FL),
        pltpu.VMEM((chips, PICKS, D), FL if rows > part else BF),
        pltpu.VMEM((chips, PICKS, D), BF),
        pltpu.VMEM((min(2, rows // part), D, part), BF),
        dma((chips,)), dma((chips,)), dma((chips,)), dma((chips,)), dma((nv,)), dma((nv,)),
        dma((chips,)), dma((chips,)), dma((chips,)), dma((chips,)), dma((2,)),
    ]
    return run(
        functools.partial(head_kernel, nb, nv, part),
        [SD((PICKS, D), FL), SD((D, rows), BF), SD((8, 128), FL)],
        scratch,
        [features, words, live, targets],
        "head",
        1,
        out_specs=[VM, HB, VM],
    )


def memory_weights(segments):
    length = segments.shape[0]
    places = jnp.arange(length, dtype=I32)
    slot_ids = jnp.arange(SLOTS, dtype=I32)
    inside = segments[None, :] == slot_ids[:, None]
    starts = jnp.sum((segments[None, :] < slot_ids[:, None]).astype(I32), axis=1)
    counts = jnp.sum(inside.astype(I32), axis=1)
    times = ((places[None, :] - starts[:, None]).astype(FL) + 0.5) / jnp.maximum(counts, 1)[:, None].astype(FL)
    centres = (jnp.arange(NB, dtype=FL) + 0.5) / NB
    offset = (times[:, None, :] - centres[None, :, None]) * NB
    basis = jnp.exp(-0.5 * offset * offset) * inside[:, None, :].astype(FL)
    total = jnp.sum(basis, axis=2, keepdims=True) + (counts == 0).astype(FL)[:, None, None]
    return (basis / total).reshape(SLOTS * NB, length)


def adamw(weight, moment, square, gradient, clip, count, decay, rate):
    gradient = gradient * clip
    moment = BETA_ONE * moment + (1 - BETA_ONE) * gradient
    square = BETA_TWO * square + (1 - BETA_TWO) * gradient * gradient
    fixed_moment = moment / (1 - BETA_ONE**count)
    fixed_square = square / (1 - BETA_TWO**count)
    weight = weight - rate * (fixed_moment / (jnp.sqrt(fixed_square) + ADAM_EPS) + decay * weight)
    return (weight, moment, square)


def slot_size(nv):
    mean = SEQ_LEN // nv
    return -(-(mean + int(5.5 * math.sqrt(mean))) // 32) * 32


def shards(
    nb, nv,
    tokens, targets, segments, counted, vocab_mask, step_count,
    table, table_moment, table_square,
    attend, attend_moment, attend_square,
    project, project_moment, project_square,
    expand, expand_moment, expand_square,
    contract, contract_moment, contract_square,
    gain, gain_moment, gain_square,
    shift, shift_moment, shift_square,
):
    rows, width = table.shape
    cap = slot_size(nv)
    table_t = table.T
    norms = jnp.concatenate([gain, shift], axis=0)
    packed = jnp.concatenate([attend[0], norms.T, jnp.zeros((width, EXTRA - 6), FL)], axis=1).astype(BF)
    a_all = lax.all_gather(packed, "batch", axis=0, tiled=True)
    p_all = lax.all_gather(project[0].astype(BF), "batch", axis=0, tiled=True)
    u_all = lax.all_gather(expand[0].astype(BF), "batch", axis=0, tiled=True)
    c_all = lax.all_gather(contract[0].astype(BF), "batch", axis=0, tiled=True)
    words = lax.all_gather(table_t.astype(BF), "batch", axis=0, tiled=True)

    mixing = memory_weights(segments).astype(BF)
    mixing_t = mixing.T
    key_seg = jnp.concatenate([jnp.repeat(jnp.arange(SLOTS, dtype=I32) + 1, NB), segments])
    key_pos = jnp.concatenate([jnp.full((SLOTS * NB,), -1, I32), jnp.arange(SEQ_LEN, dtype=I32)])
    keys = jnp.stack([key_seg, key_pos], axis=1)
    query_blk = counted // BLK
    query_seg = functools.reduce(
        lambda seg, i: jnp.where(query_blk == i, segments[i * BLK], seg), range(1, SEQ_LEN // BLK), jnp.broadcast_to(segments[0], counted.shape)
    )
    queries = jnp.concatenate([query_seg[None], counted[None], jnp.zeros((6, PICKS), I32)], axis=0)

    tok = tokens.reshape(nv, SEQ_LEN)
    x, ids, place, most, every = embed(nb, nv, cap, jnp.zeros((1,), I32), tok, table_t)
    turns = (most[0, 0].astype(I32) + cap - 1) // cap

    def more_rows(state):
        turn, total = state
        return turn + 1, total + embed(nb, nv, cap, turn[None], tok, table_t)[0]

    x = lax.while_loop(lambda state: state[0] < turns, more_rows, (jnp.int32(1), x))[1]

    hall, kv, q, hq, xq, mixed, lse, norm_rows = run(
        attend_kernel,
        [
            SD((KEYS, D), BF), SD((KEYS, 2 * D), BF), SD((PICKS, D), BF), SD((PICKS, D), BF), SD((PICKS, D), FL),
            SD((PICKS, D), BF), SD((NPAIR, 2, PICKS), FL), SD((8, D), FL),
        ],
        [],
        [x, a_all, mixing, counted[:, None], keys, queries],
        "attend", flops=7 * 10**9, moved=20 * 10**6,
    )
    x1, h2, z, act, x2, features = run(
        feed_kernel,
        [
            SD((PICKS, D), FL), SD((PICKS, D), BF), SD((PICKS, FF), FL), SD((PICKS, FF), BF), SD((PICKS, D), FL),
            SD((PICKS, D), BF),
        ],
        [],
        [xq, mixed, p_all, u_all, c_all, norm_rows],
        "feed", flops=2 * 10**9, moved=15 * 10**6,
    )
    df, dw, loss_block = head(nb, nv, features, words, vocab_mask[None, :], targets[:, None])
    loss_part = loss_block[0, 0]
    dw_sum = lax.psum_scatter(dw, "batch", scatter_dimension=0, tiled=True)

    dc, du, dp, dx1, dmixed, dnorm = run(
        feed_back_kernel,
        [
            SD((FF, D), BF), SD((D, FF), BF), SD((D, D), BF), SD((PICKS, D), FL), SD((PICKS, D), BF), SD((8, D), FL),
        ],
        [pltpu.VMEM((PICKS, D), FL)],
        [df, x2, x1, h2, z, act, mixed, p_all, u_all, c_all, norm_rows],
        "feed_back", flops=4 * 10**9, moved=30 * 10**6,
    )
    da, dx = run(
        attend_back_kernel,
        [SD((D, 3 * D + EXTRA), BF), SD((SEQ_LEN, D), BF)],
        [
            pltpu.VMEM((KEYS, 2 * D), BF), pltpu.VMEM((PICKS, D), BF), pltpu.VMEM((D, KEYS), BF),
            pltpu.VMEM((SEQ_LEN, D), FL), pltpu.VMEM((SEQ_LEN, D), FL), pltpu.VMEM((SLOTS * NB, D), BF),
        ],
        [counted, dmixed, q, kv, lse, hall, hq, a_all, x, dx1, mixing_t, keys, queries, norm_rows, dnorm],
        "attend_back", flops=12 * 10**9, moved=25 * 10**6,
        in_specs=[SM] + [VM] * 14,
    )
    sums = [
        lax.psum(lax.psum_scatter(item, "batch", scatter_dimension=0, tiled=True), "vocab").astype(FL)
        for item in (dc, du, dp, da)
    ]
    extra = unembed(nb, nv, cap, width, rows, dx, ids, place)

    def more_grads(state):
        turn, total = state
        later = later_slots(nv, cap, rows, every, turn)
        return turn + 1, total + unembed(
            nb, nv, cap, width, rows, dx, later, place - jnp.array([0, 1, 0, 0, 0, 0, 0, 0], I32)[None, :, None] * (turn * cap)
        )

    extra = lax.while_loop(lambda state: state[0] < turns, more_grads, (jnp.int32(1), extra))[1]

    grad_table = dw_sum.astype(FL) + extra
    grad_c, grad_u, grad_p, grad_a = sums
    grad_norms = grad_a[:, 3 * D : 3 * D + 6].T
    grad_a = grad_a[:, : 3 * D]
    at_root = (lax.axis_index("vocab") == 0).astype(FL)
    owned = sum(jnp.sum(item * item) for item in (grad_a, grad_p, grad_u, grad_c, grad_norms))
    squares, loss = lax.psum(
        (jnp.sum(grad_table * grad_table) + at_root * owned, at_root * loss_part), ("batch", "vocab")
    )
    gradient_norm = jnp.sqrt(squares)
    clip = jnp.minimum(1.0, MAX_NORM / (gradient_norm + 1e-06))
    count = step_count[0].astype(FL)

    def update(weight, moment, square, gradient, decay=DECAY, rate=LEARN_RATE):
        return adamw(weight, moment, square, gradient, clip, count, decay, rate)

    table_out = [item.T for item in update(table_t, table_moment.T, table_square.T, grad_table)]
    attend_out = update(attend, attend_moment, attend_square, grad_a[None])
    project_out = update(project, project_moment, project_square, grad_p[None])
    expand_out = update(expand, expand_moment, expand_square, grad_u[None])
    contract_out = update(contract, contract_moment, contract_square, grad_c[None])
    gain_out = update(gain, gain_moment, gain_square, grad_norms[:3], 0.0, NORM_RATE)
    shift_out = update(shift, shift_moment, shift_square, grad_norms[3:], 0.0, NORM_RATE)
    return (
        loss, gradient_norm, *table_out, *attend_out, *project_out, *expand_out, *contract_out, *gain_out, *shift_out,
    )


def solution(mesh):
    nb, nv = mesh.shape["batch"], mesh.shape["vocab"]
    both, split, middle, last = P(("batch", "vocab")), P("vocab", "batch"), P(None, "batch", None), P(None, "batch")
    state = (split,) * 3 + (middle,) * 12 + (last,) * 6
    return jax.shard_map(
        functools.partial(shards, nb, nv),
        mesh=mesh,
        in_specs=(P("batch"), P("batch"), both, both, P("vocab"), P()) + state,
        out_specs=(P(), P()) + state,
        check_vma=False,
    )
```

time: 1690 us -> 994 us (0.59)
  matrix products: 412 us -> 0 us
  Pallas kernels: 0 us -> 386 us
  other arithmetic: 323 us -> 66.2 us
  waiting for transfers between devices: 615 us -> 419 us
  local copies, waits for them, and re-layouts: 205 us -> 33.9 us
  blocking collectives: 99.7 us -> 39.4 us
    dot_general x33 -> x0, matrix products: 412 us -> none  [the longest x4 67.3 us: block_scores(): jnp.einsum('bqhd,bkhd->bhqk', query_block, keys, preferred_element_type=FL)]
    pallas_call x0 -> x7, Pallas kernels: none -> 386 us  [run(): pl.pallas_call(kernel, out_shape=outs, in_specs=in_specs if in_specs is n...]
    all_gather x7 -> x5, waiting for transfers between devices: 269 us -> 135 us  [the longest x1 93.1 us: shards(): words = lax.all_gather(table_t.astype(BF), 'batch', axis=0, tiled=True)]
    convert_element_type x18 -> x7, other arithmetic: 122 us -> 14.1 us  [the longest x1 4.08 us: shards(): words = lax.all_gather(table_t.astype(BF), 'batch', axis=0, tiled=True)]
    unnamed x20 -> x11, waiting for transfers between devices: 89.3 us -> 2.14 us
    reduce_sum x22 -> x6, other arithmetic: 80.4 us -> 6.27 us  [the longest x5 6.12 us: shards(): jnp.sum(item * item)]
    scatter-add x2 -> x0, other arithmetic: 71.1 us -> none  [the longest x1 66.9 us: shards(): grad_table.at[places]]
    unnamed x216 -> x77, local copies, waits for them, and re-layouts: 75.3 us -> 11.2 us
  transfers between devices with their start and end apart: 17 -> 11, of which waited for: 9 -> 7; matrix products, arithmetic and copies ran while one was open for 37% -> 5% of each run, Pallas kernels for 0% -> 27%
where the time goes in v1:
time: 994 us; the launch traced here: 986 us
  waiting for transfers between devices  419 us (42%)
  Pallas kernels  386 us (39%)
  other arithmetic  66.2 us (7%)
  blocking collectives  39.4 us (4%)
  local copies, waits for them, and re-layouts  33.9 us (3%)
  between operations  22.5 us (2%)
  loops' own time  18.2 us (2%)
    pallas_call x7, Pallas kernels, run(): pl.pallas_call(kernel, out_shape=outs, in_specs=in_specs if in_specs is n...  386 us
    reduce_scatter x4, waiting for transfers between devices, shards(): lax.psum_scatter(item, 'batch', scatter_dimension=0, tiled=True)  171 us
    all_gather x1, waiting for transfers between devices, shards(): words = lax.all_gather(table_t.astype(BF), 'batch', axis=0, tiled=True)  93.1 us
    reduce_scatter x1, waiting for transfers between devices, shards(): dw_sum = lax.psum_scatter(dw, 'batch', scatter_dimension=0, tiled=True)  91.6 us
    all_gather x1, waiting for transfers between devices, shards(): c_all = lax.all_gather(contract[0].astype(BF), 'batch', axis=0, tiled=True)  41.7 us
    psum x1, blocking collectives, shards(): lax.psum((jnp.sum(grad_table * grad_table) + at_root * owned, at_root * l...  39.4 us
    sub x6, other arithmetic, adamw(): weight - rate * (fixed_moment / (jnp.sqrt(fixed_square) + ADAM_EPS) + dec...  22.7 us
  transfers between devices with their start and end apart: 11, of which 7 were waited for; matrix products, arithmetic and copies ran while one was open for 5% of the time, Pallas kernels for 27%

profile of v1, /device:TPU:0, one launch (start us, length us, event | category | flops | bytes accessed | tf_op | source)
XLA Modules:
  0.0 986.0 jit_solution(13666197162102122690)
XLA Ops:
  7.3 1.6 convert_bitcast_fusion.1
  9.1 1.1 concatenate.16
  10.2 1.8 convert_element_type.103
  12.1 1.2 convert_element_type.105
  13.4 2.8 convert_element_type.107
  16.3 4.1 bitcast_convert_fusion
  21.1 104.5 %embed.2 = (bf16[1024,768]{1,0:T(8,128)(2,1)S(1)}, s32[8,768,1]{2,1,0:T(8,128)}, s32[4,8,1024]{2,1,0:T(8,128)S(1)}, f32[8,128]{1,0:T(8,128)}, s32[4,8,1024]{2,1,0:T(8,128)S(1)}) custom-call(s32[1]{0:T(128)} %constant.63.clone.1.round_ref, s32[8,1024]{1,0:T(8,128)S(1)} %reshape.246.tok_ref, f32[192,6400]{1,0:T(8,128)} %bitcast.112), custom_call_target="tpu_custom_call" | custom-call | tf_op jit(solution)/shard_map/embed/pallas_call | solution.py:67
  125.6 1.2 slice.42
  127.5 1.6 mul.382
  129.1 2.9 copy.207
  132.2 1.6 sub.159
  133.8 2.9 copy.206
  137.4 2.8 divide_convert_fusion
  140.3 1.3 copy.183.mix_ref
  142.5 1.2 copy.185.key_ref
  145.4 8.9 while.23
  154.9 2.6 fusion.30
  158.2 22.4 %attend.1 = (bf16[1536,768]{1,0:T(8,128)(2,1)}, bf16[1536,1536]{1,0:T(8,128)(2,1)}, bf16[128,768]{1,0:T(8,128)(2,1)}, bf16[128,768]{1,0:T(8,128)(2,1)}, f32[128,...) custom-call(bf16[1024,768]{1,0:T(8,128)(2,1)S(1)} %get-tuple-element.175.x_ref, ...), custom_call_target="tpu_custom_call" | custom-call | flops 7000000000 | bytes 20000000 | tf_op jit(solution)/shard_map/attend/pallas_call | solution.py:67
  180.6 41.7 %all-gather.17.cloned.1.call-done = bf16[1,3072,768]{2,1,0:T(8,128)(2,1)} async-done(((bf16[1,768,768]{2,1,0:T(8,128)(2,1)}), bf16[1,3072,768]{2,1,0:T(8,128)(2,1)}) %all-gather.17.cloned.1.call-update) | async-done | bytes 4718608 | tf_op jit(solution)/shard_map/all_gather | solution.py:842
  222.3 8.8 feed.1
  231.1 93.1 %all-gather.11.cloned.1.call-done.w_ref = bf16[768,6400]{1,0:T(8,128)(2,1)} async-done(((bf16[192,6400]{1,0:T(8,128)(2,1)}), bf16[768,6400]{1,0:T(8,128)(2,1)}) %all-gather.11.cloned.1.call-update) | async-done | bytes 9830416 | tf_op jit(solution)/shard_map/all_gather | solution.py:843
  324.2 107.9 %head.1 = (f32[128,768]{1,0:T(8,128)}, bf16[768,6400]{1,0:T(8,128)(2,1)}, f32[8,128]{1,0:T(8,128)}) custom-call(bf16[128,768]{1,0:T(8,128)(2,1)} %get-tuple-element.179.f_ref, bf16[768,6400]{1,0:T(8,128)(2,1)} %all-gather.11.cloned.1.call-done.w_ref, s32[1,6400]{1,0:T(1,128)} %broadcast_in_dim.91.live_ref, s32[1024,1]{1,0:T(8,128)} %copy.186.target_ref), custom_call_target="tpu_custom_call" | custom-call | tf_op jit(solution)/shard_map/head/pallas_call | solution.py:67
  432.1 15.1 %feed_back.1 = (bf16[3072,768]{1,0:T(8,128)(2,1)}, bf16[768,3072]{1,0:T(8,128)(2,1)}, bf16[768,768]{1,0:T(8,128)(2,1)}, f32[128,768]{1,0:T(8,128)}, bf16[128,768]{1,0:T(8,128)(2,1)}, /*index=5*/f32[8,768]{1,0:T(8,128)}) custom-call(f32[128,768]{1,0:T(8,128)} %get-tuple-element.182.df_ref, f32[128,768]{1,0:T(8,128)} %get-tuple-element.183.x2_ref, ...), custom_call_target="tpu_custom_call" | custom-call | flops 4000000000 | bytes 30000000 | tf_op jit(solution)/shard_map/feed_back/pallas_call | solution.py:67
  447.5 34.7 %attend_back.1 = (bf16[768,2432]{1,0:T(8,128)(2,1)}, bf16[1024,768]{1,0:T(8,128)(2,1)S(1)}) custom-call(s32[128]{0:T(128)} %pos_ref.1, bf16[128,768]{1,0:T(8,128)(2,1)} %get-tuple-element.188.do_ref, bf16[128,768]{1,0:T(8,128)(2,1)} %get-tuple-element.189.q_ref, bf16[1536,1536]{1,0:T(8,128)(2,1)} %get-tuple-element.190.kv_ref, ...), custom_call_target="tpu_custom_call" | custom-call | flops 12000000000 | bytes 25000000 | tf_op jit(solution)/shard_map/attend_back/pallas_call | solution.py:67
  483.8 50.0 %reduce-scatter.8.cloned.1.call-done = bf16[192,2432]{1,0:T(8,128)(2,1)} async-done(((bf16[768,2432]{1,0:T(8,128)(2,1)}), bf16[192,2432]{1,0:T(8,128)(2,1)}) %reduce-scatter.8.cloned.1.call-update) | async-done | bytes 933904 | tf_op jit(solution)/shard_map/reduce_scatter | solution.py:911
  533.8 60.7 %reduce-scatter.12.cloned.1.call-done = bf16[192,3072]{1,0:T(8,128)(2,1)} async-done(((bf16[768,3072]{1,0:T(8,128)(2,1)}), bf16[192,3072]{1,0:T(8,128)(2,1)}) %reduce-scatter.12.cloned.1.call-update) | async-done | bytes 1179664 | tf_op jit(solution)/shard_map/reduce_scatter | solution.py:911
  594.4 60.7 %reduce-scatter.14.cloned.1.call-done = bf16[768,768]{1,0:T(8,128)(2,1)} async-done(((bf16[3072,768]{1,0:T(8,128)(2,1)}), bf16[768,768]{1,0:T(8,128)(2,1)}) %reduce-scatter.14.cloned.1.call-update) | async-done | bytes 1179664 | tf_op jit(solution)/shard_map/reduce_scatter | solution.py:911
  660.7 1.2 slice.47
  662.5 93.1 %unembed.5 = f32[192,6400]{1,0:T(8,128)} custom-call(bf16[1024,768]{1,0:T(8,128)(2,1)S(1)} %get-tuple-element.504.x_ref, s32[8,768,1]{2,1,0:T(8,128)} %get-tuple-element.197.ids_ref, s32[4,8,1024]{2,1,0:T(8,128)S(1)} %get-tuple-element.503.place_ref), custom_call_target="tpu_custom_call" | custom-call | tf_op jit(solution)/shard_map/unembed/pallas_call | solution.py:67
  755.6 9.3 while.24
  764.9 18.9 %all-reduce.4.cloned.1.call-done = (bf16[192,2432]{1,0:T(8,128)(2,1)}, bf16[192,768]{1,0:T(8,128)(2,1)}, bf16[192,3072]{1,0:T(8,128)(2,1)}, bf16[768,768]{1,0:T(8,128)(2,1)}) async-done(((bf16[192,2432]{1,0:T(8,128)(2,1)}, bf16[192,768]{1,0:T(8,128)(2,1)}, bf16[192,3072]{1,0:T(8,128)(2,1)}, bf16[768,768]{1,0:T(8,128)(2,1)}), (bf16[192,2432]{1,0:T(8,128)(2,1)}, bf16[192,768]{1,0:T(8,128)(2,1)}, ...) | async-done | bytes 3588112 | tf_op jit(solution)/shard_map/psum | solution.py:911
  783.8 1.4 convert_element_type.111
  786.0 1.1 multiply_reduce_fusion.1
  788.3 2.5 fusion.8
  791.5 1.2 fusion.9
  794.6 91.6 %reduce-scatter.6.cloned.1.call-done = bf16[192,6400]{1,0:T(8,128)(2,1)} async-done(((bf16[768,6400]{1,0:T(8,128)(2,1)}), bf16[192,6400]{1,0:T(8,128)(2,1)}) %reduce-scatter.6.cloned.1.call-update) | async-done | bytes 2457616 | tf_op jit(solution)/shard_map/reduce_scatter | solution.py:888
  886.2 5.1 multiply_reduce_fusion
  891.9 39.4 %all-reduce = (f32[]{:T(128)}, f32[]{:T(128)}) all-reduce(f32[]{:T(128)S(6)} %mul.391, f32[]{:T(128)S(6)} %add.230), channel_id=1, replica_groups=mesh['batch'=4,'vocab'=8] {'batch','vocab'}, use_global_device_ids=true, to_apply=%region_5.6 | all-reduce | flops 2 | bytes 16 | tf_op jit(solution)/shard_map/psum | solution.py:931
  932.0 1.9 multiply_divide_fusion
  936.6 1.6 copy.201
  938.2 1.6 copy.202
  942.5 1.6 copy.204
  944.0 1.6 copy.205
  945.6 5.9 multiply_subtract_fusion.2
  951.5 1.5 multiply_subtract_fusion.3
  954.2 6.2 multiply_subtract_fusion.1
  960.4 7.3 multiply_subtract_fusion
  967.8 10.3 %fusion.32 = (f32[6400,192]{0,1:T(8,128)}, f32[6400,192]{0,1:T(8,128)}, f32[6400,192]{0,1:T(8,128)}) fusion(f32[]{:T(128)S(6)} %min.3, f32[192,6400]{1,0:T(8,128)S(1)} %bitcast.111, bf16[192,6400]{1,0:T(8,128)(2,1)S(1)} %copy-done.1, f32[6400,192]{0,1:T(8,128)S(1)} %bitcast.120, f32[]{:T(128)} %bitcast.25, f32[]{:T(128)} %bitcast.23, ...), kind=kLoop, calls=%fused_computation.106 | loop fusion | flops 22118400 | bytes 36864012 | tf_op jit(solution)/shard_map/transpose | solution.py:941
  (146 shorter events, 20.6 us)
Async XLA Ops:
  7.2 1.6 copy-start.15
  7.2 1.7 copy-start.14
  7.2 151.0 %all-gather.9.cloned.1.call-start = ((), (), s32[]{:S(2)}) async-start(), calls=%async_computation.5 | async-start | bytes 4669440 | tf_op jit(solution)/shard_map/all_gather | solution.py:839
  8.8 3.3 copy-start.2
  10.2 170.4 %all-gather.13.cloned.1.call-start = ((), (), s32[]{:S(2)}) async-start(), calls=%async_computation.12 | async-start | bytes 1474560 | tf_op jit(solution)/shard_map/all_gather | solution.py:840
  12.1 168.5 %all-gather.15.cloned.1.call-start = ((), (), s32[]{:S(2)}) async-start(), calls=%async_computation.13 | async-start | bytes 5898240 | tf_op jit(solution)/shard_map/all_gather | solution.py:841
  13.3 209.0 %all-gather.17.cloned.1.call-start = ((), (), s32[]{:S(2)}) async-start(), calls=%async_computation.14 | async-start | bytes 5898240 | tf_op jit(solution)/shard_map/all_gather | solution.py:842
  16.2 308.0 %all-gather.11.cloned.1.call-start = ((), (), s32[]{:S(2)}) async-start(), calls=%async_computation.6 | async-start | bytes 12288000 | tf_op jit(solution)/shard_map/all_gather | solution.py:843
  20.3 0.8 copy-start.16
  20.4 463.4 %reduce-scatter.10.cloned.1.call-start = ((), (), s32[]{:S(2)}) async-start(), calls=%async_computation.9 | async-start | bytes 1474560 | tf_op jit(solution)/shard_map/reduce_scatter | solution.py:911
  21.1 106.4 %copy-start.13 = (s32[1024]{0:T(1024)S(1)}, s32[1024]{0:T(1024)}, u32[]{:S(2)}) copy-start(s32[1024]{0:T(1024)} %param.34) | copy-start | bytes 12292
  137.4 4.2 copy-start.19
  137.4 5.1 copy-start.18
  140.3 5.2 copy-start.7
  140.3 3.5 copy-start.17
  140.3 4.1 copy-start.20
  154.3 26.2 %copy-start = (bf16[1024,768]{1,0:T(8,128)(2,1)}, bf16[1024,768]{1,0:T(8,128)(2,1)S(1)}, u32[]{:S(2)}) copy-start(bf16[1024,768]{1,0:T(8,128)(2,1)S(1)} %get-tuple-element.175.x_ref) | copy-start | bytes 4718596
  447.2 86.5 %reduce-scatter.8.cloned.1.call-start = ((), (), s32[]{:S(2)}) async-start(), calls=%async_computation.8 | async-start | bytes 4669440 | tf_op jit(solution)/shard_map/reduce_scatter | solution.py:911
  482.2 112.2 %reduce-scatter.12.cloned.1.call-start = ((), (), s32[]{:S(2)}) async-start(), calls=%async_computation.10 | async-start | bytes 5898240 | tf_op jit(solution)/shard_map/reduce_scatter | solution.py:911
  483.0 172.2 %reduce-scatter.14.cloned.1.call-start = ((), (), s32[]{:S(2)}) async-start(), calls=%async_computation.11 | async-start | bytes 5898240 | tf_op jit(solution)/shard_map/reduce_scatter | solution.py:911
  483.7 300.1 %all-reduce.4.cloned.1.call-start = ((), (), s32[]{:S(2)}) async-start(), calls=%async_computation.15 | async-start | bytes 7176192 | tf_op jit(solution)/shard_map/psum | solution.py:911
  655.1 231.1 %reduce-scatter.6.cloned.1.call-start = ((), (), s32[]{:S(2)}) async-start(), calls=%async_computation.7 | async-start | bytes 12288000 | tf_op jit(solution)/shard_map/reduce_scatter | solution.py:888
  655.2 3.0 copy-start.21
  655.2 3.1 copy-start.22
  655.2 3.9 copy-start.23
  655.2 4.6 copy-start.24
  662.5 93.1 %copy-start.25 = (s32[8]{0:T(128)S(1)}, s32[8]{0:T(128)}, u32[]{:S(2)}) copy-start(s32[8]{0:T(128)} %constant.171.clone..sunk.2) | copy-start | bytes 100
  783.8 1.4 copy-start.10
  783.8 7.7 copy-start.5
  945.6 5.9 copy-start.9
  945.6 5.9 copy-start.11
  945.6 5.9 copy-start.12
  945.6 7.4 copy-start.8
  951.5 2.3 copy-start.3
  951.5 2.6 copy-start.6
  954.1 6.2 copy-start.4
  954.1 13.6 %slice-start = ((s8[4915200]{0:T(1024)(128)(4,1)}), s8[4194304]{0:T(1024)(128)(4,1)S(1)}, s32[]{:S(2)}) async-start(s8[4915200]{0:T(1024)(128)(4,1)} %bitcast.110), calls=%async_computation.16 | async-start | bytes 8388608
  954.1 13.6 %slice-start.2 = ((s8[4915200]{0:T(1024)(128)(4,1)}), s8[4194304]{0:T(1024)(128)(4,1)S(1)}, s32[]{:S(2)}) async-start(s8[4915200]{0:T(1024)(128)(4,1)} %bitcast.114), calls=%async_computation.18 | async-start | bytes 8388608
  954.2 13.6 %slice-start.4 = ((s8[4915200]{0:T(1024)(128)(4,1)}), s8[4194304]{0:T(1024)(128)(4,1)S(1)}, s32[]{:S(2)}) async-start(s8[4915200]{0:T(1024)(128)(4,1)} %bitcast.119), calls=%async_computation.20 | async-start | bytes 8388608
  960.3 7.4 slice-start.1
  960.3 7.4 slice-start.3
  960.3 7.4 copy-start.1
  960.3 7.4 slice-start.5
Sparse Core Ops, SparseCore 0:
  10.5 52.9 all-gather.8
  65.9 27.7 all-gather.12
  96.1 66.8 all-gather.14
  165.2 57.0 all-gather.16
  224.6 99.5 all-gather.10
  447.4 31.0 reduce-scatter.9
  482.3 51.3 reduce-scatter.7
  537.3 57.0 reduce-scatter.11
  598.0 57.0 reduce-scatter.13
  657.6 126.0 all-reduce.3
  787.2 98.9 reduce-scatter.5

commit v2 on v1

--- a/solution.py
+++ b/solution.py
@@ -21,7 +21,8 @@
 BLK = 256
 PAIR = 2 * HD
 NPAIR = H // 2
-EXTRA = 128
+EXTRA = 256
+WIDE = (3 * D + EXTRA, D, FF, D)
 
 NORM_EPS = 1e-05
 MAX_NORM = 0.02
@@ -110,14 +111,19 @@
 
 
 def embed_kernel(
-    nb, nv, cap, part, round_ref, tok_ref, table_ref, x_ref, ids_ref, place_ref, most_ref, tok_ref_all,
-    words, before, ranks, work, sent, got, spread, mixed, turned,
-    tok_out, tok_in, row_out, row_in, mix_out, mix_in,
+    nb, nv, cap, part, first, *refs
 ):
+    round_ref, tok_ref, table_ref = refs[:3]
+    shards, refs = (refs[3:7], refs[7:]) if first else ((), refs[3:])
+    x_ref, ids_ref, place_ref, most_ref, tok_ref_all = refs[:5]
+    wholes, refs = (refs[5:9], refs[9:]) if first else ((), refs[5:])
+    words, before, ranks, work, sent, got, spread, mixed, turned = refs[:9]
+    tok_out, tok_in, row_out, row_in, mix_out, mix_in = refs[9:15]
     b, v = lax.axis_index("batch"), lax.axis_index("vocab")
     width, rows = table_ref.shape
     shift = round_ref[0] * cap
     meet((("batch", nb), ("vocab", nv)))
+    gather = WeightGather(nb, shards, wholes, *refs[15:20]) if first else None
 
     def tok_copy(step):
         return send(
@@ -126,6 +132,8 @@
 
     for step in range(1, nb):
         tok_copy(step).start()
+    if first:
+        gather.start()
     tok_ref_all[b] = tok_ref[...]
     words[...] = table_ref[...].astype(BF)
     before[...] = (iota((SEQ_LEN, SEQ_LEN), 0) < iota((SEQ_LEN, SEQ_LEN), 1)).astype(FL).astype(BF)
@@ -182,6 +190,8 @@
             got[v] = block
 
     each(1, nv + 1, build)
+    if first:
+        gather.pass_on()
 
     keys = []
     for p in range(nb):
@@ -225,9 +235,91 @@
     for step in range(1, nb):
         mix_copy(step).wait()
     x_ref[...] = turned[...].reshape(nb * width, SEQ_LEN).T
-
-
-def embed(nb, nv, cap, turn, tok, table):
+    if first:
+        gather.finish()
+
+
+class WeightGather:
+    def __init__(self, nb, shards, wholes, own_sem, out_sem, in_sem, pair_out, pair_in):
+        self.nb, self.shards, self.wholes = nb, shards, wholes
+        self.own_sem, self.out_sem, self.in_sem, self.pair_out, self.pair_in = own_sem, out_sem, in_sem, pair_out, pair_in
+        self.b, v = lax.axis_index("batch"), lax.axis_index("vocab")
+        self.core = lax.rem(v, 2)
+        self.sibling = {"vocab": v + 1 - 2 * self.core}
+
+    def flip(self, bits):
+        b = self.b
+        low, high = lax.rem(b, 2), b // 2
+        return (high if bits < 2 else 1 - high) * 2 + (low if bits % 2 == 0 else 1 - low)
+
+    def place(self, w, owner, top, size):
+        rows, cols = self.shards[w].shape
+        first = pl.multiple_of(owner * rows + top, 16)
+        return self.wholes[w].at[pl.ds(first, size), lanes(self.core * (cols // 2), cols // 2)]
+
+    def routes(self, w):
+        rows = self.shards[w].shape[0]
+        if self.nb == 4:
+            half = rows // 2
+            return [
+                (self.b, 0, rows, self.flip(1), self.flip(1)),
+                (self.b, 0, rows, self.flip(2), self.flip(2)),
+                (self.flip(1), 0, half, self.flip(2), self.flip(3)),
+                (self.flip(2), half, half, self.flip(1), self.flip(3)),
+            ]
+        others = [lax.rem(self.b + step, self.nb) for step in range(1, self.nb)]
+        came = [lax.rem(self.b - step + self.nb, self.nb) for step in range(1, self.nb)]
+        return [(self.b, 0, rows, other, source) for other, source in zip(others, came)]
+
+    def own_copy(self, w):
+        rows = self.shards[w].shape[0]
+        first = pl.multiple_of(self.b * rows, 16)
+        return pltpu.make_async_copy(self.shards[w], self.wholes[w].at[pl.ds(first, rows), :], self.own_sem.at[w])
+
+    def copy(self, w, k):
+        owner, top, size, device, _ = self.routes(w)[k]
+        cols = self.shards[w].shape[1]
+        if self.nb == 4 and k >= 2:
+            source = self.place(w, owner, top, size)
+        else:
+            source = self.shards[w].at[:, lanes(self.core * (cols // 2), cols // 2)]
+        target = self.place(w, owner, top, size)
+        return send(source, target, self.out_sem.at[w, k], self.in_sem.at[w, k], {"batch": device})
+
+    def pair(self, w, k):
+        _, top, size, _, arrived = self.routes(w)[k]
+        ref = self.place(w, arrived, top, size)
+        return send(ref, ref, self.pair_out.at[w, k], self.pair_in.at[w, k], self.sibling)
+
+    def start(self):
+        for w in range(4):
+            for k in range(2 if self.nb == 4 else self.nb - 1):
+                self.copy(w, k).start()
+        for w in range(4):
+            self.own_copy(w).start()
+
+    def pass_on(self):
+        if self.nb != 4:
+            return
+        for w in range(4):
+            for k in range(2):
+                self.copy(w, k).wait_recv()
+                self.copy(w, k + 2).start()
+                self.pair(w, k).start()
+
+    def finish(self):
+        for w in range(4):
+            for k in range(2 if self.nb == 4 else 0, len(self.routes(w))):
+                self.copy(w, k).wait_recv()
+                self.pair(w, k).start()
+        for w in range(4):
+            self.own_copy(w).wait()
+            for k in range(len(self.routes(w))):
+                self.copy(w, k).wait_send()
+                self.pair(w, k).wait()
+
+
+def embed(nb, nv, cap, turn, tok, table, shards=()):
     width, rows = table.shape
     part = chunk_of(rows, 640)
     count = nb * cap
@@ -238,6 +330,8 @@
         SD((8, 128), FL),
         SD((nb, nv, SEQ_LEN), I32),
     ]
+    first = len(shards) > 0
+    outs += [SD((nb * item.shape[0], item.shape[1]), BF) for item in shards]
     dma = pltpu.SemaphoreType.DMA
     scratch = [
         pltpu.VMEM((width, rows), BF),
@@ -251,16 +345,186 @@
         pltpu.VMEM((nb, width, SEQ_LEN), BF),
         dma((nb,)), dma((nb,)), dma((nv,)), dma((nv,)), dma((nb,)), dma((nb,)),
     ]
+    if first:
+        scratch += [dma((4,)), dma((4, 4)), dma((4, 4)), dma((4, 4)), dma((4, 4))]
     return run(
-        functools.partial(embed_kernel, nb, nv, cap, part), outs, scratch, [turn, tok, table], "embed", 0,
-        in_specs=[SM, VM, VM],
-    )
-
-
-def unembed_kernel(
-    nb, nv, cap, part, x_ref, ids_ref, place_ref, out_ref,
-    turned, parts, sent, got, mix_out, mix_in, row_out, row_in,
-):
+        functools.partial(embed_kernel, nb, nv, cap, part, first), outs, scratch, [turn, tok, table, *shards],
+        "embed" if first else "embed_more", 0 if first else 3,
+        in_specs=[SM, VM, VM] + [HB] * len(shards), out_specs=[VM] * 5 + [HB] * len(shards),
+    )
+
+
+class GradientSum:
+    def __init__(self, nb, nv, grads, sums, refs):
+        self.nb, self.nv, self.grads, self.sums = nb, nv, grads, sums
+        self.own, self.near, self.shard, self.total = refs[0:4], refs[4:8], refs[8:12], refs[12:16]
+        self.bits, self.result = refs[16:20], refs[20:24]
+        (self.load_sem, self.pair_out, self.pair_in, self.mix_out, self.mix_in, self.cut_out, self.cut_in,
+         self.all_out, self.all_in, self.last_out, self.last_in, self.store_sem) = refs[24:36]
+        self.b, v = lax.axis_index("batch"), lax.axis_index("vocab")
+        self.core, self.chip, self.chips = lax.rem(v, 2), v // 2, nv // 2
+        self.sibling = {"vocab": v + 1 - 2 * self.core}
+
+    def half(self, w, core):
+        cols = self.grads[w].shape[1] // 2
+        return lanes(core * cols, cols)
+
+    def load(self, w):
+        return pltpu.make_async_copy(self.grads[w].at[:, self.half(w, self.core)], self.own[w], self.load_sem.at[w])
+
+    def pair(self, w):
+        source = self.grads[w].at[:, self.half(w, 1 - self.core)]
+        return send(source, self.near[w], self.pair_out.at[w], self.pair_in.at[w], self.sibling)
+
+    def start(self):
+        for w in range(4):
+            self.pair(w).start()
+            self.load(w).start()
+
+    def mix(self, w, step):
+        other = lax.rem(self.b + step, self.nb)
+        rows = self.own[w].shape[0] // self.nb
+        source = self.own[w].at[pl.ds(pl.multiple_of(other * rows, 16), rows), :]
+        return send(source, self.shard[w].at[step], self.mix_out.at[w, step], self.mix_in.at[w, step], {"batch": other})
+
+    def scatter(self):
+        for w in range(4):
+            self.load(w).wait()
+            self.pair(w).wait()
+            rows = self.own[w].shape[0] // self.nb
+
+            def add(i, w=w, rows=rows):
+                cut = pl.ds(pl.multiple_of(i * rows, 16), rows)
+                self.own[w][cut, :] = (self.own[w][cut, :].astype(FL) + self.near[w][cut, :].astype(FL)).astype(BF)
+
+            each(0, self.nb, add)
+            for step in range(1, self.nb):
+                self.mix(w, step).start()
+
+    def pieces(self, w):
+        rows = self.total[w].shape[0]
+        count = max(n for n in range(1, self.chips + 1) if rows % (16 * n) == 0)
+        return count, rows // count
+
+    def peer(self, step):
+        other = lax.rem(self.chip + step, self.chips)
+        return other, {"vocab": other * 2 + self.core}
+
+    def cut(self, w, step):
+        other, device = self.peer(step)
+        size = self.pieces(w)[1]
+        source = self.total[w].at[pl.ds(pl.multiple_of(other * size, 16), size), :]
+        return send(source, self.bits[w].at[step], self.cut_out.at[w, step], self.cut_in.at[w, step], device)
+
+    def back(self, w, step):
+        size = self.pieces(w)[1]
+        place = self.result[w].at[pl.ds(pl.multiple_of(self.chip * size, 16), size), :]
+        return send(place, place, self.all_out.at[w, step], self.all_in.at[w, step], self.peer(step)[1])
+
+    def back_recv(self, w, step):
+        source = lax.rem(self.chip - step + self.chips, self.chips)
+        size = self.pieces(w)[1]
+        place = self.result[w].at[pl.ds(pl.multiple_of(source * size, 16), size), :]
+        return send(place, place, self.all_out.at[w, step], self.all_in.at[w, step], self.peer(step)[1])
+
+    def reduce(self):
+        for w in range(4):
+            rows = self.total[w].shape[0]
+            for step in range(1, self.nb):
+                self.mix(w, step).wait()
+            here = pl.ds(pl.multiple_of(self.b * rows, 16), rows)
+            value = self.own[w][here, :].astype(FL)
+            for step in range(1, self.nb):
+                value = value + self.shard[w][step].astype(FL)
+            self.total[w][...] = value.astype(BF)
+            count = self.pieces(w)[0]
+
+            def go(step, w=w, count=count):
+                @pl.when(self.peer(step)[0] < count)
+                def _():
+                    self.cut(w, step).start()
+
+            each(1, self.chips, go)
+
+    def collect(self):
+        for w in range(4):
+            count, size = self.pieces(w)
+            mine = pl.ds(pl.multiple_of(self.chip * size, 16), size)
+
+            @pl.when(self.chip < count)
+            def _(w=w, mine=mine):
+                def add(step, value):
+                    self.cut(w, step).wait_recv()
+                    return value + self.bits[w][step].astype(FL)
+
+                value = lax.fori_loop(1, self.chips, add, self.total[w][mine, :].astype(FL))
+                self.result[w][mine, :] = value.astype(BF)
+                each(1, self.chips, lambda step: self.back(w, step).start())
+
+            def sent(step, w=w, count=count):
+                @pl.when(self.peer(step)[0] < count)
+                def _():
+                    self.cut(w, step).wait_send()
+
+            each(1, self.chips, sent)
+
+    def last(self, w):
+        return send(
+            self.result[w], self.sums[w].at[:, self.half(w, self.core)], self.last_out.at[w], self.last_in.at[w], self.sibling
+        )
+
+    def store(self, w):
+        return pltpu.make_async_copy(self.result[w], self.sums[w].at[:, self.half(w, self.core)], self.store_sem.at[w])
+
+    def finish(self):
+        for w in range(4):
+            count = self.pieces(w)[0]
+
+            def got(step, w=w, count=count):
+                @pl.when(lax.rem(self.chip - step + self.chips, self.chips) < count)
+                def _():
+                    self.back_recv(w, step).wait_recv()
+
+            each(1, self.chips, got)
+            self.last(w).start()
+            self.store(w).start()
+        for w in range(4):
+            count = self.pieces(w)[0]
+
+            @pl.when(self.chip < count)
+            def _(w=w):
+                each(1, self.chips, lambda step: self.back(w, step).wait_send())
+
+            self.store(w).wait()
+            self.last(w).wait_send()
+            other = self.sums[w].at[:, self.half(w, 1 - self.core)]
+            send(other, other, self.last_out.at[w], self.last_in.at[w], self.sibling).wait_recv()
+
+
+def gradient_scratch(nb, nv, grads):
+    chips = nv // 2
+    halves = [(item.shape[0], item.shape[1] // 2) for item in grads]
+    shards = [(rows // nb, cols) for rows, cols in halves]
+    sizes = [rows // max(n for n in range(1, chips + 1) if rows % (16 * n) == 0) for rows, _ in shards]
+    dma = pltpu.SemaphoreType.DMA
+    return (
+        [pltpu.VMEM(item, BF) for item in halves] * 2
+        + [pltpu.VMEM((nb, *item), BF) for item in shards]
+        + [pltpu.VMEM(item, BF) for item in shards]
+        + [pltpu.VMEM((chips, size, item[1]), BF) for size, item in zip(sizes, shards)]
+        + [pltpu.VMEM(item, BF) for item in shards]
+        + [dma((4,)), dma((4,)), dma((4,)), dma((4, nb)), dma((4, nb)), dma((4, chips)), dma((4, chips))]
+        + [dma((4, chips)), dma((4, chips)), dma((4,)), dma((4,)), dma((4,))]
+    )
+
+
+def unembed_kernel(nb, nv, cap, part, first, *refs):
+    x_ref, ids_ref, place_ref = refs[:3]
+    grads, refs = (refs[3:7], refs[7:]) if first else ((), refs[3:])
+    out_ref = refs[0]
+    sums, refs = (refs[1:5], refs[5:]) if first else ((), refs[1:])
+    turned, parts, sent, got, mix_out, mix_in, row_out, row_in = refs[:8]
+    layer = GradientSum(nb, nv, grads, sums, refs[8:]) if first else None
     b, v = lax.axis_index("batch"), lax.axis_index("vocab")
     width, rows = out_ref.shape
     meet((("batch", nb), ("vocab", nv)))
@@ -272,6 +536,8 @@
 
     for step in range(1, nb):
         mix_copy(step).start()
+    if first:
+        layer.start()
     parts[b] = turned[b]
     for step in range(1, nb):
         mix_copy(step).wait()
@@ -301,6 +567,8 @@
             got[v] = block
 
     each(1, nv + 1, build)
+    if first:
+        layer.scatter()
     out_ref[...] = jnp.zeros_like(out_ref)
 
     def take(step):
@@ -318,10 +586,16 @@
 
         each(0, rows // part, piece)
 
-    each(0, nv, take)
-
-
-def unembed(nb, nv, cap, width, rows, grad, ids, place):
+    each(0, nv // 2, take)
+    if first:
+        layer.reduce()
+    each(nv // 2, nv, take)
+    if first:
+        layer.collect()
+        layer.finish()
+
+
+def unembed(nb, nv, cap, width, rows, grad, ids, place, grads=()):
     part = chunk_of(rows, 640)
     count = nb * cap
     dma = pltpu.SemaphoreType.DMA
@@ -332,10 +606,19 @@
         pltpu.VMEM((nv, width, count), BF),
         dma((nb,)), dma((nb,)), dma((nv,)), dma((nv,)),
     ]
+    first = len(grads) > 0
+    if first:
+        scratch += gradient_scratch(nb, nv, grads)
     return run(
-        functools.partial(unembed_kernel, nb, nv, cap, part), [SD((width, rows), FL)], scratch,
-        [grad, ids, place], "unembed", 2,
-    )[0]
+        functools.partial(unembed_kernel, nb, nv, cap, part, first),
+        [SD((width, rows), FL)] + [SD((item.shape[0] // nb, item.shape[1]), BF) for item in grads],
+        scratch,
+        [grad, ids, place, *grads],
+        "unembed" if first else "unembed_more",
+        2 if first else 4,
+        in_specs=[VM] * 3 + [HB] * len(grads),
+        out_specs=[VM] + [HB] * len(grads),
+    )
 
 
 def later_slots(nv, cap, rows, every, turn):
@@ -374,11 +657,24 @@
     return (key_ref[:, 0:1] == query_ref[0:1, :]) & (key_ref[:, 1:2] <= query_ref[1:2, :])
 
 
+def memory_weights(segments, slot):
+    length = segments.shape[1]
+    inside = (segments == slot).astype(FL)
+    start = jnp.sum((segments < slot).astype(FL), axis=1, keepdims=True)
+    count = jnp.sum(inside, axis=1, keepdims=True)
+    times = (iota((1, length), 1).astype(FL) - start + 0.5) / jnp.maximum(count, 1.0)
+    centres = (iota((NB, 1), 0).astype(FL) + 0.5) / NB
+    offset = (times - centres) * NB
+    basis = jnp.exp(-0.5 * offset * offset) * inside
+    total = jnp.sum(basis, axis=1, keepdims=True) + (count == 0.0).astype(FL)
+    return basis / total
+
+
 def attend_kernel(
-    x_ref, a_ref, mix_ref, pick_ref, key_ref, query_ref,
-    hall_ref, kv_ref, q_ref, hq_ref, xq_ref, o_ref, lse_ref, norm_ref,
+    x_ref, a_ref, seg_ref, pick_ref, key_ref, query_ref,
+    hall_ref, kv_ref, q_ref, hq_ref, xq_ref, o_ref, lse_ref, norm_ref, mixt_ref,
 ):
-    norm_ref[...] = a_ref[:, 3 * D :].astype(FL).T[:8, :]
+    norm_ref[...] = a_ref[:, 3 * D : 3 * D + 128].astype(FL).T[:8, :]
     gain, bias = norm_ref[0:1, :], norm_ref[3:4, :]
 
     def normalize(i):
@@ -387,7 +683,10 @@
 
     each(0, SEQ_LEN // BLK, normalize)
     normed = hall_ref[SLOTS * NB :, :]
-    hall_ref[: SLOTS * NB, :] = nn(mix_ref[...], normed).astype(BF)
+    for slot in range(SLOTS):
+        mixing = memory_weights(seg_ref[...], slot).astype(BF)
+        hall_ref[slot * NB : (slot + 1) * NB, :] = nn(mixing, normed).astype(BF)
+        mixt_ref[:, slot * NB : (slot + 1) * NB] = mixing.T
 
     def project(i):
         kv_ref[pl.ds(i * BLK, BLK), :] = nn(hall_ref[pl.ds(i * BLK, BLK), :], a_ref[:, D : 3 * D]).astype(BF)
@@ -790,21 +1089,6 @@
     )
 
 
-def memory_weights(segments):
-    length = segments.shape[0]
-    places = jnp.arange(length, dtype=I32)
-    slot_ids = jnp.arange(SLOTS, dtype=I32)
-    inside = segments[None, :] == slot_ids[:, None]
-    starts = jnp.sum((segments[None, :] < slot_ids[:, None]).astype(I32), axis=1)
-    counts = jnp.sum(inside.astype(I32), axis=1)
-    times = ((places[None, :] - starts[:, None]).astype(FL) + 0.5) / jnp.maximum(counts, 1)[:, None].astype(FL)
-    centres = (jnp.arange(NB, dtype=FL) + 0.5) / NB
-    offset = (times[:, None, :] - centres[None, :, None]) * NB
-    basis = jnp.exp(-0.5 * offset * offset) * inside[:, None, :].astype(FL)
-    total = jnp.sum(basis, axis=2, keepdims=True) + (counts == 0).astype(FL)[:, None, None]
-    return (basis / total).reshape(SLOTS * NB, length)
-
-
 def adamw(weight, moment, square, gradient, clip, count, decay, rate):
     gradient = gradient * clip
     moment = BETA_ONE * moment + (1 - BETA_ONE) * gradient
@@ -836,14 +1120,9 @@
     table_t = table.T
     norms = jnp.concatenate([gain, shift], axis=0)
     packed = jnp.concatenate([attend[0], norms.T, jnp.zeros((width, EXTRA - 6), FL)], axis=1).astype(BF)
-    a_all = lax.all_gather(packed, "batch", axis=0, tiled=True)
-    p_all = lax.all_gather(project[0].astype(BF), "batch", axis=0, tiled=True)
-    u_all = lax.all_gather(expand[0].astype(BF), "batch", axis=0, tiled=True)
-    c_all = lax.all_gather(contract[0].astype(BF), "batch", axis=0, tiled=True)
+    pieces = (packed, project[0].astype(BF), expand[0].astype(BF), contract[0].astype(BF))
     words = lax.all_gather(table_t.astype(BF), "batch", axis=0, tiled=True)
 
-    mixing = memory_weights(segments).astype(BF)
-    mixing_t = mixing.T
     key_seg = jnp.concatenate([jnp.repeat(jnp.arange(SLOTS, dtype=I32) + 1, NB), segments])
     key_pos = jnp.concatenate([jnp.full((SLOTS * NB,), -1, I32), jnp.arange(SEQ_LEN, dtype=I32)])
     keys = jnp.stack([key_seg, key_pos], axis=1)
@@ -854,7 +1133,9 @@
     queries = jnp.concatenate([query_seg[None], counted[None], jnp.zeros((6, PICKS), I32)], axis=0)
 
     tok = tokens.reshape(nv, SEQ_LEN)
-    x, ids, place, most, every = embed(nb, nv, cap, jnp.zeros((1,), I32), tok, table_t)
+    x, ids, place, most, every, a_all, p_all, u_all, c_all = embed(
+        nb, nv, cap, jnp.zeros((1,), I32), tok, table_t, pieces
+    )
     turns = (most[0, 0].astype(I32) + cap - 1) // cap
 
     def more_rows(state):
@@ -863,14 +1144,14 @@
 
     x = lax.while_loop(lambda state: state[0] < turns, more_rows, (jnp.int32(1), x))[1]
 
-    hall, kv, q, hq, xq, mixed, lse, norm_rows = run(
+    hall, kv, q, hq, xq, mixed, lse, norm_rows, mixing_t = run(
         attend_kernel,
         [
             SD((KEYS, D), BF), SD((KEYS, 2 * D), BF), SD((PICKS, D), BF), SD((PICKS, D), BF), SD((PICKS, D), FL),
-            SD((PICKS, D), BF), SD((NPAIR, 2, PICKS), FL), SD((8, D), FL),
+            SD((PICKS, D), BF), SD((NPAIR, 2, PICKS), FL), SD((8, D), FL), SD((SEQ_LEN, SLOTS * NB), BF),
         ],
         [],
-        [x, a_all, mixing, counted[:, None], keys, queries],
+        [x, a_all, segments[None, :], counted[:, None], keys, queries],
         "attend", flops=7 * 10**9, moved=20 * 10**6,
     )
     x1, h2, z, act, x2, features = run(
@@ -907,23 +1188,20 @@
         "attend_back", flops=12 * 10**9, moved=25 * 10**6,
         in_specs=[SM] + [VM] * 14,
     )
-    sums = [
-        lax.psum(lax.psum_scatter(item, "batch", scatter_dimension=0, tiled=True), "vocab").astype(FL)
-        for item in (dc, du, dp, da)
-    ]
-    extra = unembed(nb, nv, cap, width, rows, dx, ids, place)
+    extra, *sums = unembed(nb, nv, cap, width, rows, dx, ids, place, (da, dp, du, dc))
+    sums = [item.astype(FL) for item in sums]
 
     def more_grads(state):
         turn, total = state
         later = later_slots(nv, cap, rows, every, turn)
         return turn + 1, total + unembed(
             nb, nv, cap, width, rows, dx, later, place - jnp.array([0, 1, 0, 0, 0, 0, 0, 0], I32)[None, :, None] * (turn * cap)
-        )
+        )[0]
 
     extra = lax.while_loop(lambda state: state[0] < turns, more_grads, (jnp.int32(1), extra))[1]
 
     grad_table = dw_sum.astype(FL) + extra
-    grad_c, grad_u, grad_p, grad_a = sums
+    grad_a, grad_p, grad_u, grad_c = sums
     grad_norms = grad_a[:, 3 * D : 3 * D + 6].T
     grad_a = grad_a[:, : 3 * D]
     at_root = (lax.axis_index("vocab") == 0).astype(FL)

time: 994 us -> 700 us (0.70)
  waiting for transfers between devices: 419 us -> 0.06 us
  Pallas kernels: 386 us -> 544 us
  local copies, waits for them, and re-layouts: 33.9 us -> 17.9 us
    reduce_scatter x4 -> x0, waiting for transfers between devices: 171 us -> none  [shards(): lax.psum_scatter(item, 'batch', scatter_dimension=0, tiled=True)]
    pallas_call x7, Pallas kernels: 386 us -> 544 us  [run(): pl.pallas_call(kernel, out_shape=outs, in_specs=in_specs if in_specs is n...]
    all_gather x1, waiting for transfers between devices: 93.1 us -> 0.01 us  [shards(): words = lax.all_gather(table_t.astype(BF), 'batch', axis=0, tiled=True)]
    reduce_scatter x1, waiting for transfers between devices: 91.6 us -> 0.02 us  [shards(): dw_sum = lax.psum_scatter(dw, 'batch', scatter_dimension=0, tiled=True)]
    all_gather x4 -> x0, waiting for transfers between devices: 41.7 us -> none  [the longest x1 41.7 us: shards(): c_all = lax.all_gather(contract[0].astype(BF), 'batch', axis=0, tiled=True)]
    psum x1 -> x0, waiting for transfers between devices: 18.9 us -> none  [shards(): lax.psum(lax.psum_scatter(item, 'batch', scatter_dimension=0, tiled=True)...]
  transfers between devices with their start and end apart: 11 -> 2, of which waited for: 7 -> 0; matrix products, arithmetic and copies ran while one was open for 5% -> 4% of each run, Pallas kernels for 27% -> 63%
where the time goes in v2:
time: 700 us; the launch traced here: 694 us
  Pallas kernels  544 us (78%)
  other arithmetic  59.3 us (8%)
  blocking collectives  41.1 us (6%)
  between operations  22.9 us (3%)
  local copies, waits for them, and re-layouts  17.9 us (3%)
  loops' own time  9.19 us (1%)
    pallas_call x7, Pallas kernels, run(): pl.pallas_call(kernel, out_shape=outs, in_specs=in_specs if in_specs is n...  544 us
    psum x1, blocking collectives, shards(): lax.psum((jnp.sum(grad_table * grad_table) + at_root * owned, at_root * l...  41.1 us
    sub x6, other arithmetic, adamw(): weight - rate * (fixed_moment / (jnp.sqrt(fixed_square) + ADAM_EPS) + dec...  21.7 us
  transfers between devices with their start and end apart: 2, of which 0 were waited for; matrix products, arithmetic and copies ran while one was open for 4% of the time, Pallas kernels for 63%

profile of v2, /device:TPU:0, one launch (start us, length us, event | category | flops | bytes accessed | tf_op | source)
XLA Modules:
  0.0 694.2 jit_solution(5249958583268945001)
XLA Ops:
  7.2 4.1 bitcast_convert_fusion
  11.4 0.7 copy-done.24
  12.3 1.7 convert_bitcast_fusion.3
  14.0 1.1 concatenate.16.refs_3_
  15.2 2.0 convert_bitcast_fusion.4.refs_4_
  17.1 1.1 convert_bitcast_fusion.1.refs_6_
  18.3 1.2 convert_bitcast_fusion.2.refs_5_
  19.5 158.6 %embed.1 = (bf16[1024,768]{1,0:T(8,128)(2,1)S(1)}, s32[8,768,1]{2,1,0:T(8,128)}, s32[4,8,1024]{2,1,0:T(8,128)S(1)}, f32[8,128]{1,0:T(8,128)}, s32[4,8,1024]{2,1,...) custom-call(s32[1]{0:T(128)} %constant.63.clone.1.refs_0_, ...), custom_call_target="tpu_custom_call" | custom-call | tf_op jit(solution)/shard_map/embed/pallas_call | solution.py:68
  178.0 1.2 slice.42
  179.9 0.7 copy.177.pick_ref
  180.8 1.2 copy.178.key_ref
  182.0 0.6 broadcast_in_dim.83.live_ref
  182.7 1.0 copy.179.target_ref
  183.7 9.0 %while.23 = (s32[]{:T(128)}, bf16[1024,768]{1,0:T(8,128)(2,1)S(1)}, s32[]{:T(128)}, s32[8,1024]{1,0:T(8,128)S(1)}, f32[192,6400]{1,0:T(8,128)}, /*index=5*/s32[]{:T(128)}) while((s32[]{:T(128)}, bf16[1024,768]{1,0:T(8,128)(2,1)S(1)}, s32[]{:T(128)}, s32[8,1024]{1,0:T(8,128)S(1)}, f32[192,6400]{1,0:T(8,128)}, /*index=5*/s32[]{:T(128)}) %tuple.86), condition=%wide.region_1.2_spmd, body=%wide.region_0.1_spmd.sunk | while | flops 786434 | bytes 4718669 | solution.py:1145
  192.7 0.6 fusion.36
  193.3 2.6 fusion.24
  195.9 0.7 add_add_fusion.query_ref
  196.5 23.1 %attend.1 = (bf16[1536,768]{1,0:T(8,128)(2,1)}, bf16[1536,1536]{1,0:T(8,128)(2,1)}, bf16[128,768]{1,0:T(8,128)(2,1)}, bf16[128,768]{1,0:T(8,128)(2,1)}, f32[128,...) custom-call(bf16[1024,768]{1,0:T(8,128)(2,1)S(1)} %get-tuple-element, ...), custom_call_target="tpu_custom_call" | custom-call | flops 7000000000 | bytes 20000000 | tf_op jit(solution)/shard_map/attend/pallas_call | solution.py:68
  219.6 8.8 %feed.1 = (f32[128,768]{1,0:T(8,128)}, bf16[128,768]{1,0:T(8,128)(2,1)}, f32[128,3072]{1,0:T(8,128)}, bf16[128,3072]{1,0:T(8,128)(2,1)}, f32[128,768]{1,0:T(8,128)}, /*index=5*/bf16[128,768]{1,0:T(8,128)(2,1)}) custom-call(f32[128,768]{1,0:T(8,128)} %get-tuple-element.187.xq_ref, bf16[128,768]{1,0:T(8,128)(2,1)} %get-tuple-element.188.o_ref, ...), custom_call_target="tpu_custom_call" | custom-call | flops 2000000000 | bytes 15000000 | tf_op jit(solution)/shard_map/feed/pallas_call | solution.py:68
  228.4 108.1 %head.1 = (f32[128,768]{1,0:T(8,128)}, bf16[768,6400]{1,0:T(8,128)(2,1)}, f32[8,128]{1,0:T(8,128)}) custom-call(bf16[128,768]{1,0:T(8,128)(2,1)} %get-tuple-element.193.f_ref, bf16[768,6400]{1,0:T(8,128)(2,1)} %all-gather.2.cloned.1.call-done.w_ref, s32[1,6400]{1,0:T(1,128)} %broadcast_in_dim.83.live_ref, s32[1024,1]{1,0:T(8,128)} %copy.179.target_ref), custom_call_target="tpu_custom_call" | custom-call | tf_op jit(solution)/shard_map/head/pallas_call | solution.py:68
  336.6 0.8 copy.185
  337.3 0.8 copy.191
  339.1 0.8 copy.183
  339.9 0.8 copy.182
  340.7 1.2 slice.47
  341.9 15.9 %feed_back.1 = (bf16[3072,768]{1,0:T(8,128)(2,1)}, bf16[768,3072]{1,0:T(8,128)(2,1)}, bf16[768,768]{1,0:T(8,128)(2,1)}, f32[128,768]{1,0:T(8,128)}, bf16[128,768]{1,0:T(8,128)(2,1)}, /*index=5*/f32[8,768]{1,0:T(8,128)}) custom-call(f32[128,768]{1,0:T(8,128)} %get-tuple-element.196.df_ref, f32[128,768]{1,0:T(8,128)} %get-tuple-element.197.x2_ref, ...), custom_call_target="tpu_custom_call" | custom-call | flops 4000000000 | bytes 30000000 | tf_op jit(solution)/shard_map/feed_back/pallas_call | solution.py:68
  357.8 35.3 %attend_back.1 = (bf16[768,2560]{1,0:T(8,128)(2,1)}, bf16[1024,768]{1,0:T(8,128)(2,1)S(1)}) custom-call(s32[128]{0:T(128)} %pos_ref.1, bf16[128,768]{1,0:T(8,128)(2,1)} %get-tuple-element.202.do_ref, bf16[128,768]{1,0:T(8,128)(2,1)} %get-tuple-element.203.q_ref, bf16[1536,1536]{1,0:T(8,128)(2,1)} %get-tuple-element.204.kv_ref, ...), custom_call_target="tpu_custom_call" | custom-call | flops 12000000000 | bytes 25000000 | tf_op jit(solution)/shard_map/attend_back/pallas_call | solution.py:68
  393.1 194.0 %unembed.1 = (f32[192,6400]{1,0:T(8,128)}, bf16[192,2560]{1,0:T(8,128)(2,1)}, bf16[192,768]{1,0:T(8,128)(2,1)}, bf16[192,3072]{1,0:T(8,128)(2,1)}, bf16[768,768]{1,0:T(8,128)(2,1)}) custom-call(bf16[1024,768]{1,0:T(8,128)(2,1)S(1)} %get-tuple-element.518.refs_0_, s32[8,768,1]{2,1,0:T(8,128)} %get-tuple-element.212.refs_1_, ...), custom_call_target="tpu_custom_call" | custom-call | tf_op jit(solution)/shard_map/unembed/pallas_call | solution.py:68
  587.1 1.5 convert_element_type.62
  588.6 0.8 fusion.19
  589.9 1.1 multiply_reduce_fusion.1
  592.2 2.5 fusion.8
  595.4 1.2 fusion.9
  597.2 1.5 multiply_reduce_fusion.2
  600.4 5.2 multiply_reduce_fusion
  606.3 41.1 %all-reduce = (f32[]{:T(128)}, f32[]{:T(128)}) all-reduce(f32[]{:T(128)S(6)} %mul.336, f32[]{:T(128)S(6)} %add.169), channel_id=1, replica_groups=mesh['batch'=4,'vocab'=8] {'batch','vocab'}, use_global_device_ids=true, to_apply=%region_2.3 | all-reduce | flops 2 | bytes 16 | tf_op jit(solution)/shard_map/psum | solution.py:1209
  648.6 0.7 copy.193
  649.2 0.7 copy.194
  649.9 0.7 copy.195
  650.8 0.7 copy.196
  651.5 0.7 copy.197
  652.2 0.7 copy.198
  652.9 5.9 multiply_subtract_fusion.2
  658.8 1.5 multiply_subtract_fusion.3
  660.3 0.8 copy-done.5
  661.1 6.9 %multiply_subtract_fusion.1 = (f32[1,192,3072]{2,1,0:T(8,128)}, f32[1,192,3072]{2,1,0:T(8,128)}, f32[1,192,3072]{2,1,0:T(8,128)}) fusion(f32[1,192,3072]{2,1,0:T(8,128)S(1)} %copy-done.5, f32[]{:T(128)} %bitcast.23, f32[]{:T(128)} %bitcast.21, f32[]{:T(128)S(6)} %min.3, bf16[192,3072]{1,0:T(8,128)(2,1)S(1)} %copy-done.10, f32[1,192,3072]{2,1,0:T(8,128)} %param.49, ...), kind=kLoop, calls=%fused_computation.36 | loop fusion | flops 10027008 | bytes 15335436 | tf_op jit(solution)/shard_map/sub | solution.py:1098
  668.1 7.4 %multiply_subtract_fusion = (f32[1,768,768]{2,1,0:T(8,128)}, f32[1,768,768]{2,1,0:T(8,128)}, f32[1,768,768]{2,1,0:T(8,128)}) fusion(f32[1,768,768]{2,1,0:T(8,128)S(1)} %copy-done.7, f32[]{:T(128)} %bitcast.23, f32[]{:T(128)} %bitcast.21, f32[]{:T(128)S(6)} %min.3, bf16[768,768]{1,0:T(8,128)(2,1)S(1)} %copy-done.9, f32[1,768,768]{2,1,0:T(8,128)} %param.52, ...), kind=kLoop, calls=%fused_computation.35 | loop fusion | flops 10027008 | bytes 15335436 | tf_op jit(solution)/shard_map/sub | solution.py:1098
  675.6 10.3 %fusion.26 = (f32[6400,192]{0,1:T(8,128)}, f32[6400,192]{0,1:T(8,128)}, f32[6400,192]{0,1:T(8,128)}) fusion(f32[]{:T(128)S(6)} %min.3, f32[192,6400]{1,0:T(8,128)S(1)} %bitcast.111, bf16[192,6400]{1,0:T(8,128)(2,1)S(1)} %copy-done.3, f32[6400,192]{0,1:T(8,128)S(1)} %bitcast.113, f32[]{:T(128)} %bitcast.23, f32[]{:T(128)} %bitcast.21, f32[6400,192]{0,1:T(8,128)} %param.39, ...), kind=kLoop, calls=%fused_computation.91 | loop fusion | flops 22118400 | bytes 36864012 | tf_op jit(solution)/shard_map/transpose | solution.py:1219
  (120 shorter events, 2.3 us)
Async XLA Ops:
  7.2 221.2 %all-gather.2.cloned.1.call-start = ((), (), s32[]{:S(2)}) async-start(), calls=%async_computation.1 | async-start | bytes 12288000 | tf_op jit(solution)/shard_map/all_gather | solution.py:1124
  11.3 0.8 copy-start.24
  11.3 0.8 copy-start.22
  11.3 0.8 copy-start.20
  11.3 589.0 %reduce-scatter.2.cloned.1.call-start = ((), (), s32[]{:S(2)}) async-start(), calls=%async_computation.2 | async-start | bytes 12288000 | tf_op jit(solution)/shard_map/reduce_scatter | solution.py:1169
  12.3 4.8 copy-start.6
  15.2 3.1 copy-start.4
  19.4 160.5 %copy-start.28 = (s32[128]{0:T(128)S(1)}, s32[128]{0:T(128)}, u32[]{:S(2)}) copy-start(s32[128]{0:T(128)} %pos_ref.1) | copy-start | bytes 1540
  19.4 161.3 %copy-start.26 = (s32[1024]{0:T(1024)S(1)}, s32[1024]{0:T(1024)}, u32[]{:S(2)}) copy-start(s32[1024]{0:T(1024)} %param.34) | copy-start | bytes 12292
  19.4 161.3 %copy-start.27 = (s32[1536,1]{0,1:T(1,128)S(1)}, s32[1536,1]{0,1:T(1,128)}, u32[]{:S(2)}) copy-start(s32[1536,1]{0,1:T(1,128)} %constant.73.clone.1) | copy-start | bytes 18436
  19.4 162.6 %copy-start.25 = (s32[6400]{0:T(1024)S(1)}, s32[6400]{0:T(1024)}, u32[]{:S(2)}) copy-start(s32[6400]{0:T(1024)} %param.36) | copy-start | bytes 76804
  19.4 163.2 %copy-start.29 = (s32[1024]{0:T(1024)S(1)}, s32[1024]{0:T(1024)}, u32[]{:S(2)}) copy-start(s32[1024]{0:T(1024)} %param.33) | copy-start | bytes 12292
  192.7 27.0 %copy-start = (bf16[1024,768]{1,0:T(8,128)(2,1)}, bf16[1024,768]{1,0:T(8,128)(2,1)S(1)}, u32[]{:S(2)}) copy-start(bf16[1024,768]{1,0:T(8,128)(2,1)S(1)} %get-tuple-element.185.x_ref) | copy-start | bytes 4718596
  336.5 2.3 copy-start.30
  336.5 2.5 copy-start.31
  336.5 2.6 copy-start.32
  336.5 3.4 copy-start.33
  587.1 1.5 copy-start.12
  588.6 1.3 copy-start.1
  588.6 6.8 copy-start.8
  588.6 11.4 %copy-start.34 = (s32[8]{0:T(128)S(1)}, s32[8]{0:T(128)}, u32[]{:S(2)}) copy-start(s32[8]{0:T(128)} %constant.160.clone..sunk.2) | copy-start | bytes 100
  600.3 5.9 copy-start.2
  600.3 47.8 %copy-start.16 = (f32[3,192]{0,1:T(8,128)S(1)}, f32[3,192]{0,1:T(8,128)}, u32[]{:S(2)}) copy-start(f32[3,192]{0,1:T(8,128)} %copy.183) | copy-start | bytes 6916
  600.4 47.8 %copy-start.17 = (f32[3,192]{0,1:T(8,128)S(1)}, f32[3,192]{0,1:T(8,128)}, u32[]{:S(2)}) copy-start(f32[3,192]{0,1:T(8,128)} %copy.182) | copy-start | bytes 6916
  600.4 48.0 %copy-start.21 = (f32[3,192]{1,0:T(4,128)S(1)}, f32[3,192]{1,0:T(4,128)}, u32[]{:S(2)}) copy-start(f32[3,192]{1,0:T(4,128)} %param.53) | copy-start | bytes 6916
  600.4 48.2 %copy-start.19 = (f32[3,192]{0,1:T(8,128)S(1)}, f32[3,192]{0,1:T(8,128)}, u32[]{:S(2)}) copy-start(f32[3,192]{0,1:T(8,128)} %copy.185) | copy-start | bytes 6916
  600.4 50.3 %copy-start.23 = (f32[3,192]{1,0:T(4,128)S(1)}, f32[3,192]{1,0:T(4,128)}, u32[]{:S(2)}) copy-start(f32[3,192]{1,0:T(4,128)} %param.56) | copy-start | bytes 6916
  605.6 45.2 %copy-start.18 = (f32[3,192]{0,1:T(8,128)S(1)}, f32[3,192]{0,1:T(8,128)}, u32[]{:S(2)}) copy-start(f32[3,192]{0,1:T(8,128)} %copy.191) | copy-start | bytes 6916
  652.8 5.9 copy-start.11
  652.9 5.9 copy-start.13
  652.9 6.0 copy-start.14
  652.9 6.0 copy-start.15
  652.9 7.5 %copy-start.10 = (bf16[192,3072]{1,0:T(8,128)(2,1)S(1)}, bf16[192,3072]{1,0:T(8,128)(2,1)}, u32[]{:S(2)}) copy-start(bf16[192,3072]{1,0:T(8,128)(2,1)} %get-tuple-element.223) | copy-start | bytes 3538948
  658.8 2.3 copy-start.5
  658.8 9.3 %copy-start.9 = (bf16[768,768]{1,0:T(8,128)(2,1)S(1)}, bf16[768,768]{1,0:T(8,128)(2,1)}, u32[]{:S(2)}) copy-start(bf16[768,768]{1,0:T(8,128)(2,1)} %get-tuple-element.224) | copy-start | bytes 3538948
  661.1 7.0 %copy-start.7 = (f32[1,768,768]{2,1,0:T(8,128)S(1)}, f32[1,768,768]{2,1,0:T(8,128)}, u32[]{:S(2)}) copy-start(f32[1,768,768]{2,1,0:T(8,128)} %param.50) | copy-start | bytes 7077892
  661.1 14.4 %slice-start = ((s8[4915200]{0:T(1024)(128)(4,1)}), s8[4194304]{0:T(1024)(128)(4,1)S(1)}, s32[]{:S(2)}) async-start(s8[4915200]{0:T(1024)(128)(4,1)} %bitcast.107), calls=%async_computation.3 | async-start | bytes 8388608
  661.1 14.4 %slice-start.2 = ((s8[4915200]{0:T(1024)(128)(4,1)}), s8[4194304]{0:T(1024)(128)(4,1)S(1)}, s32[]{:S(2)}) async-start(s8[4915200]{0:T(1024)(128)(4,1)} %bitcast.110), calls=%async_computation.5 | async-start | bytes 8388608
  661.1 14.4 %slice-start.4 = ((s8[4915200]{0:T(1024)(128)(4,1)}), s8[4194304]{0:T(1024)(128)(4,1)S(1)}, s32[]{:S(2)}) async-start(s8[4915200]{0:T(1024)(128)(4,1)} %bitcast.112), calls=%async_computation.7 | async-start | bytes 8388608
  668.1 7.4 %slice-start.1 = ((s8[4915200]{0:T(1024)(128)(4,1)}), s8[720896]{0:T(1024)(128)(4,1)S(1)}, s32[]{:S(2)}) async-start(s8[4915200]{0:T(1024)(128)(4,1)} %bitcast.107), calls=%async_computation.4 | async-start | bytes 1441792
  668.1 7.4 %slice-start.3 = ((s8[4915200]{0:T(1024)(128)(4,1)}), s8[720896]{0:T(1024)(128)(4,1)S(1)}, s32[]{:S(2)}) async-start(s8[4915200]{0:T(1024)(128)(4,1)} %bitcast.110), calls=%async_computation.6 | async-start | bytes 1441792
  668.1 7.4 %copy-start.3 = (bf16[192,6400]{1,0:T(8,128)(2,1)S(1)}, bf16[192,6400]{1,0:T(8,128)(2,1)}, u32[]{:S(2)}) copy-start(bf16[192,6400]{1,0:T(8,128)(2,1)} %reduce-scatter.2.cloned.1.call-done) | copy-start | bytes 7372804
  668.1 7.4 %slice-start.5 = ((s8[4915200]{0:T(1024)(128)(4,1)}), s8[720896]{0:T(1024)(128)(4,1)S(1)}, s32[]{:S(2)}) async-start(s8[4915200]{0:T(1024)(128)(4,1)} %bitcast.112), calls=%async_computation.8 | async-start | bytes 1441792
Sparse Core Ops, SparseCore 0:
  11.5 171.3 all-gather.1
  336.7 130.8 reduce-scatter.1

commit v3 on v2

--- a/solution.py
+++ b/solution.py
@@ -653,8 +653,23 @@
     return jnp.where(keep, value, jnp.zeros_like(value))
 
 
-def visible_keys(key_ref, query_ref):
-    return (key_ref[:, 0:1] == query_ref[0:1, :]) & (key_ref[:, 1:2] <= query_ref[1:2, :])
+def visible_keys(seg_ref, pos_ref):
+    position = pos_ref[...]
+    block = position // BLK
+    marks = [seg_ref[:, i * BLK : i * BLK + 1] for i in range(SEQ_LEN // BLK)]
+    segment = jnp.zeros_like(position)
+    for i, mark in enumerate(marks):
+        segment = jnp.where(block == i, mark, segment)
+    row = iota((BLK, PICKS), 0)
+    parts = [jnp.broadcast_to(segment == slot + 1, (NB, PICKS)) for slot in range(SLOTS)]
+    parts += [(segment == mark) & (row + i * BLK <= position) for i, mark in enumerate(marks)]
+    return parts
+
+
+def masked(visible, scores):
+    return jnp.concatenate(
+        [jnp.where(keep, scores[i * BLK : (i + 1) * BLK, :], NEG_BIG) for i, keep in enumerate(visible)], axis=0
+    )
 
 
 def memory_weights(segments, slot):
@@ -671,7 +686,7 @@
 
 
 def attend_kernel(
-    x_ref, a_ref, seg_ref, pick_ref, key_ref, query_ref,
+    x_ref, a_ref, seg_ref, pos_ref,
     hall_ref, kv_ref, q_ref, hq_ref, xq_ref, o_ref, lse_ref, norm_ref, mixt_ref,
 ):
     norm_ref[...] = a_ref[:, 3 * D : 3 * D + 128].astype(FL).T[:8, :]
@@ -692,11 +707,11 @@
         kv_ref[pl.ds(i * BLK, BLK), :] = nn(hall_ref[pl.ds(i * BLK, BLK), :], a_ref[:, D : 3 * D]).astype(BF)
 
     each(0, KEYS // BLK, project)
-    pick = (pick_ref[...] == iota((PICKS, SEQ_LEN), 1)).astype(FL).astype(BF)
+    pick = (pos_ref[...] == iota((SEQ_LEN, PICKS), 0)).astype(FL).astype(BF).T
     hq_ref[...] = nn(pick, normed).astype(BF)
     xq_ref[...] = nn(pick, x_ref[...])
     q_ref[...] = nn(hq_ref[...], a_ref[:, :D]).astype(BF)
-    visible = visible_keys(key_ref, query_ref)
+    visible = visible_keys(seg_ref, pos_ref)
 
     def attend(p):
         keys = kv_ref[:, lanes(p * PAIR, PAIR)]
@@ -704,7 +719,7 @@
         queries = q_ref[:, lanes(p * PAIR, PAIR)] * HD ** (-0.5)
         outs = []
         for head in range(2):
-            scores = jnp.where(visible, nt(keys, head_lanes(queries, head)), NEG_BIG)
+            scores = masked(visible, nt(keys, head_lanes(queries, head)))
             peak = jnp.max(scores, axis=0, keepdims=True)
             expo = jnp.exp(scores - peak)
             total = jnp.sum(expo, axis=0, keepdims=True)
@@ -772,10 +787,10 @@
 
 
 def attend_back_kernel(
-    pos_ref, do_ref, q_ref, kv_ref, lse_ref, hall_ref, hq_ref, a_ref, x_ref, dx1_ref, mixt_ref, key_ref, query_ref,
+    pos_ref, do_ref, q_ref, kv_ref, lse_ref, hall_ref, hq_ref, a_ref, x_ref, dx1_ref, mixt_ref, seg_ref, row_ref,
     norm_ref, dnorm_ref, da_ref, dx_ref, dkv, dq, hallt, dh, dxin, dmem,
 ):
-    visible = visible_keys(key_ref, query_ref)
+    visible = visible_keys(seg_ref, row_ref)
 
     def attend(p):
         cut = lanes(p * PAIR, PAIR)
@@ -788,7 +803,7 @@
         dk = dv = None
         for head in range(2):
             own, grad = head_lanes(queries, head), head_lanes(grads, head)
-            scores = jnp.where(visible, nt(keys, own), NEG_BIG)
+            scores = masked(visible, nt(keys, own))
             probs = jnp.exp(scores - lse_ref[p, head : head + 1, :])
             dprobs = nt(values, grad)
             inner = jnp.sum(probs * dprobs, axis=0, keepdims=True)
@@ -1089,6 +1104,63 @@
     )
 
 
+def norm_kernel(
+    nb, nv, extra_ref, dw_ref, a_ref, p_ref, u_ref, c_ref, loss_ref, out_ref,
+    mine, near, lines, vocab_out, vocab_in, batch_out, batch_in,
+):
+    b, v = lax.axis_index("batch"), lax.axis_index("vocab")
+    meet((("batch", nb), ("vocab", nv)))
+
+    def squares(refs, part):
+        cols = refs[0].shape[1]
+
+        def add(j, total):
+            value = refs[0][:, lanes(j * part, part)].astype(FL)
+            for ref in refs[1:]:
+                value = value + ref[:, lanes(j * part, part)].astype(FL)
+            return total + jnp.sum(value * value, axis=0, keepdims=True)
+
+        line = lax.fori_loop(0, cols // part, add, jnp.zeros((1, part), FL))
+        return jnp.sum(line, axis=1, keepdims=True)
+
+    own = squares((extra_ref, dw_ref), chunk_of(dw_ref.shape[1], 640))
+    layer = squares((a_ref,), 512) + squares((p_ref,), 384) + squares((u_ref,), 512) + squares((c_ref,), 384)
+    own = own + jnp.where(v == 0, layer, jnp.zeros_like(layer))
+    line = iota((8, 128), 0)
+    mine[...] = jnp.where(line == 0, own, jnp.where((line == 1) & (v == 0), loss_ref[...], 0.0))
+
+    def vocab_copy(step):
+        return send(mine, near.at[v], vocab_out.at[step], vocab_in.at[step], {"vocab": lax.rem(v + step, nv)})
+
+    each(1, nv, lambda step: vocab_copy(step).start())
+    near[v] = mine[...]
+    each(1, nv, lambda step: vocab_copy(step).wait())
+    mine[...] = lax.fori_loop(0, nv, lambda u, total: total + near[u], jnp.zeros((8, 128), FL))
+
+    def batch_copy(step):
+        return send(mine, lines.at[b], batch_out.at[step], batch_in.at[step], {"batch": lax.rem(b + step, nb)})
+
+    each(1, nb, lambda step: batch_copy(step).start())
+    lines[b] = mine[...]
+    each(1, nb, lambda step: batch_copy(step).wait())
+    out_ref[...] = lax.fori_loop(0, nb, lambda u, total: total + lines[u], jnp.zeros((8, 128), FL))
+
+
+def norm(nb, nv, extra, dw, sums, loss):
+    dma = pltpu.SemaphoreType.DMA
+    return run(
+        functools.partial(norm_kernel, nb, nv),
+        [SD((8, 128), FL)],
+        [
+            pltpu.VMEM((8, 128), FL), pltpu.VMEM((nv, 8, 128), FL), pltpu.VMEM((nb, 8, 128), FL),
+            dma((nv,)), dma((nv,)), dma((nb,)), dma((nb,)),
+        ],
+        [extra, dw, *sums, loss],
+        "norm",
+        5,
+    )[0]
+
+
 def adamw(weight, moment, square, gradient, clip, count, decay, rate):
     gradient = gradient * clip
     moment = BETA_ONE * moment + (1 - BETA_ONE) * gradient
@@ -1123,15 +1195,7 @@
     pieces = (packed, project[0].astype(BF), expand[0].astype(BF), contract[0].astype(BF))
     words = lax.all_gather(table_t.astype(BF), "batch", axis=0, tiled=True)
 
-    key_seg = jnp.concatenate([jnp.repeat(jnp.arange(SLOTS, dtype=I32) + 1, NB), segments])
-    key_pos = jnp.concatenate([jnp.full((SLOTS * NB,), -1, I32), jnp.arange(SEQ_LEN, dtype=I32)])
-    keys = jnp.stack([key_seg, key_pos], axis=1)
-    query_blk = counted // BLK
-    query_seg = functools.reduce(
-        lambda seg, i: jnp.where(query_blk == i, segments[i * BLK], seg), range(1, SEQ_LEN // BLK), jnp.broadcast_to(segments[0], counted.shape)
-    )
-    queries = jnp.concatenate([query_seg[None], counted[None], jnp.zeros((6, PICKS), I32)], axis=0)
-
+    seg_row, pos_row = segments[None, :], counted[None, :]
     tok = tokens.reshape(nv, SEQ_LEN)
     x, ids, place, most, every, a_all, p_all, u_all, c_all = embed(
         nb, nv, cap, jnp.zeros((1,), I32), tok, table_t, pieces
@@ -1142,7 +1206,12 @@
         turn, total = state
         return turn + 1, total + embed(nb, nv, cap, turn[None], tok, table_t)[0]
 
-    x = lax.while_loop(lambda state: state[0] < turns, more_rows, (jnp.int32(1), x))[1]
+    x = lax.cond(
+        turns > 1,
+        lambda x: lax.while_loop(lambda state: state[0] < turns, more_rows, (jnp.int32(1), x))[1],
+        lambda x: x,
+        x,
+    )
 
     hall, kv, q, hq, xq, mixed, lse, norm_rows, mixing_t = run(
         attend_kernel,
@@ -1151,7 +1220,7 @@
             SD((PICKS, D), BF), SD((NPAIR, 2, PICKS), FL), SD((8, D), FL), SD((SEQ_LEN, SLOTS * NB), BF),
         ],
         [],
-        [x, a_all, segments[None, :], counted[:, None], keys, queries],
+        [x, a_all, seg_row, pos_row],
         "attend", flops=7 * 10**9, moved=20 * 10**6,
     )
     x1, h2, z, act, x2, features = run(
@@ -1165,7 +1234,6 @@
         "feed", flops=2 * 10**9, moved=15 * 10**6,
     )
     df, dw, loss_block = head(nb, nv, features, words, vocab_mask[None, :], targets[:, None])
-    loss_part = loss_block[0, 0]
     dw_sum = lax.psum_scatter(dw, "batch", scatter_dimension=0, tiled=True)
 
     dc, du, dp, dx1, dmixed, dnorm = run(
@@ -1184,12 +1252,11 @@
             pltpu.VMEM((KEYS, 2 * D), BF), pltpu.VMEM((PICKS, D), BF), pltpu.VMEM((D, KEYS), BF),
             pltpu.VMEM((SEQ_LEN, D), FL), pltpu.VMEM((SEQ_LEN, D), FL), pltpu.VMEM((SLOTS * NB, D), BF),
         ],
-        [counted, dmixed, q, kv, lse, hall, hq, a_all, x, dx1, mixing_t, keys, queries, norm_rows, dnorm],
+        [counted, dmixed, q, kv, lse, hall, hq, a_all, x, dx1, mixing_t, seg_row, pos_row, norm_rows, dnorm],
         "attend_back", flops=12 * 10**9, moved=25 * 10**6,
         in_specs=[SM] + [VM] * 14,
     )
     extra, *sums = unembed(nb, nv, cap, width, rows, dx, ids, place, (da, dp, du, dc))
-    sums = [item.astype(FL) for item in sums]
 
     def more_grads(state):
         turn, total = state
@@ -1198,17 +1265,19 @@
             nb, nv, cap, width, rows, dx, later, place - jnp.array([0, 1, 0, 0, 0, 0, 0, 0], I32)[None, :, None] * (turn * cap)
         )[0]
 
-    extra = lax.while_loop(lambda state: state[0] < turns, more_grads, (jnp.int32(1), extra))[1]
-
+    extra = lax.cond(
+        turns > 1,
+        lambda extra: lax.while_loop(lambda state: state[0] < turns, more_grads, (jnp.int32(1), extra))[1],
+        lambda extra: extra,
+        extra,
+    )
+
+    totals = norm(nb, nv, extra, dw_sum, sums, loss_block)
     grad_table = dw_sum.astype(FL) + extra
-    grad_a, grad_p, grad_u, grad_c = sums
+    grad_a, grad_p, grad_u, grad_c = (item.astype(FL) for item in sums)
     grad_norms = grad_a[:, 3 * D : 3 * D + 6].T
     grad_a = grad_a[:, : 3 * D]
-    at_root = (lax.axis_index("vocab") == 0).astype(FL)
-    owned = sum(jnp.sum(item * item) for item in (grad_a, grad_p, grad_u, grad_c, grad_norms))
-    squares, loss = lax.psum(
-        (jnp.sum(grad_table * grad_table) + at_root * owned, at_root * loss_part), ("batch", "vocab")
-    )
+    squares, loss = totals[0, 0], totals[1, 0]
     gradient_norm = jnp.sqrt(squares)
     clip = jnp.minimum(1.0, MAX_NORM / (gradient_norm + 1e-06))
     count = step_count[0].astype(FL)

time: 700 us -> 662 us (0.946)
  blocking collectives: 41.1 us -> 0 us
  Pallas kernels: 544 us -> 562 us
  other arithmetic: 59.3 us -> 41.9 us
  loops' own time: 9.19 us -> 16.4 us
    psum x1 -> x0, blocking collectives: 41.1 us -> none  [shards(): lax.psum((jnp.sum(grad_table * grad_table) + at_root * owned, at_root * l...]
    pallas_call x7 -> x8, Pallas kernels: 544 us -> 562 us  [run(): pl.pallas_call(kernel, out_shape=outs, in_specs=in_specs if in_specs is n...]
    reduce_sum x6 -> x0, other arithmetic: 12.2 us -> none  [the longest x5 7.02 us: shards(): jnp.sum(item * item)]
    another operation x2, loops' own time: 9.19 us -> 16.4 us  [the longest x1 8.87 us: shards(): lax.cond(turns > 1, lambda x: lax.while_loop(lambda state: state[0] < tur...]
  transfers between devices with their start and end apart: 2 -> 2, of which waited for: 0 -> 0; matrix products, arithmetic and copies ran while one was open for 4% -> 2% of each run, Pallas kernels for 63% -> 67%
where the time goes in v3:
time: 662 us; the launch traced here: 656 us
  Pallas kernels  562 us (85%)
  other arithmetic  41.9 us (6%)
  between operations  18.3 us (3%)
  local copies, waits for them, and re-layouts  17.1 us (3%)
  loops' own time  16.4 us (2%)
    pallas_call x8, Pallas kernels, run(): pl.pallas_call(kernel, out_shape=outs, in_specs=in_specs if in_specs is n...  562 us
    sub x6, other arithmetic, adamw(): weight - rate * (fixed_moment / (jnp.sqrt(fixed_square) + ADAM_EPS) + dec...  19.9 us
  transfers between devices with their start and end apart: 2, of which 0 were waited for; matrix products, arithmetic and copies ran while one was open for 2% of the time, Pallas kernels for 67%

profile of v3, /device:TPU:0, one launch (start us, length us, event | category | flops | bytes accessed | tf_op | source)
XLA Modules:
  0.0 656.4 jit_solution(16032342046876062734)
XLA Ops:
  7.2 4.1 bitcast_convert_fusion
  11.4 0.7 copy-done.23
  12.1 0.1 copy.169
  12.3 1.7 convert_bitcast_fusion.3
  14.0 1.1 concatenate.9.refs_3_
  15.2 2.0 convert_bitcast_fusion.4.refs_4_
  17.1 1.1 convert_bitcast_fusion.1.refs_6_
  18.3 1.2 convert_bitcast_fusion.2.refs_5_
  19.4 158.4 %embed.1 = (bf16[1024,768]{1,0:T(8,128)(2,1)S(1)}, s32[8,768,1]{2,1,0:T(8,128)}, s32[4,8,1024]{2,1,0:T(8,128)S(1)}, f32[8,128]{1,0:T(8,128)}, s32[4,8,1024]{2,1,...) custom-call(s32[1]{0:T(128)} %constant.47.clone.1.refs_0_, ...), custom_call_target="tpu_custom_call" | custom-call | tf_op jit(solution)/shard_map/embed/pallas_call | solution.py:68
  177.9 1.2 slice.33
  179.7 1.0 copy.170.target_ref
  180.8 0.6 broadcast_in_dim.49.live_ref
  181.4 8.9 %conditional.2 = (bf16[1024,768]{1,0:T(8,128)(2,1)S(1)}) conditional(s32[]{:T(128)} %convert_element_type.63, bf16[1024,768]{1,0:T(8,128)(2,1)S(1)} %get-tuple-element.222, (s32[]{:T(128)}, s32[8,1024]{1,0:T(8,128)S(1)}, f32[192,6400]{1,0:T(8,128)}, bf16[1024,768]{1,0:T(8,128)(2,1)S(1)}) %tuple.103), branch_computations={%region_0.1_spmd, %region_1.4_spmd} | conditional | flops 786434 | bytes 4718725 | solution.py:1209
  190.3 23.5 %attend.1 = (bf16[1536,768]{1,0:T(8,128)(2,1)}, bf16[1536,1536]{1,0:T(8,128)(2,1)}, bf16[128,768]{1,0:T(8,128)(2,1)}, bf16[128,768]{1,0:T(8,128)(2,1)}, f32[128,...) custom-call(bf16[1024,768]{1,0:T(8,128)(2,1)S(1)} %get-tuple-element, ...), custom_call_target="tpu_custom_call" | custom-call | flops 7000000000 | bytes 20000000 | tf_op jit(solution)/shard_map/attend/pallas_call | solution.py:68
  213.8 8.8 %feed.1 = (f32[128,768]{1,0:T(8,128)}, bf16[128,768]{1,0:T(8,128)(2,1)}, f32[128,3072]{1,0:T(8,128)}, bf16[128,3072]{1,0:T(8,128)(2,1)}, f32[128,768]{1,0:T(8,128)}, /*index=5*/bf16[128,768]{1,0:T(8,128)(2,1)}) custom-call(f32[128,768]{1,0:T(8,128)} %get-tuple-element.224.xq_ref, bf16[128,768]{1,0:T(8,128)(2,1)} %get-tuple-element.225.o_ref, ...), custom_call_target="tpu_custom_call" | custom-call | flops 2000000000 | bytes 15000000 | tf_op jit(solution)/shard_map/feed/pallas_call | solution.py:68
  222.6 108.1 %head.1 = (f32[128,768]{1,0:T(8,128)}, bf16[768,6400]{1,0:T(8,128)(2,1)}, f32[8,128]{1,0:T(8,128)}) custom-call(bf16[128,768]{1,0:T(8,128)(2,1)} %get-tuple-element.230.f_ref, bf16[768,6400]{1,0:T(8,128)(2,1)} %all-gather.2.cloned.1.call-done.w_ref, s32[1,6400]{1,0:T(1,128)} %broadcast_in_dim.49.live_ref, s32[1024,1]{1,0:T(8,128)} %copy.170.target_ref), custom_call_target="tpu_custom_call" | custom-call | tf_op jit(solution)/shard_map/head/pallas_call | solution.py:68
  330.7 0.8 copy.181
  331.5 0.8 copy.175
  333.0 0.1 copy.172
  333.2 0.1 copy.173
  333.3 0.8 copy.178
  334.1 0.8 copy.179
  334.9 15.3 %feed_back.1 = (bf16[3072,768]{1,0:T(8,128)(2,1)}, bf16[768,3072]{1,0:T(8,128)(2,1)}, bf16[768,768]{1,0:T(8,128)(2,1)}, f32[128,768]{1,0:T(8,128)}, bf16[128,768]{1,0:T(8,128)(2,1)}, /*index=5*/f32[8,768]{1,0:T(8,128)}) custom-call(f32[128,768]{1,0:T(8,128)} %get-tuple-element.231.df_ref, f32[128,768]{1,0:T(8,128)} %get-tuple-element.232.x2_ref, ...), custom_call_target="tpu_custom_call" | custom-call | flops 4000000000 | bytes 30000000 | tf_op jit(solution)/shard_map/feed_back/pallas_call | solution.py:68
  350.2 34.5 %attend_back.1 = (bf16[768,2560]{1,0:T(8,128)(2,1)}, bf16[1024,768]{1,0:T(8,128)(2,1)S(1)}) custom-call(s32[128]{0:T(128)} %pos_ref.1, bf16[128,768]{1,0:T(8,128)(2,1)} %get-tuple-element.237.do_ref, bf16[128,768]{1,0:T(8,128)(2,1)} %get-tuple-element.238.q_ref, bf16[1536,1536]{1,0:T(8,128)(2,1)} %get-tuple-element.239.kv_ref, ...), custom_call_target="tpu_custom_call" | custom-call | flops 12000000000 | bytes 25000000 | tf_op jit(solution)/shard_map/attend_back/pallas_call | solution.py:68
  384.7 196.8 %unembed.1 = (f32[192,6400]{1,0:T(8,128)}, bf16[192,2560]{1,0:T(8,128)(2,1)}, bf16[192,768]{1,0:T(8,128)(2,1)}, bf16[192,3072]{1,0:T(8,128)(2,1)}, bf16[768,768]{1,0:T(8,128)(2,1)}) custom-call(bf16[1024,768]{1,0:T(8,128)(2,1)S(1)} %get-tuple-element.272.refs_0_, s32[8,768,1]{2,1,0:T(8,128)} %get-tuple-element.247.refs_1_, ...), custom_call_target="tpu_custom_call" | custom-call | tf_op jit(solution)/shard_map/unembed/pallas_call | solution.py:68
  581.5 7.5 %conditional.3 = (f32[192,6400]{1,0:T(8,128)}) conditional(s32[]{:T(128)} %convert_element_type.63, f32[192,6400]{1,0:T(8,128)} %get-tuple-element.273, (s32[]{:T(128)}, s32[4,8,1024]{2,1,0:T(8,128)S(1)}, s32[4,8,1024]{2,1,0:T(8,128)S(1)}, bf16[1024,768]{1,0:T(8,128)(2,1)S(1)}, f32[192,6400]{1,0:T(8,128)}) %tuple.41), branch_computations={%region_4.5_spmd, %region_5.11_spmd.clone} | conditional | flops 30846956 | bytes 16905888 | solution.py:1268
  589.0 1.4 convert_element_type.67
  590.5 1.3 copy-done.6
  591.8 17.1 %norm.1 = f32[8,128]{1,0:T(8,128)} custom-call(f32[192,6400]{1,0:T(8,128)} %get-tuple-element.595.extra_ref, bf16[192,6400]{1,0:T(8,128)(2,1)} %reduce-scatter.2.cloned.1.call-done.dw_ref, bf16[192,2560]{1,0:T(8,128)(2,1)} %get-tuple-element.256.a_ref, bf16[192,768]{1,0:T(8,128)(2,1)} %get-tuple-element.257.p_ref, ...), custom_call_target="tpu_custom_call" | custom-call | tf_op jit(solution)/shard_map/norm/pallas_call | solution.py:68
  608.9 1.3 fusion.20
  611.0 0.2 multiply_divide_fusion
  611.2 0.1 copy.180
  611.3 0.1 copy.182
  611.4 0.9 sub.119
  612.3 0.7 copy.186
  613.1 0.1 copy.176
  613.3 0.7 copy.183
  613.9 0.7 copy.184
  614.6 0.7 copy.185
  615.3 0.7 copy.187
  616.0 0.7 copy.188
  616.7 7.0 %multiply_subtract_fusion = (f32[1,768,768]{2,1,0:T(8,128)}, f32[1,768,768]{2,1,0:T(8,128)}, f32[1,768,768]{2,1,0:T(8,128)}) fusion(f32[1,768,768]{2,1,0:T(8,128)S(1)} %copy-done.3, f32[]{:T(128)} %bitcast.17, f32[]{:T(128)} %bitcast.15, f32[]{:T(128)S(6)} %min.3, bf16[768,768]{1,0:T(8,128)(2,1)} %get-tuple-element.259.c_ref, f32[1,768,768]{2,1,0:T(8,128)} %param.56, ...), kind=kLoop, calls=%fused_computation.24 | loop fusion | flops 10027008 | bytes 15335436 | tf_op jit(solution)/shard_map/sub | solution.py:1170
  623.8 4.4 multiply_subtract_fusion.1
  628.2 1.5 multiply_subtract_fusion.3
  629.7 6.1 multiply_subtract_fusion.2
  635.9 0.6 slice-done.3
  636.5 1.2 copy-done.1
  637.6 10.3 %fusion.13 = (f32[6400,192]{0,1:T(8,128)}, f32[6400,192]{0,1:T(8,128)}, f32[6400,192]{0,1:T(8,128)}) fusion(f32[]{:T(128)S(6)} %min.3, f32[192,6400]{1,0:T(8,128)S(1)} %bitcast.93, bf16[192,6400]{1,0:T(8,128)(2,1)S(1)} %copy-done.1, f32[6400,192]{0,1:T(8,128)S(1)} %bitcast.95, f32[]{:T(128)} %bitcast.17, f32[]{:T(128)} %bitcast.15, f32[6400,192]{0,1:T(8,128)} %param.43, ...), kind=kLoop, calls=%fused_computation.63 | loop fusion | flops 22118400 | bytes 36864012 | tf_op jit(solution)/shard_map/transpose | solution.py:1288
  (91 shorter events, 0.5 us)
Async XLA Ops:
  7.2 215.4 %all-gather.2.cloned.1.call-start = ((), (), s32[]{:S(2)}) async-start(), calls=%async_computation.1 | async-start | bytes 12288000 | tf_op jit(solution)/shard_map/all_gather | solution.py:1196
  11.3 0.8 copy-start.23
  11.3 0.8 copy-start.21
  11.3 0.8 copy-start.19
  11.3 580.4 %reduce-scatter.2.cloned.1.call-start = ((), (), s32[]{:S(2)}) async-start(), calls=%async_computation.2 | async-start | bytes 12288000 | tf_op jit(solution)/shard_map/reduce_scatter | solution.py:1237
  12.3 4.8 copy-start.2
  15.2 3.1 copy-start.4
  19.4 160.3 %copy-start.25 = (s32[1024]{0:T(1024)S(1)}, s32[1024]{0:T(1024)}, u32[]{:S(2)}) copy-start(s32[1024]{0:T(1024)} %param.37) | copy-start | bytes 12292
  19.4 161.3 %copy-start.24 = (s32[6400]{0:T(1024)S(1)}, s32[6400]{0:T(1024)}, u32[]{:S(2)}) copy-start(s32[6400]{0:T(1024)} %param.40) | copy-start | bytes 76804
  190.3 23.5 %copy-start = (bf16[1024,768]{1,0:T(8,128)(2,1)}, bf16[1024,768]{1,0:T(8,128)(2,1)S(1)}, u32[]{:S(2)}) copy-start(bf16[1024,768]{1,0:T(8,128)(2,1)S(1)} %get-tuple-element.594.x_ref) | copy-start | bytes 4718596
  330.6 2.4 copy-start.26
  330.7 2.5 copy-start.27
  330.7 2.6 copy-start.28
  330.7 3.4 copy-start.29
  590.5 1.3 copy-start.6
  591.8 19.2 %copy-start.16 = (f32[3,192]{0,1:T(8,128)S(1)}, f32[3,192]{0,1:T(8,128)}, u32[]{:S(2)}) copy-start(f32[3,192]{0,1:T(8,128)} %copy.178) | copy-start | bytes 6916
  591.8 19.2 %copy-start.17 = (f32[3,192]{0,1:T(8,128)S(1)}, f32[3,192]{0,1:T(8,128)}, u32[]{:S(2)}) copy-start(f32[3,192]{0,1:T(8,128)} %copy.179) | copy-start | bytes 6916
  591.8 19.5 %copy-start.20 = (f32[3,192]{1,0:T(4,128)S(1)}, f32[3,192]{1,0:T(4,128)}, u32[]{:S(2)}) copy-start(f32[3,192]{1,0:T(4,128)} %param.60) | copy-start | bytes 6916
  591.8 21.3 %copy-start.22 = (f32[3,192]{1,0:T(4,128)S(1)}, f32[3,192]{1,0:T(4,128)}, u32[]{:S(2)}) copy-start(f32[3,192]{1,0:T(4,128)} %param.57) | copy-start | bytes 6916
  591.8 21.4 %copy-start.18 = (f32[3,192]{0,1:T(8,128)S(1)}, f32[3,192]{0,1:T(8,128)}, u32[]{:S(2)}) copy-start(f32[3,192]{0,1:T(8,128)} %copy.175) | copy-start | bytes 6916
  608.9 7.7 %copy-start.3 = (f32[1,768,768]{2,1,0:T(8,128)S(1)}, f32[1,768,768]{2,1,0:T(8,128)}, u32[]{:S(2)}) copy-start(f32[1,768,768]{2,1,0:T(8,128)} %param.54) | copy-start | bytes 7077892
  616.6 7.1 %copy-start.5 = (f32[1,192,3072]{2,1,0:T(8,128)S(1)}, f32[1,192,3072]{2,1,0:T(8,128)}, u32[]{:S(2)}) copy-start(f32[1,192,3072]{2,1,0:T(8,128)} %param.51) | copy-start | bytes 7077892
  616.6 7.1 %copy-start.9 = (bf16[192,3072]{1,0:T(8,128)(2,1)S(1)}, bf16[192,3072]{1,0:T(8,128)(2,1)}, u32[]{:S(2)}) copy-start(bf16[192,3072]{1,0:T(8,128)(2,1)} %get-tuple-element.258.u_ref) | copy-start | bytes 3538948
  616.6 7.1 %copy-start.10 = (f32[1,192,3072]{2,1,0:T(8,128)S(1)}, f32[1,192,3072]{2,1,0:T(8,128)}, u32[]{:S(2)}) copy-start(f32[1,192,3072]{2,1,0:T(8,128)} %param.53) | copy-start | bytes 7077892
  616.6 7.1 %copy-start.11 = (f32[1,192,3072]{2,1,0:T(8,128)S(1)}, f32[1,192,3072]{2,1,0:T(8,128)}, u32[]{:S(2)}) copy-start(f32[1,192,3072]{2,1,0:T(8,128)} %param.52) | copy-start | bytes 7077892
  616.7 19.2 %slice-start.4 = ((s8[4915200]{0:T(1024)(128)(4,1)}), s8[720896]{0:T(1024)(128)(4,1)S(1)}, s32[]{:S(2)}) async-start(s8[4915200]{0:T(1024)(128)(4,1)} %bitcast.94), calls=%async_computation.7 | async-start | bytes 1441792
  623.7 4.5 copy-start.12
  623.7 4.4 copy-start.13
  623.7 4.4 copy-start.14
  623.8 4.4 copy-start.15
  623.8 6.0 copy-start.7
  623.8 5.9 copy-start.8
  623.8 12.0 %slice-start.5 = ((s8[4915200]{0:T(1024)(128)(4,1)}), s8[4194304]{0:T(1024)(128)(4,1)S(1)}, s32[]{:S(2)}) async-start(s8[4915200]{0:T(1024)(128)(4,1)} %bitcast.94), calls=%async_computation.8 | async-start | bytes 8388608
  628.2 7.6 %slice-start = ((s8[4915200]{0:T(1024)(128)(4,1)}), s8[4194304]{0:T(1024)(128)(4,1)S(1)}, s32[]{:S(2)}) async-start(s8[4915200]{0:T(1024)(128)(4,1)} %bitcast.90), calls=%async_computation.3 | async-start | bytes 8388608
  628.2 7.6 %slice-start.2 = ((s8[4915200]{0:T(1024)(128)(4,1)}), s8[4194304]{0:T(1024)(128)(4,1)S(1)}, s32[]{:S(2)}) async-start(s8[4915200]{0:T(1024)(128)(4,1)} %bitcast.92), calls=%async_computation.5 | async-start | bytes 8388608
  629.7 6.1 slice-start.1
  629.7 6.7 %slice-start.3 = ((s8[4915200]{0:T(1024)(128)(4,1)}), s8[720896]{0:T(1024)(128)(4,1)S(1)}, s32[]{:S(2)}) async-start(s8[4915200]{0:T(1024)(128)(4,1)} %bitcast.92), calls=%async_computation.6 | async-start | bytes 1441792
  629.7 7.9 %copy-start.1 = (bf16[192,6400]{1,0:T(8,128)(2,1)S(1)}, bf16[192,6400]{1,0:T(8,128)(2,1)}, u32[]{:S(2)}) copy-start(bf16[192,6400]{1,0:T(8,128)(2,1)} %reduce-scatter.2.cloned.1.call-done.dw_ref) | copy-start | bytes 7372804
Sparse Core Ops, SparseCore 0:
  11.5 171.3 all-gather.1
  330.8 154.2 reduce-scatter.1

commit v4 on v3

--- a/solution.py
+++ b/solution.py
@@ -111,19 +111,22 @@
 
 
 def embed_kernel(
-    nb, nv, cap, part, first, *refs
+    nb, nv, cap, part, rows, first, split, *refs
 ):
-    round_ref, tok_ref, table_ref = refs[:3]
+    round_ref, tok_ref, words = refs[:3]
     shards, refs = (refs[3:7], refs[7:]) if first else ((), refs[3:])
+    target_ref, refs = (refs[0], refs[1:]) if split else (None, refs)
     x_ref, ids_ref, place_ref, most_ref, tok_ref_all = refs[:5]
     wholes, refs = (refs[5:9], refs[9:]) if first else ((), refs[5:])
-    words, before, ranks, work, sent, got, spread, mixed, turned = refs[:9]
-    tok_out, tok_in, row_out, row_in, mix_out, mix_in = refs[9:15]
+    (quarter_ref, target_all), refs = (refs[:2], refs[2:]) if split else ((None, None), refs)
+    before, ranks, work, sent, got, spread, mixed, turned = refs[:8]
+    tok_out, tok_in, row_out, row_in, mix_out, mix_in = refs[8:14]
     b, v = lax.axis_index("batch"), lax.axis_index("vocab")
-    width, rows = table_ref.shape
+    width = words.shape[0]
     shift = round_ref[0] * cap
     meet((("batch", nb), ("vocab", nv)))
-    gather = WeightGather(nb, shards, wholes, *refs[15:20]) if first else None
+    gather = WeightGather(nb, shards, wholes, *refs[14:19]) if first else None
+    quarter_out, quarter_in, quarter_own, target_out, target_in = refs[19:24] if split else [None] * 5
 
     def tok_copy(step):
         return send(
@@ -132,10 +135,33 @@
 
     for step in range(1, nb):
         tok_copy(step).start()
+
+    def target_copy(step):
+        return send(
+            target_ref, target_all.at[b], target_out.at[step], target_in.at[step], {"batch": lax.rem(b + step, nb)}
+        )
+
+    def quarter(owner):
+        return words.at[:, lanes(owner * (words.shape[1] // nb), words.shape[1] // nb)]
+
+    def quarter_copy(step):
+        other = lax.rem(b + step, nb)
+        place = quarter_ref.at[pl.ds(pl.multiple_of(b * width, 16), width), :]
+        return send(quarter(other), place, quarter_out.at[step], quarter_in.at[step], {"batch": other})
+
+    def quarter_keep():
+        place = quarter_ref.at[pl.ds(pl.multiple_of(b * width, 16), width), :]
+        return pltpu.make_async_copy(quarter(b), place, quarter_own.at[0])
+
+    if split:
+        target_all[b] = target_ref[...]
+        for step in range(1, nb):
+            target_copy(step).start()
     if first:
         gather.start()
+    if split:
+        quarter_keep().start()
     tok_ref_all[b] = tok_ref[...]
-    words[...] = table_ref[...].astype(BF)
     before[...] = (iota((SEQ_LEN, SEQ_LEN), 0) < iota((SEQ_LEN, SEQ_LEN), 1)).astype(FL).astype(BF)
     for step in range(1, nb):
         tok_copy(step).wait()
@@ -192,6 +218,9 @@
     each(1, nv + 1, build)
     if first:
         gather.pass_on()
+    if split:
+        for step in range(1, nb):
+            quarter_copy(step).start()
 
     keys = []
     for p in range(nb):
@@ -237,6 +266,11 @@
     x_ref[...] = turned[...].reshape(nb * width, SEQ_LEN).T
     if first:
         gather.finish()
+    if split:
+        quarter_keep().wait()
+        for step in range(1, nb):
+            target_copy(step).wait()
+            quarter_copy(step).wait()
 
 
 class WeightGather:
@@ -319,8 +353,9 @@
                 self.pair(w, k).wait()
 
 
-def embed(nb, nv, cap, turn, tok, table, shards=()):
-    width, rows = table.shape
+def embed(nb, nv, cap, rows, turn, tok, table, shards=(), targets=None):
+    width = table.shape[0]
+    split = targets is not None
     part = chunk_of(rows, 640)
     count = nb * cap
     outs = [
@@ -332,9 +367,10 @@
     ]
     first = len(shards) > 0
     outs += [SD((nb * item.shape[0], item.shape[1]), BF) for item in shards]
+    if split:
+        outs += [SD((D, table.shape[1] // nb), BF), SD((nb, *targets.shape), I32)]
     dma = pltpu.SemaphoreType.DMA
     scratch = [
-        pltpu.VMEM((width, rows), BF),
         pltpu.VMEM((SEQ_LEN, SEQ_LEN), BF),
         pltpu.VMEM((nb, nv, SEQ_LEN), I32),
         pltpu.VMEM((count, width), FL),
@@ -347,10 +383,15 @@
     ]
     if first:
         scratch += [dma((4,)), dma((4, 4)), dma((4, 4)), dma((4, 4)), dma((4, 4))]
+    if split:
+        scratch += [dma((nb,)), dma((nb,)), dma((1,)), dma((nb,)), dma((nb,))]
+    extra = [targets] if split else []
     return run(
-        functools.partial(embed_kernel, nb, nv, cap, part, first), outs, scratch, [turn, tok, table, *shards],
+        functools.partial(embed_kernel, nb, nv, cap, part, rows, first, split), outs, scratch,
+        [turn, tok, table, *shards, *extra],
         "embed" if first else "embed_more", 0 if first else 3,
-        in_specs=[SM, VM, VM] + [HB] * len(shards), out_specs=[VM] * 5 + [HB] * len(shards),
+        in_specs=[SM, VM, VM] + [HB] * len(shards) + [VM] * len(extra),
+        out_specs=[VM] * 5 + [HB] * len(shards) + ([HB, VM] if split else []),
     )
 
 
@@ -377,7 +418,7 @@
         return send(source, self.near[w], self.pair_out.at[w], self.pair_in.at[w], self.sibling)
 
     def start(self):
-        for w in range(4):
+        for w in (2, 3, 0, 1):
             self.pair(w).start()
             self.load(w).start()
 
@@ -387,19 +428,18 @@
         source = self.own[w].at[pl.ds(pl.multiple_of(other * rows, 16), rows), :]
         return send(source, self.shard[w].at[step], self.mix_out.at[w, step], self.mix_in.at[w, step], {"batch": other})
 
-    def scatter(self):
-        for w in range(4):
-            self.load(w).wait()
-            self.pair(w).wait()
-            rows = self.own[w].shape[0] // self.nb
-
-            def add(i, w=w, rows=rows):
-                cut = pl.ds(pl.multiple_of(i * rows, 16), rows)
-                self.own[w][cut, :] = (self.own[w][cut, :].astype(FL) + self.near[w][cut, :].astype(FL)).astype(BF)
-
-            each(0, self.nb, add)
-            for step in range(1, self.nb):
-                self.mix(w, step).start()
+    def scatter(self, w):
+        self.load(w).wait()
+        self.pair(w).wait()
+        rows = self.own[w].shape[0] // self.nb
+
+        def add(i, w=w, rows=rows):
+            cut = pl.ds(pl.multiple_of(i * rows, 16), rows)
+            self.own[w][cut, :] = (self.own[w][cut, :].astype(FL) + self.near[w][cut, :].astype(FL)).astype(BF)
+
+        each(0, self.nb, add)
+        for step in range(1, self.nb):
+            self.mix(w, step).start()
 
     def pieces(self, w):
         rows = self.total[w].shape[0]
@@ -427,46 +467,44 @@
         place = self.result[w].at[pl.ds(pl.multiple_of(source * size, 16), size), :]
         return send(place, place, self.all_out.at[w, step], self.all_in.at[w, step], self.peer(step)[1])
 
-    def reduce(self):
-        for w in range(4):
-            rows = self.total[w].shape[0]
-            for step in range(1, self.nb):
-                self.mix(w, step).wait()
-            here = pl.ds(pl.multiple_of(self.b * rows, 16), rows)
-            value = self.own[w][here, :].astype(FL)
-            for step in range(1, self.nb):
-                value = value + self.shard[w][step].astype(FL)
-            self.total[w][...] = value.astype(BF)
-            count = self.pieces(w)[0]
-
-            def go(step, w=w, count=count):
-                @pl.when(self.peer(step)[0] < count)
-                def _():
-                    self.cut(w, step).start()
-
-            each(1, self.chips, go)
-
-    def collect(self):
-        for w in range(4):
-            count, size = self.pieces(w)
-            mine = pl.ds(pl.multiple_of(self.chip * size, 16), size)
-
-            @pl.when(self.chip < count)
-            def _(w=w, mine=mine):
-                def add(step, value):
-                    self.cut(w, step).wait_recv()
-                    return value + self.bits[w][step].astype(FL)
-
-                value = lax.fori_loop(1, self.chips, add, self.total[w][mine, :].astype(FL))
-                self.result[w][mine, :] = value.astype(BF)
-                each(1, self.chips, lambda step: self.back(w, step).start())
-
-            def sent(step, w=w, count=count):
-                @pl.when(self.peer(step)[0] < count)
-                def _():
-                    self.cut(w, step).wait_send()
-
-            each(1, self.chips, sent)
+    def reduce(self, w):
+        rows = self.total[w].shape[0]
+        for step in range(1, self.nb):
+            self.mix(w, step).wait()
+        here = pl.ds(pl.multiple_of(self.b * rows, 16), rows)
+        value = self.own[w][here, :].astype(FL)
+        for step in range(1, self.nb):
+            value = value + self.shard[w][step].astype(FL)
+        self.total[w][...] = value.astype(BF)
+        count = self.pieces(w)[0]
+
+        def go(step, w=w, count=count):
+            @pl.when(self.peer(step)[0] < count)
+            def _():
+                self.cut(w, step).start()
+
+        each(1, self.chips, go)
+
+    def collect(self, w):
+        count, size = self.pieces(w)
+        mine = pl.ds(pl.multiple_of(self.chip * size, 16), size)
+
+        @pl.when(self.chip < count)
+        def _(w=w, mine=mine):
+            def add(step, value):
+                self.cut(w, step).wait_recv()
+                return value + self.bits[w][step].astype(FL)
+
+            value = lax.fori_loop(1, self.chips, add, self.total[w][mine, :].astype(FL))
+            self.result[w][mine, :] = value.astype(BF)
+            each(1, self.chips, lambda step: self.back(w, step).start())
+
+        def sent(step, w=w, count=count):
+            @pl.when(self.peer(step)[0] < count)
+            def _():
+                self.cut(w, step).wait_send()
+
+        each(1, self.chips, sent)
 
     def last(self, w):
         return send(
@@ -518,11 +556,14 @@
     )
 
 
-def unembed_kernel(nb, nv, cap, part, first, *refs):
+def unembed_kernel(nb, nv, cap, part, first, split, *refs):
     x_ref, ids_ref, place_ref = refs[:3]
     grads, refs = (refs[3:7], refs[7:]) if first else ((), refs[3:])
+    quarter_ref, refs = (refs[0], refs[1:]) if split else (None, refs)
     out_ref = refs[0]
     sums, refs = (refs[1:5], refs[5:]) if first else ((), refs[1:])
+    dw_ref, refs = (refs[0], refs[1:]) if split else (None, refs)
+    (quarter_out, quarter_in, quarter_own), refs = (refs[:3], refs[3:]) if split else ([None] * 3, refs)
     turned, parts, sent, got, mix_out, mix_in, row_out, row_in = refs[:8]
     layer = GradientSum(nb, nv, grads, sums, refs[8:]) if first else None
     b, v = lax.axis_index("batch"), lax.axis_index("vocab")
@@ -541,6 +582,19 @@
     parts[b] = turned[b]
     for step in range(1, nb):
         mix_copy(step).wait()
+
+    def quarter_place():
+        size = quarter_ref.shape[1]
+        return dw_ref.at[:, lanes(b * size, size)]
+
+    def quarter_copy(step):
+        other = lax.rem(b + step, nb)
+        source = quarter_ref.at[pl.ds(pl.multiple_of(other * width, 16), width), :]
+        return send(source, quarter_place(), quarter_out.at[step], quarter_in.at[step], {"batch": other})
+
+    def quarter_keep():
+        source = quarter_ref.at[pl.ds(pl.multiple_of(b * width, 16), width), :]
+        return pltpu.make_async_copy(source, quarter_place(), quarter_own.at[0])
 
     def row_copy(step):
         return send(
@@ -566,9 +620,13 @@
         def _():
             got[v] = block
 
+    if first:
+        layer.scatter(2)
     each(1, nv + 1, build)
     if first:
-        layer.scatter()
+        layer.scatter(3)
+    if split:
+        quarter_keep().start()
     out_ref[...] = jnp.zeros_like(out_ref)
 
     def take(step):
@@ -586,16 +644,35 @@
 
         each(0, rows // part, piece)
 
-    each(0, nv // 2, take)
     if first:
-        layer.reduce()
-    each(nv // 2, nv, take)
-    if first:
-        layer.collect()
+        quarter = nv // 4
+        each(0, quarter, take)
+        layer.reduce(2)
+        layer.scatter(0)
+        each(quarter, 2 * quarter, take)
+        layer.reduce(3)
+        layer.scatter(1)
+        if split:
+            for step in range(1, nb):
+                quarter_copy(step).start()
+        each(2 * quarter, 3 * quarter, take)
+        layer.collect(2)
+        each(3 * quarter, nv, take)
+        layer.collect(3)
+        for w in (0, 1):
+            layer.reduce(w)
+        for w in (0, 1):
+            layer.collect(w)
         layer.finish()
-
-
-def unembed(nb, nv, cap, width, rows, grad, ids, place, grads=()):
+        if split:
+            quarter_keep().wait()
+            for step in range(1, nb):
+                quarter_copy(step).wait()
+    else:
+        each(0, nv, take)
+
+
+def unembed(nb, nv, cap, width, rows, grad, ids, place, grads=(), quarter=None):
     part = chunk_of(rows, 640)
     count = nb * cap
     dma = pltpu.SemaphoreType.DMA
@@ -606,18 +683,24 @@
         pltpu.VMEM((nv, width, count), BF),
         dma((nb,)), dma((nb,)), dma((nv,)), dma((nv,)),
     ]
-    first = len(grads) > 0
+    first, split = len(grads) > 0, quarter is not None
+    if split:
+        scratch = [dma((nb,)), dma((nb,)), dma((1,))] + scratch
     if first:
         scratch += gradient_scratch(nb, nv, grads)
+    outs = [SD((width, rows), FL)] + [SD((item.shape[0] // nb, item.shape[1]), BF) for item in grads]
+    extra = [quarter] if split else []
+    if split:
+        outs.append(SD((width, nb * quarter.shape[1]), BF))
     return run(
-        functools.partial(unembed_kernel, nb, nv, cap, part, first),
-        [SD((width, rows), FL)] + [SD((item.shape[0] // nb, item.shape[1]), BF) for item in grads],
+        functools.partial(unembed_kernel, nb, nv, cap, part, first, split),
+        outs,
         scratch,
-        [grad, ids, place, *grads],
+        [grad, ids, place, *grads, *extra],
         "unembed" if first else "unembed_more",
         2 if first else 4,
-        in_specs=[VM] * 3 + [HB] * len(grads),
-        out_specs=[VM] + [HB] * len(grads),
+        in_specs=[VM] * 3 + [HB] * (len(grads) + len(extra)),
+        out_specs=[VM] + [HB] * (len(grads) + len(extra)),
     )
 
 
@@ -1104,6 +1187,299 @@
     )
 
 
+def wide_head_kernel(
+    nb, nv, block_rows, f_ref, w_ref, live_ref, target_ref, df_ref, dw_ref, loss_ref,
+    fall, ft, expo, words_sum, mine, first_got, merged, second_got, tile, third_got, tiles, coef, group, half, handed, mix_got,
+    far_sum, far_got,
+    z_out, z_in, mix_out, mix_in, near_out, near_in, s_out, s_in, pair_out, pair_in, give_out, give_in, sum_out, sum_in,
+):
+    b, v = lax.axis_index("batch"), lax.axis_index("vocab")
+    rows = w_ref.shape[1]
+    core, chip, chips = lax.rem(v, 2), v // 2, nv // 2
+    sibling = {"vocab": v + 1 - 2 * core}
+    base = v * block_rows + b * rows
+    live = live_ref[:, lanes(b * rows, rows)] > 0
+    span = nv * PICKS
+    meet((("batch", nb), ("vocab", nv)))
+
+    def peer(step):
+        return {"vocab": lax.rem(chip + step, chips) * 2 + core}
+
+    def other(step):
+        return {"batch": lax.rem(b + step, nb)}
+
+    def slot(s, k):
+        return lax.rem(b - s + nb, nb) * nv + lax.rem(chip - k + chips, chips) * 2 + core
+
+    def z_copy(k):
+        return send(f_ref, fall.at[b * nv + v], z_out.at[k], z_in.at[k], peer(k))
+
+    def mix_copy(s, k):
+        place = fall.at[slot(0, k)]
+        return send(place, place, mix_out.at[k, s], mix_in.at[k, s], other(s))
+
+    def near_copy(s, k):
+        place = fall.at[slot(s, k)]
+        return send(place, place, near_out.at[k, s], near_in.at[k, s], sibling)
+
+    def arrive(s, k):
+        if s == 0:
+
+            @pl.when(k > 0)
+            def _():
+                z_copy(k).wait_recv()
+
+            each(1, nb, lambda t: mix_copy(t, k).start())
+        else:
+            mix_copy(s, k).wait_recv()
+        near_copy(s, k).start()
+
+    fall[b * nv + v] = f_ref[...]
+    each(1, chips, lambda k: z_copy(k).start())
+    arrive(0, 0)
+
+    def logits(s, k):
+        near_copy(s, k).wait_recv()
+        p, c = lax.rem(b - s + nb, nb), lax.rem(chip - k + chips, chips)
+        first = p * nv + c * 2
+        start = pl.multiple_of(first * PICKS, 2 * PICKS)
+        features = fall[pl.ds(first, 2)].reshape(2 * PICKS, D)
+        ft[:, pl.ds(start, 2 * PICKS)] = features.T
+        line = target_ref[p, :, pl.ds(pl.multiple_of(c * 2 * PICKS, 2 * PICKS), 2 * PICKS)].astype(FL)
+        target = jnp.broadcast_to(line, (128, 2 * PICKS)).T[:, 0:1].astype(I32) - base
+        value = nn(features, w_ref[...])
+        peak = jnp.max(jnp.where(live, value, NEG_BIG), axis=1, keepdims=True)
+        hot = target == iota((2 * PICKS, rows), 1)
+        e = jnp.where(live, jnp.exp(value - peak), 0.0)
+        expo[pl.ds(start, 2 * PICKS), :] = e.astype(BF)
+        total = jnp.sum(e, axis=1, keepdims=True)
+        picked = jnp.sum(jnp.where(hot, value, 0.0), axis=1, keepdims=True)
+        valid = jnp.sum(jnp.where(hot & live, 1.0, 0.0), axis=1, keepdims=True)
+        lane = iota((2 * PICKS, 128), 1)
+        wide = jnp.where(lane == 0, peak, jnp.where(lane == 1, total, jnp.where(lane == 2, picked, valid))).T
+        mine[c * 2, p] = wide[:8, :PICKS]
+        mine[c * 2 + 1, p] = wide[:8, PICKS:]
+
+    for s in range(nb):
+
+        def one(k, s=s):
+            @pl.when(k + 1 < chips)
+            def _():
+                arrive(s, k + 1)
+
+            if s + 1 < nb:
+
+                @pl.when(k + 1 == chips)
+                def _():
+                    arrive(s + 1, 0)
+
+            logits(s, k)
+
+        each(0, chips, one)
+
+    def merge(read, count):
+        peak = lax.fori_loop(
+            0, count, lambda u, top: jnp.maximum(top, read(u)[0:1, :]), jnp.full((1, PICKS), NEG_BIG, FL)
+        )
+
+        def add(u, carry):
+            one = read(u)
+            return carry[0] + one[1:2, :] * jnp.exp(one[0:1, :] - peak), carry[1] + one[2:3, :], carry[2] + one[3:4, :]
+
+        zero = jnp.zeros((1, PICKS), FL)
+        return (peak, *lax.fori_loop(0, count, add, (zero, zero, zero)))
+
+    def tile_of(rows_of):
+        line = iota((8, PICKS), 0)
+        value = jnp.zeros((8, PICKS), FL)
+        for i, row in enumerate(rows_of):
+            value = jnp.where(line == i, row, value)
+        return value
+
+    def first_copy(t):
+        u = lax.rem(v + t, nv)
+        return send(mine.at[u], first_got.at[v], s_out.at[0, t], s_in.at[0, t], {"vocab": u})
+
+    each(1, nv, lambda t: first_copy(t).start())
+    first_got[v] = mine[v]
+    each(1, nv, lambda t: first_copy(t).wait())
+    for p in range(nb):
+        merged[p] = tile_of(merge(lambda u, p=p: first_got[u, p], nv))
+
+    def second_copy(t):
+        return send(merged.at[lax.rem(b + t, nb)], second_got.at[b], s_out.at[1, t], s_in.at[1, t], other(t))
+
+    each(1, nb, lambda t: second_copy(t).start())
+    second_got[b] = merged[b]
+    each(1, nb, lambda t: second_copy(t).wait())
+    peak, total, picked, valid = merge(lambda u: second_got[u], nb)
+    tile[...] = tile_of((peak + jnp.log(jnp.maximum(total, 1e-37)), picked, valid))
+
+    def third_copy(t):
+        return send(tile, third_got.at[b], s_out.at[2, t], s_in.at[2, t], other(t))
+
+    each(1, nb, lambda t: third_copy(t).start())
+    third_got[b] = tile[...]
+    each(1, nb, lambda t: third_copy(t).wait())
+
+    def last_copy(t):
+        return send(third_got, tiles.at[v], s_out.at[3, t], s_in.at[3, t], {"vocab": lax.rem(v + t, nv)})
+
+    each(1, nv, lambda t: last_copy(t).start())
+    tiles[v] = third_got[...]
+    each(1, nv, lambda t: last_copy(t).wait())
+
+    def coefficients(p):
+        count = lax.fori_loop(0, nv, lambda u, total: total + tiles[u, p, 2:3, :], jnp.zeros((1, PICKS), FL))
+        share = 1.0 / (jnp.maximum(jnp.sum(count, axis=1, keepdims=True), 1.0) * nb)
+
+        def spread(c, loss):
+            rows_of = []
+            for side in range(2):
+                u = c * 2 + side
+                lse, picked, valid = (tiles[u, p, i : i + 1, :] for i in range(3))
+                weight = valid * share
+                loss = loss + weight * (lse - picked)
+                rows_of.append((weight * jnp.exp(mine[u, p, 0:1, :] - lse), weight))
+            line = iota((128, 2 * PICKS), 0)
+            alpha = jnp.concatenate([rows_of[0][0], rows_of[1][0]], axis=1)
+            weight = jnp.concatenate([rows_of[0][1], rows_of[1][1]], axis=1)
+            start = pl.multiple_of(p * span + c * 2 * PICKS, 2 * PICKS)
+            coef[pl.ds(start, 2 * PICKS), :] = jnp.where(line == 0, alpha, weight).T
+            return loss
+
+        loss = lax.fori_loop(0, chips, spread, jnp.zeros((1, PICKS), FL))
+
+        @pl.when(p == b)
+        def _():
+            loss_ref[...] = jnp.broadcast_to(jnp.sum(loss, axis=1, keepdims=True), loss_ref.shape)
+
+    each(0, nb, coefficients)
+
+    def shard(k, side):
+        return pl.ds(pl.multiple_of((2 * k + side) * PICKS, PICKS), PICKS)
+
+    def pair_copy(s, k):
+        return send(handed.at[s, k], half.at[s, k], pair_out.at[s, k], pair_in.at[s, k], sibling)
+
+    def give_copy(s):
+        return send(handed.at[s], mix_got.at[s], give_out.at[s], give_in.at[s], other(s))
+
+    def exchange(s):
+        def add(k):
+            pair_copy(s, k).wait()
+            handed[s, k] = (group[shard(k, core), :] + half[s, k].astype(FL)).astype(BF)
+
+        each(0, chips, add)
+        if s > 0:
+            give_copy(s).start()
+
+    for s in list(range(1, nb)) + [0]:
+        p = lax.rem(b + s, nb)
+
+        def strip(c, p=p):
+            start = pl.multiple_of(p * span + c * 2 * PICKS, 2 * PICKS)
+            here = pl.ds(start, 2 * PICKS)
+            line = target_ref[p, :, pl.ds(pl.multiple_of(c * 2 * PICKS, 2 * PICKS), 2 * PICKS)].astype(FL)
+            target = jnp.broadcast_to(line, (128, 2 * PICKS)).T[:, 0:1].astype(I32) - base
+            two = coef[here, :]
+            hot = target == iota((2 * PICKS, rows), 1)
+            value = two[:, 0:1] * expo[here, :].astype(FL) - jnp.where(hot, two[:, 1:2], 0.0)
+            expo[here, :] = value.astype(BF)
+
+        each(0, chips, strip)
+        def features_grad(i, p=p):
+            here = pl.ds(pl.multiple_of(i * 512, 512), 512)
+            group[here, :] = nt(expo[pl.ds(pl.multiple_of(p * span + i * 512, 512), 512), :], w_ref[...])
+
+        each(0, span // 512, features_grad)
+
+        def swap(k, s=s):
+            handed[s, k] = group[shard(k, 1 - core), :].astype(BF)
+            pair_copy(s, k).start()
+
+        each(0, chips, swap)
+        exchange(s)
+
+    words_sum[...] = jnp.zeros_like(words_sum)
+
+    def words_grad(i):
+        cut = lanes(i * 512, 512)
+        words_sum[...] += nn(ft[:, cut], expo[cut, :])
+
+    each(0, nb * span // 512, words_grad)
+    dw_ref[...] = words_sum[...].astype(BF)
+
+    for s in range(1, nb):
+        give_copy(s).wait()
+
+    def total_of(k):
+        value = handed[0, k].astype(FL)
+        for s in range(1, nb):
+            value = value + mix_got[s, k].astype(FL)
+        return value
+
+    def sum_copy(t):
+        return send(far_sum.at[t], far_got.at[t], sum_out.at[t], sum_in.at[t], peer(t))
+
+    def pass_on(t):
+        far_sum[t] = total_of(lax.rem(chip + t, chips)).astype(BF)
+        sum_copy(t).start()
+
+    each(1, chips, pass_on)
+    df_ref[...] = total_of(chip)
+
+    def collect(t):
+        sum_copy(t).wait()
+        df_ref[...] += far_got[t].astype(FL)
+
+    each(1, chips, collect)
+    each(1, chips, lambda k: z_copy(k).wait_send())
+    for s in range(nb):
+        each(0, chips, lambda k, s=s: near_copy(s, k).wait_send())
+        if s > 0:
+            each(0, chips, lambda k, s=s: mix_copy(s, k).wait_send())
+
+
+def wide_head(nb, nv, block_rows, features, words, live, targets):
+    rows = words.shape[1]
+    tokens = nb * nv * PICKS
+    chips = nv // 2
+    dma = pltpu.SemaphoreType.DMA
+    most = max(nb, nv)
+    scratch = [
+        pltpu.VMEM((nb * nv, PICKS, D), BF),
+        pltpu.VMEM((D, tokens), BF),
+        pltpu.VMEM((tokens, rows), BF),
+        pltpu.VMEM((D, rows), FL),
+        pltpu.VMEM((nv, nb, 8, PICKS), FL),
+        pltpu.VMEM((nv, nb, 8, PICKS), FL),
+        pltpu.VMEM((nb, 8, PICKS), FL),
+        pltpu.VMEM((nb, 8, PICKS), FL),
+        pltpu.VMEM((8, PICKS), FL),
+        pltpu.VMEM((nb, 8, PICKS), FL),
+        pltpu.VMEM((nv, nb, 8, PICKS), FL),
+        pltpu.VMEM((tokens, 128), FL),
+        pltpu.VMEM((nv * PICKS, D), FL),
+        pltpu.VMEM((nb, chips, PICKS, D), BF),
+        pltpu.VMEM((nb, chips, PICKS, D), BF),
+        pltpu.VMEM((nb, chips, PICKS, D), BF),
+        pltpu.VMEM((chips, PICKS, D), BF),
+        pltpu.VMEM((chips, PICKS, D), BF),
+        dma((chips,)), dma((chips,)), dma((chips, nb)), dma((chips, nb)), dma((chips, nb)), dma((chips, nb)),
+        dma((4, most)), dma((4, most)), dma((nb, chips)), dma((nb, chips)), dma((nb,)), dma((nb,)),
+        dma((chips,)), dma((chips,)),
+    ]
+    return run(
+        functools.partial(wide_head_kernel, nb, nv, block_rows),
+        [SD((PICKS, D), FL), SD((D, rows), BF), SD((8, 128), FL)],
+        scratch,
+        [features, words, live, targets],
+        "wide_head",
+        1,
+    )
+
+
 def norm_kernel(
     nb, nv, extra_ref, dw_ref, a_ref, p_ref, u_ref, c_ref, loss_ref, out_ref,
     mine, near, lines, vocab_out, vocab_in, batch_out, batch_in,
@@ -1123,7 +1499,7 @@
         line = lax.fori_loop(0, cols // part, add, jnp.zeros((1, part), FL))
         return jnp.sum(line, axis=1, keepdims=True)
 
-    own = squares((extra_ref, dw_ref), chunk_of(dw_ref.shape[1], 640))
+    own = squares((extra_ref, dw_ref), chunk_of(extra_ref.shape[1], 640))
     layer = squares((a_ref,), 512) + squares((p_ref,), 384) + squares((u_ref,), 512) + squares((c_ref,), 384)
     own = own + jnp.where(v == 0, layer, jnp.zeros_like(layer))
     line = iota((8, 128), 0)
@@ -1193,25 +1569,26 @@
     norms = jnp.concatenate([gain, shift], axis=0)
     packed = jnp.concatenate([attend[0], norms.T, jnp.zeros((width, EXTRA - 6), FL)], axis=1).astype(BF)
     pieces = (packed, project[0].astype(BF), expand[0].astype(BF), contract[0].astype(BF))
-    words = lax.all_gather(table_t.astype(BF), "batch", axis=0, tiled=True)
+    split = nb * nv * PICKS <= 4096
+    rounded = table_t.astype(BF)
+    quarter = -(-rows // (nb * 128)) * 128
+    if split:
+        rounded = jnp.pad(rounded, ((0, 0), (0, nb * quarter - rows)))
+    else:
+        words = lax.all_gather(rounded, "batch", axis=0, tiled=True)
 
     seg_row, pos_row = segments[None, :], counted[None, :]
     tok = tokens.reshape(nv, SEQ_LEN)
-    x, ids, place, most, every, a_all, p_all, u_all, c_all = embed(
-        nb, nv, cap, jnp.zeros((1,), I32), tok, table_t, pieces
+    x, ids, place, most, every, a_all, p_all, u_all, c_all, *rest = embed(
+        nb, nv, cap, rows, jnp.zeros((1,), I32), tok, rounded, pieces, targets[None, :] if split else None
     )
     turns = (most[0, 0].astype(I32) + cap - 1) // cap
 
     def more_rows(state):
         turn, total = state
-        return turn + 1, total + embed(nb, nv, cap, turn[None], tok, table_t)[0]
-
-    x = lax.cond(
-        turns > 1,
-        lambda x: lax.while_loop(lambda state: state[0] < turns, more_rows, (jnp.int32(1), x))[1],
-        lambda x: x,
-        x,
-    )
+        return turn + 1, total + embed(nb, nv, cap, rows, turn[None], tok, rounded)[0]
+
+    x = lax.while_loop(lambda state: state[0] < turns, more_rows, (jnp.int32(1), x))[1]
 
     hall, kv, q, hq, xq, mixed, lse, norm_rows, mixing_t = run(
         attend_kernel,
@@ -1233,8 +1610,12 @@
         [xq, mixed, p_all, u_all, c_all, norm_rows],
         "feed", flops=2 * 10**9, moved=15 * 10**6,
     )
-    df, dw, loss_block = head(nb, nv, features, words, vocab_mask[None, :], targets[:, None])
-    dw_sum = lax.psum_scatter(dw, "batch", scatter_dimension=0, tiled=True)
+    if split:
+        live = jnp.pad(vocab_mask, (0, nb * quarter - rows))[None, :]
+        df, dw, loss_block = wide_head(nb, nv, rows, features, rest[0], live, rest[1])
+    else:
+        df, dw, loss_block = head(nb, nv, features, words, vocab_mask[None, :], targets[:, None])
+        dw_sum = lax.psum_scatter(dw, "batch", scatter_dimension=0, tiled=True)
 
     dc, du, dp, dx1, dmixed, dnorm = run(
         feed_back_kernel,
@@ -1256,7 +1637,9 @@
         "attend_back", flops=12 * 10**9, moved=25 * 10**6,
         in_specs=[SM] + [VM] * 14,
     )
-    extra, *sums = unembed(nb, nv, cap, width, rows, dx, ids, place, (da, dp, du, dc))
+    extra, *sums = unembed(nb, nv, cap, width, rows, dx, ids, place, (da, dp, du, dc), dw if split else None)
+    if split:
+        dw_sum = sums.pop()
 
     def more_grads(state):
         turn, total = state
@@ -1265,15 +1648,10 @@
             nb, nv, cap, width, rows, dx, later, place - jnp.array([0, 1, 0, 0, 0, 0, 0, 0], I32)[None, :, None] * (turn * cap)
         )[0]
 
-    extra = lax.cond(
-        turns > 1,
-        lambda extra: lax.while_loop(lambda state: state[0] < turns, more_grads, (jnp.int32(1), extra))[1],
-        lambda extra: extra,
-        extra,
-    )
+    extra = lax.while_loop(lambda state: state[0] < turns, more_grads, (jnp.int32(1), extra))[1]
 
     totals = norm(nb, nv, extra, dw_sum, sums, loss_block)
-    grad_table = dw_sum.astype(FL) + extra
+    grad_table = dw_sum[:, :rows].astype(FL) + extra
     grad_a, grad_p, grad_u, grad_c = (item.astype(FL) for item in sums)
     grad_norms = grad_a[:, 3 * D : 3 * D + 6].T
     grad_a = grad_a[:, : 3 * D]

time: 662 us -> 613 us (0.926)
  Pallas kernels: 562 us -> 541 us
  between operations: 18.3 us -> 5.01 us
  loops' own time: 16.4 us -> 8.77 us
    pallas_call x8, Pallas kernels: 562 us -> 541 us  [run(): pl.pallas_call(kernel, out_shape=outs, in_specs=in_specs if in_specs is n...]
    another operation x2, loops' own time: 16.4 us -> 8.77 us  [the longest x1 8.54 us: shards(): lax.while_loop(lambda state: state[0] < turns, more_rows, (jnp.int32(1), x))]
  transfers between devices with their start and end apart: 2 -> 0, of which waited for: 0 -> 0; matrix products, arithmetic and copies ran while one was open for 2% -> 0% of each run, Pallas kernels for 67% -> 0%
where the time goes in v4:
time: 613 us; the launch traced here: 607 us
  Pallas kernels  541 us (88%)
  other arithmetic  37.3 us (6%)
  local copies, waits for them, and re-layouts  15.4 us (3%)
  loops' own time  8.77 us (1%)
    pallas_call x8, Pallas kernels, run(): pl.pallas_call(kernel, out_shape=outs, in_specs=in_specs if in_specs is n...  541 us
    sub x6, other arithmetic, adamw(): weight - rate * (fixed_moment / (jnp.sqrt(fixed_square) + ADAM_EPS) + dec...  19.1 us

profile of v4, /device:TPU:0, one launch (start us, length us, event | category | flops | bytes accessed | tf_op | source)
XLA Modules:
  0.0 607.1 jit_solution(8041269769043055689)
XLA Ops:
  0.7 2.6 bitcast_convert_fusion
  3.3 1.6 pad.8.refs_2_
  5.0 1.7 convert_bitcast_fusion.3
  6.8 0.1 copy.164
  6.9 1.1 concatenate.9.refs_3_
  8.1 1.1 convert_bitcast_fusion.1.refs_6_
  9.2 1.0 copy-done.4
  10.2 1.2 convert_bitcast_fusion.2.refs_5_
  11.3 0.7 convert_bitcast_fusion.4.refs_4_
  12.1 138.7 %embed.1 = (bf16[1024,768]{1,0:T(8,128)(2,1)S(1)}, s32[8,768,1]{2,1,0:T(8,128)}, s32[4,8,1024]{2,1,0:T(8,128)S(1)}, f32[8,128]{1,0:T(8,128)}, s32[4,8,1024]{2,1,...) custom-call(s32[1]{0:T(128)} %constant.47.clone.1.refs_0_, ...), custom_call_target="tpu_custom_call" | custom-call | tf_op jit(solution)/shard_map/embed/pallas_call | solution.py:68
  150.8 1.2 slice.36
  152.6 8.5 %while.23 = (s32[]{:T(128)}, bf16[1024,768]{1,0:T(8,128)(2,1)S(1)}, s32[]{:T(128)}, s32[8,1024]{1,0:T(8,128)S(1)}, bf16[192,6656]{1,0:T(8,128)(2,1)}, /*index=5*/s32[]{:T(128)}) while((s32[]{:T(128)}, bf16[1024,768]{1,0:T(8,128)(2,1)S(1)}, s32[]{:T(128)}, s32[8,1024]{1,0:T(8,128)S(1)}, bf16[192,6656]{1,0:T(8,128)(2,1)}, ...), condition=%wide.region_1.2_spmd, body=%wide.region_0.1_spmd.sunk | while | flops 786434 | bytes 4718661 | solution.py:1591
  161.2 23.5 %attend.1 = (bf16[1536,768]{1,0:T(8,128)(2,1)}, bf16[1536,1536]{1,0:T(8,128)(2,1)}, bf16[128,768]{1,0:T(8,128)(2,1)}, bf16[128,768]{1,0:T(8,128)(2,1)}, f32[128,...) custom-call(bf16[1024,768]{1,0:T(8,128)(2,1)S(1)} %get-tuple-element, ...), custom_call_target="tpu_custom_call" | custom-call | flops 7000000000 | bytes 20000000 | tf_op jit(solution)/shard_map/attend/pallas_call | solution.py:68
  184.7 8.8 %feed.1 = (f32[128,768]{1,0:T(8,128)}, bf16[128,768]{1,0:T(8,128)(2,1)}, f32[128,3072]{1,0:T(8,128)}, bf16[128,3072]{1,0:T(8,128)(2,1)}, f32[128,768]{1,0:T(8,128)}, /*index=5*/bf16[128,768]{1,0:T(8,128)(2,1)}) custom-call(f32[128,768]{1,0:T(8,128)} %get-tuple-element.190.xq_ref, bf16[128,768]{1,0:T(8,128)(2,1)} %get-tuple-element.191.o_ref, ...), custom_call_target="tpu_custom_call" | custom-call | flops 2000000000 | bytes 15000000 | tf_op jit(solution)/shard_map/feed/pallas_call | solution.py:68
  193.5 0.6 broadcast_in_dim.50.live_ref
  194.1 133.6 %wide_head.1 = (f32[128,768]{1,0:T(8,128)}, bf16[768,1664]{1,0:T(8,128)(2,1)}, f32[8,128]{1,0:T(8,128)}) custom-call(bf16[128,768]{1,0:T(8,128)(2,1)} %get-tuple-element.196.f_ref, bf16[768,1664]{1,0:T(8,128)(2,1)} %get-tuple-element.197.w_ref, s32[1,6656]{1,0:T(1,128)} %broadcast_in_dim.50.live_ref, s32[4,1,1024]{2,1,0:T(1,128)} %get-tuple-element.198.target_ref), custom_call_target="tpu_custom_call" | custom-call | tf_op jit(solution)/shard_map/wide_head/pallas_call | solution.py:68
  327.8 15.1 %feed_back.1 = (bf16[3072,768]{1,0:T(8,128)(2,1)}, bf16[768,3072]{1,0:T(8,128)(2,1)}, bf16[768,768]{1,0:T(8,128)(2,1)}, f32[128,768]{1,0:T(8,128)}, bf16[128,768]{1,0:T(8,128)(2,1)}, /*index=5*/f32[8,768]{1,0:T(8,128)}) custom-call(f32[128,768]{1,0:T(8,128)} %get-tuple-element.199.df_ref, f32[128,768]{1,0:T(8,128)} %get-tuple-element.200.x2_ref, ...), custom_call_target="tpu_custom_call" | custom-call | flops 4000000000 | bytes 30000000 | tf_op jit(solution)/shard_map/feed_back/pallas_call | solution.py:68
  342.9 34.4 %attend_back.1 = (bf16[768,2560]{1,0:T(8,128)(2,1)}, bf16[1024,768]{1,0:T(8,128)(2,1)S(1)}) custom-call(s32[128]{0:T(128)} %pos_ref.1, bf16[128,768]{1,0:T(8,128)(2,1)} %get-tuple-element.205.do_ref, bf16[128,768]{1,0:T(8,128)(2,1)} %get-tuple-element.206.q_ref, bf16[1536,1536]{1,0:T(8,128)(2,1)} %get-tuple-element.207.kv_ref, ...), custom_call_target="tpu_custom_call" | custom-call | flops 12000000000 | bytes 25000000 | tf_op jit(solution)/shard_map/attend_back/pallas_call | solution.py:68
  377.3 170.3 %unembed.1 = (f32[192,6400]{1,0:T(8,128)}, bf16[192,2560]{1,0:T(8,128)(2,1)}, bf16[192,768]{1,0:T(8,128)(2,1)}, bf16[192,3072]{1,0:T(8,128)(2,1)}, bf16[768,768]{1,0:T(8,128)(2,1)}, /*index=5*/bf16[192,6656]{1,0:T(8,128)(2,1)}) custom-call(bf16[1024,768]{1,0:T(8,128)(2,1)S(1)} %get-tuple-element.520.refs_0_, s32[8,768,1]{2,1,0:T(8,128)} %get-tuple-element.215.refs_1_, ...), custom_call_target="tpu_custom_call" | custom-call | tf_op jit(solution)/shard_map/unembed/pallas_call | solution.py:68
  547.7 0.2 while.24
  547.9 16.2 %norm.1 = f32[8,128]{1,0:T(8,128)} custom-call(f32[192,6400]{1,0:T(8,128)} %get-tuple-element.224.extra_ref, bf16[192,6656]{1,0:T(8,128)(2,1)} %get-tuple-element.225.dw_ref, bf16[192,2560]{1,0:T(8,128)(2,1)} %get-tuple-element.226.a_ref, bf16[192,768]{1,0:T(8,128)(2,1)} %get-tuple-element.227.p_ref, bf16[192,3072]{1,0:T(8,128)(2,1)} %get-tuple-element.228.u_ref, ...), custom_call_target="tpu_custom_call" | custom-call | tf_op jit(solution)/shard_map/norm/pallas_call | solution.py:68
  564.1 1.2 fusion.23
  566.1 0.2 convert_element_type.64
  566.3 1.3 copy-done.6
  568.5 0.1 copy.166
  568.7 0.1 copy.167
  568.8 0.1 copy.172
  569.0 0.1 copy.173
  569.1 0.2 multiply_divide_fusion
  569.3 0.1 copy.174
  569.4 0.1 copy.176
  569.5 0.1 copy.175
  569.7 0.7 copy.180
  570.3 0.1 copy.168
  570.4 0.1 copy.170
  570.5 0.1 copy.169
  570.7 0.7 copy.177
  571.4 0.7 copy.178
  572.0 0.7 copy.179
  572.7 0.7 copy.181
  573.4 0.7 copy.182
  574.1 7.0 %multiply_subtract_fusion = (f32[1,768,768]{2,1,0:T(8,128)}, f32[1,768,768]{2,1,0:T(8,128)}, f32[1,768,768]{2,1,0:T(8,128)}) fusion(f32[1,768,768]{2,1,0:T(8,128)S(1)} %copy-done.3, f32[]{:T(128)} %bitcast.17, f32[]{:T(128)} %bitcast.15, f32[]{:T(128)S(6)} %min.3, bf16[768,768]{1,0:T(8,128)(2,1)} %get-tuple-element.229.c_ref, f32[1,768,768]{2,1,0:T(8,128)} %param.52, ...), kind=kLoop, calls=%fused_computation.29 | loop fusion | flops 10027008 | bytes 15335436 | tf_op jit(solution)/shard_map/sub | solution.py:1546
  581.2 4.4 multiply_subtract_fusion.1
  585.7 1.5 multiply_subtract_fusion.3
  587.2 1.4 copy-done.7
  588.6 0.5 copy-done.8
  589.1 6.2 %multiply_subtract_fusion.2 = (f32[1,192,2304]{2,1,0:T(8,128)}, f32[1,192,2304]{2,1,0:T(8,128)}, f32[1,192,2304]{2,1,0:T(8,128)}) fusion(f32[1,192,2304]{2,1,0:T(8,128)S(1)} %copy-done.8, f32[]{:T(128)} %bitcast.17, f32[]{:T(128)} %bitcast.15, f32[]{:T(128)S(6)} %min.3, f32[192,2560]{1,0:T(8,128)S(1)} %copy-done.7, f32[1,192,2304]{2,1,0:T(8,128)} %param.43, ...), kind=kLoop, calls=%fused_computation.37 | loop fusion | flops 7077888 | bytes 12386316 | tf_op jit(solution)/shard_map/sub | solution.py:1546
  595.3 10.3 %fusion.16 = (f32[6400,192]{0,1:T(8,128)}, f32[6400,192]{0,1:T(8,128)}, f32[6400,192]{0,1:T(8,128)}) fusion(f32[]{:T(128)S(6)} %min.3, f32[192,6400]{1,0:T(8,128)S(1)} %bitcast.98, bf16[192,6656]{1,0:T(8,128)(2,1)S(1)} %copy-done.1, f32[6400,192]{0,1:T(8,128)S(1)} %bitcast.102, f32[]{:T(128)} %bitcast.17, f32[]{:T(128)} %bitcast.15, f32[6400,192]{0,1:T(8,128)} %param.39, ...), kind=kLoop, calls=%fused_computation.67 | loop fusion | flops 22118400 | bytes 36864012 | tf_op jit(solution)/shard_map/transpose | solution.py:1666
  (80 shorter events, 0.3 us)
Async XLA Ops:
  3.3 1.7 copy-start.20
  5.0 1.8 copy-start.19
  5.0 1.8 copy-start.18
  5.0 3.1 copy-start.2
  8.1 2.1 copy-start.4
  10.2 1.2 copy-start.13
  161.2 23.5 %copy-start = (bf16[1024,768]{1,0:T(8,128)(2,1)}, bf16[1024,768]{1,0:T(8,128)(2,1)S(1)}, u32[]{:S(2)}) copy-start(bf16[1024,768]{1,0:T(8,128)(2,1)S(1)} %get-tuple-element.188.x_ref) | copy-start | bytes 4718596
  184.7 8.8 %copy-start.21 = (s32[6400]{0:T(1024)S(1)}, s32[6400]{0:T(1024)}, u32[]{:S(2)}) copy-start(s32[6400]{0:T(1024)} %param.36) | copy-start | bytes 76804
  377.3 170.3 %copy-start.26 = (s32[8]{0:T(128)S(1)}, s32[8]{0:T(128)}, u32[]{:S(2)}) copy-start(s32[8]{0:T(128)} %constant.130.clone..sunk.2) | copy-start | bytes 100
  547.9 18.2 %copy-start.10 = (bf16[192,2560]{1,0:T(8,128)(2,1)S(1)}, bf16[192,2560]{1,0:T(8,128)(2,1)}, u32[]{:S(2)}) copy-start(bf16[192,2560]{1,0:T(8,128)(2,1)} %get-tuple-element.226.a_ref) | copy-start | bytes 2949124
  564.1 4.4 copy-start.22
  564.1 4.6 copy-start.23
  564.1 4.7 copy-start.24
  564.1 4.8 copy-start.25
  566.3 1.3 copy-start.6
  567.6 6.5 %copy-start.3 = (f32[1,768,768]{2,1,0:T(8,128)S(1)}, f32[1,768,768]{2,1,0:T(8,128)}, u32[]{:S(2)}) copy-start(f32[1,768,768]{2,1,0:T(8,128)} %param.50) | copy-start | bytes 7077892
  574.1 7.1 %copy-start.5 = (f32[1,192,3072]{2,1,0:T(8,128)S(1)}, f32[1,192,3072]{2,1,0:T(8,128)}, u32[]{:S(2)}) copy-start(f32[1,192,3072]{2,1,0:T(8,128)} %param.47) | copy-start | bytes 7077892
  574.1 7.1 %copy-start.9 = (bf16[192,3072]{1,0:T(8,128)(2,1)S(1)}, bf16[192,3072]{1,0:T(8,128)(2,1)}, u32[]{:S(2)}) copy-start(bf16[192,3072]{1,0:T(8,128)(2,1)} %get-tuple-element.228.u_ref) | copy-start | bytes 3538948
  574.1 7.1 %copy-start.11 = (f32[1,192,3072]{2,1,0:T(8,128)S(1)}, f32[1,192,3072]{2,1,0:T(8,128)}, u32[]{:S(2)}) copy-start(f32[1,192,3072]{2,1,0:T(8,128)} %param.49) | copy-start | bytes 7077892
  574.1 7.1 %copy-start.12 = (f32[1,192,3072]{2,1,0:T(8,128)S(1)}, f32[1,192,3072]{2,1,0:T(8,128)}, u32[]{:S(2)}) copy-start(f32[1,192,3072]{2,1,0:T(8,128)} %param.48) | copy-start | bytes 7077892
  574.1 21.2 %slice-start.4 = ((s8[4915200]{0:T(1024)(128)(4,1)}), s8[720896]{0:T(1024)(128)(4,1)S(1)}, s32[]{:S(2)}) async-start(s8[4915200]{0:T(1024)(128)(4,1)} %bitcast.101), calls=%async_computation.4 | async-start | bytes 1441792
  581.1 4.5 copy-start.14
  581.2 4.5 copy-start.15
  581.2 4.5 copy-start.16
  581.2 4.5 copy-start.17
  581.2 14.1 %slice-start.2 = ((s8[4915200]{0:T(1024)(128)(4,1)}), s8[4194304]{0:T(1024)(128)(4,1)S(1)}, s32[]{:S(2)}) async-start(s8[4915200]{0:T(1024)(128)(4,1)} %bitcast.99), calls=%async_computation.2 | async-start | bytes 8388608
  581.2 14.1 %slice-start.5 = ((s8[4915200]{0:T(1024)(128)(4,1)}), s8[4194304]{0:T(1024)(128)(4,1)S(1)}, s32[]{:S(2)}) async-start(s8[4915200]{0:T(1024)(128)(4,1)} %bitcast.101), calls=%async_computation.5 | async-start | bytes 8388608
  585.6 2.9 copy-start.7
  585.6 3.5 copy-start.8
  585.7 9.6 %slice-start.3 = ((s8[4915200]{0:T(1024)(128)(4,1)}), s8[720896]{0:T(1024)(128)(4,1)S(1)}, s32[]{:S(2)}) async-start(s8[4915200]{0:T(1024)(128)(4,1)} %bitcast.99), calls=%async_computation.3 | async-start | bytes 1441792
  587.2 8.1 %slice-start = ((s8[4915200]{0:T(1024)(128)(4,1)}), s8[4194304]{0:T(1024)(128)(4,1)S(1)}, s32[]{:S(2)}) async-start(s8[4915200]{0:T(1024)(128)(4,1)} %bitcast.97), calls=%async_computation | async-start | bytes 8388608
  589.1 6.2 %slice-start.1 = ((s8[4915200]{0:T(1024)(128)(4,1)}), s8[720896]{0:T(1024)(128)(4,1)S(1)}, s32[]{:S(2)}) async-start(s8[4915200]{0:T(1024)(128)(4,1)} %bitcast.97), calls=%async_computation.1 | async-start | bytes 1441792
  589.1 6.2 %copy-start.1 = (bf16[192,6656]{1,0:T(8,128)(2,1)S(1)}, bf16[192,6656]{1,0:T(8,128)(2,1)}, u32[]{:S(2)}) copy-start(bf16[192,6656]{1,0:T(8,128)(2,1)} %get-tuple-element.225.dw_ref) | copy-start | bytes 7667716

commit v5 on v4

--- a/solution.py
+++ b/solution.py
@@ -114,10 +114,10 @@
     nb, nv, cap, part, rows, first, split, *refs
 ):
     round_ref, tok_ref, words = refs[:3]
-    shards, refs = (refs[3:7], refs[7:]) if first else ((), refs[3:])
+    shards, refs = (refs[3:5], refs[5:]) if first else ((), refs[3:])
     target_ref, refs = (refs[0], refs[1:]) if split else (None, refs)
     x_ref, ids_ref, place_ref, most_ref, tok_ref_all = refs[:5]
-    wholes, refs = (refs[5:9], refs[9:]) if first else ((), refs[5:])
+    wholes, refs = (refs[5:7], refs[7:]) if first else ((), refs[5:])
     (quarter_ref, target_all), refs = (refs[:2], refs[2:]) if split else ((None, None), refs)
     before, ranks, work, sent, got, spread, mixed, turned = refs[:8]
     tok_out, tok_in, row_out, row_in, mix_out, mix_in = refs[8:14]
@@ -176,7 +176,7 @@
         for owner in range(nv):
             theirs = (ids >= owner * rows) & (ids < (owner + 1) * rows)
             most = jnp.maximum(most, jnp.sum(theirs.astype(FL), axis=1, keepdims=True))
-    most_ref[...] = jnp.broadcast_to(jnp.max(most, axis=0, keepdims=True), most_ref.shape)
+    most_ref[0] = jnp.max(most).astype(I32)
 
     def row_copy(step):
         return send(
@@ -215,12 +215,13 @@
         def _():
             got[v] = block
 
-    each(1, nv + 1, build)
+    each(1, nv // 2 + 1, build)
     if first:
         gather.pass_on()
     if split:
         for step in range(1, nb):
             quarter_copy(step).start()
+    each(nv // 2 + 1, nv + 1, build)
 
     keys = []
     for p in range(nb):
@@ -273,6 +274,10 @@
             quarter_copy(step).wait()
 
 
+def weight_semaphores(count):
+    return [pltpu.SemaphoreType.DMA((count,))] + [pltpu.SemaphoreType.DMA((count, 4))] * 4
+
+
 class WeightGather:
     def __init__(self, nb, shards, wholes, own_sem, out_sem, in_sem, pair_out, pair_in):
         self.nb, self.shards, self.wholes = nb, shards, wholes
@@ -326,27 +331,27 @@
         return send(ref, ref, self.pair_out.at[w, k], self.pair_in.at[w, k], self.sibling)
 
     def start(self):
-        for w in range(4):
+        for w in range(len(self.shards)):
             for k in range(2 if self.nb == 4 else self.nb - 1):
                 self.copy(w, k).start()
-        for w in range(4):
+        for w in range(len(self.shards)):
             self.own_copy(w).start()
 
     def pass_on(self):
         if self.nb != 4:
             return
-        for w in range(4):
+        for w in range(len(self.shards)):
             for k in range(2):
                 self.copy(w, k).wait_recv()
                 self.copy(w, k + 2).start()
                 self.pair(w, k).start()
 
     def finish(self):
-        for w in range(4):
+        for w in range(len(self.shards)):
             for k in range(2 if self.nb == 4 else 0, len(self.routes(w))):
                 self.copy(w, k).wait_recv()
                 self.pair(w, k).start()
-        for w in range(4):
+        for w in range(len(self.shards)):
             self.own_copy(w).wait()
             for k in range(len(self.routes(w))):
                 self.copy(w, k).wait_send()
@@ -362,7 +367,7 @@
         SD((SEQ_LEN, D), BF),
         SD((nv, count, 1), I32),
         SD((nb, 8, SEQ_LEN), I32),
-        SD((8, 128), FL),
+        SD((1,), I32),
         SD((nb, nv, SEQ_LEN), I32),
     ]
     first = len(shards) > 0
@@ -382,7 +387,7 @@
         dma((nb,)), dma((nb,)), dma((nv,)), dma((nv,)), dma((nb,)), dma((nb,)),
     ]
     if first:
-        scratch += [dma((4,)), dma((4, 4)), dma((4, 4)), dma((4, 4)), dma((4, 4))]
+        scratch += weight_semaphores(len(shards))
     if split:
         scratch += [dma((nb,)), dma((nb,)), dma((1,)), dma((nb,)), dma((nb,))]
     extra = [targets] if split else []
@@ -391,23 +396,34 @@
         [turn, tok, table, *shards, *extra],
         "embed" if first else "embed_more", 0 if first else 3,
         in_specs=[SM, VM, VM] + [HB] * len(shards) + [VM] * len(extra),
-        out_specs=[VM] * 5 + [HB] * len(shards) + ([HB, VM] if split else []),
+        out_specs=[VM] * 3 + [SM, VM] + [HB] * len(shards) + ([HB, VM] if split else []),
     )
 
 
 class GradientSum:
-    def __init__(self, nb, nv, grads, sums, refs):
+    def __init__(self, nb, nv, grads, refs, totals=None, sums=None):
         self.nb, self.nv, self.grads, self.sums = nb, nv, grads, sums
-        self.own, self.near, self.shard, self.total = refs[0:4], refs[4:8], refs[8:12], refs[12:16]
-        self.bits, self.result = refs[16:20], refs[20:24]
-        (self.load_sem, self.pair_out, self.pair_in, self.mix_out, self.mix_in, self.cut_out, self.cut_in,
-         self.all_out, self.all_in, self.last_out, self.last_in, self.store_sem) = refs[24:36]
+        self.todo = [w for w, item in enumerate(grads) if item is not None]
+        take = iter(refs)
+        spread = lambda keys: {w: next(take) for w in keys}
+        everything = range(len(grads))
+        self.own, self.near, self.shard = spread(self.todo), spread(self.todo), spread(self.todo)
+        if sums is not None:
+            self.total = spread(self.todo)
+            self.total.update(totals)
+            self.bits, self.result = spread(everything), spread(everything)
+        else:
+            self.total = totals
+        self.load_sem, self.pair_out, self.pair_in, self.mix_out, self.mix_in = (next(take) for _ in range(5))
+        if sums is not None:
+            (self.cut_out, self.cut_in, self.all_out, self.all_in, self.last_out, self.last_in,
+             self.store_sem) = take
         self.b, v = lax.axis_index("batch"), lax.axis_index("vocab")
         self.core, self.chip, self.chips = lax.rem(v, 2), v // 2, nv // 2
         self.sibling = {"vocab": v + 1 - 2 * self.core}
 
     def half(self, w, core):
-        cols = self.grads[w].shape[1] // 2
+        cols = self.total[w].shape[1]
         return lanes(core * cols, cols)
 
     def load(self, w):
@@ -418,7 +434,7 @@
         return send(source, self.near[w], self.pair_out.at[w], self.pair_in.at[w], self.sibling)
 
     def start(self):
-        for w in (2, 3, 0, 1):
+        for w in sorted(self.todo, reverse=True):
             self.pair(w).start()
             self.load(w).start()
 
@@ -467,7 +483,7 @@
         place = self.result[w].at[pl.ds(pl.multiple_of(source * size, 16), size), :]
         return send(place, place, self.all_out.at[w, step], self.all_in.at[w, step], self.peer(step)[1])
 
-    def reduce(self, w):
+    def gather(self, w):
         rows = self.total[w].shape[0]
         for step in range(1, self.nb):
             self.mix(w, step).wait()
@@ -476,9 +492,13 @@
         for step in range(1, self.nb):
             value = value + self.shard[w][step].astype(FL)
         self.total[w][...] = value.astype(BF)
+
+    def reduce(self, w):
+        if w in self.todo:
+            self.gather(w)
         count = self.pieces(w)[0]
 
-        def go(step, w=w, count=count):
+        def go(step):
             @pl.when(self.peer(step)[0] < count)
             def _():
                 self.cut(w, step).start()
@@ -539,33 +559,36 @@
             send(other, other, self.last_out.at[w], self.last_in.at[w], self.sibling).wait_recv()
 
 
-def gradient_scratch(nb, nv, grads):
+def gradient_scratch(nb, nv, shapes, todo, whole=True):
     chips = nv // 2
-    halves = [(item.shape[0], item.shape[1] // 2) for item in grads]
+    halves = [(rows, cols // 2) for rows, cols in shapes]
     shards = [(rows // nb, cols) for rows, cols in halves]
     sizes = [rows // max(n for n in range(1, chips + 1) if rows % (16 * n) == 0) for rows, _ in shards]
     dma = pltpu.SemaphoreType.DMA
-    return (
-        [pltpu.VMEM(item, BF) for item in halves] * 2
-        + [pltpu.VMEM((nb, *item), BF) for item in shards]
-        + [pltpu.VMEM(item, BF) for item in shards]
-        + [pltpu.VMEM((chips, size, item[1]), BF) for size, item in zip(sizes, shards)]
-        + [pltpu.VMEM(item, BF) for item in shards]
-        + [dma((4,)), dma((4,)), dma((4,)), dma((4, nb)), dma((4, nb)), dma((4, chips)), dma((4, chips))]
-        + [dma((4, chips)), dma((4, chips)), dma((4,)), dma((4,)), dma((4,))]
-    )
+    count = len(shapes)
+    refs = [pltpu.VMEM(halves[w], BF) for w in todo] * 2 + [pltpu.VMEM((nb, *shards[w]), BF) for w in todo]
+    if whole:
+        refs += [pltpu.VMEM(shards[w], BF) for w in todo]
+        refs += [pltpu.VMEM((chips, size, item[1]), BF) for size, item in zip(sizes, shards)]
+        refs += [pltpu.VMEM(item, BF) for item in shards]
+    refs += [dma((count,)), dma((count,)), dma((count,)), dma((count, nb)), dma((count, nb))]
+    if whole:
+        refs += [dma((count, chips))] * 4 + [dma((count,))] * 3
+    return refs
 
 
 def unembed_kernel(nb, nv, cap, part, first, split, *refs):
     x_ref, ids_ref, place_ref = refs[:3]
     grads, refs = (refs[3:7], refs[7:]) if first else ((), refs[3:])
+    if first:
+        totals, grads = {2: grads[2]}, (grads[0], grads[1], None, grads[3])
     quarter_ref, refs = (refs[0], refs[1:]) if split else (None, refs)
     out_ref = refs[0]
     sums, refs = (refs[1:5], refs[5:]) if first else ((), refs[1:])
     dw_ref, refs = (refs[0], refs[1:]) if split else (None, refs)
     (quarter_out, quarter_in, quarter_own), refs = (refs[:3], refs[3:]) if split else ([None] * 3, refs)
     turned, parts, sent, got, mix_out, mix_in, row_out, row_in = refs[:8]
-    layer = GradientSum(nb, nv, grads, sums, refs[8:]) if first else None
+    layer = GradientSum(nb, nv, grads, refs[8:], totals, sums) if first else None
     b, v = lax.axis_index("batch"), lax.axis_index("vocab")
     width, rows = out_ref.shape
     meet((("batch", nb), ("vocab", nv)))
@@ -579,6 +602,7 @@
         mix_copy(step).start()
     if first:
         layer.start()
+        layer.reduce(2)
     parts[b] = turned[b]
     for step in range(1, nb):
         mix_copy(step).wait()
@@ -621,10 +645,13 @@
             got[v] = block
 
     if first:
-        layer.scatter(2)
-    each(1, nv + 1, build)
+        layer.scatter(3)
+    each(1, nv // 2 + 1, build)
     if first:
-        layer.scatter(3)
+        layer.collect(2)
+    each(nv // 2 + 1, nv + 1, build)
+    if first:
+        layer.scatter(0)
     if split:
         quarter_keep().start()
     out_ref[...] = jnp.zeros_like(out_ref)
@@ -647,22 +674,19 @@
     if first:
         quarter = nv // 4
         each(0, quarter, take)
-        layer.reduce(2)
-        layer.scatter(0)
-        each(quarter, 2 * quarter, take)
         layer.reduce(3)
         layer.scatter(1)
         if split:
             for step in range(1, nb):
                 quarter_copy(step).start()
+        each(quarter, 2 * quarter, take)
+        layer.reduce(0)
         each(2 * quarter, 3 * quarter, take)
-        layer.collect(2)
+        layer.collect(3)
+        layer.reduce(1)
         each(3 * quarter, nv, take)
-        layer.collect(3)
-        for w in (0, 1):
-            layer.reduce(w)
-        for w in (0, 1):
-            layer.collect(w)
+        layer.collect(0)
+        layer.collect(1)
         layer.finish()
         if split:
             quarter_keep().wait()
@@ -687,8 +711,9 @@
     if split:
         scratch = [dma((nb,)), dma((nb,)), dma((1,))] + scratch
     if first:
-        scratch += gradient_scratch(nb, nv, grads)
-    outs = [SD((width, rows), FL)] + [SD((item.shape[0] // nb, item.shape[1]), BF) for item in grads]
+        shapes = [item.shape if w != 2 else (nb * item.shape[0], 2 * item.shape[1]) for w, item in enumerate(grads)]
+        scratch += gradient_scratch(nb, nv, shapes, (0, 1, 3))
+    outs = [SD((width, rows), FL)] + [SD((item[0] // nb, item[1]), BF) for item in (shapes if first else ())]
     extra = [quarter] if split else []
     if split:
         outs.append(SD((width, nb * quarter.shape[1]), BF))
@@ -699,7 +724,7 @@
         [grad, ids, place, *grads, *extra],
         "unembed" if first else "unembed_more",
         2 if first else 4,
-        in_specs=[VM] * 3 + [HB] * (len(grads) + len(extra)),
+        in_specs=[VM] * 3 + ([HB, HB, VM, HB] if first else []) + [HB] * len(extra),
         out_specs=[VM] + [HB] * (len(grads) + len(extra)),
     )
 
@@ -769,9 +794,12 @@
 
 
 def attend_kernel(
-    x_ref, a_ref, seg_ref, pos_ref,
-    hall_ref, kv_ref, q_ref, hq_ref, xq_ref, o_ref, lse_ref, norm_ref, mixt_ref,
+    nb, nv, x_ref, a_ref, seg_ref, pos_ref, p_ref, c_ref,
+    hall_ref, kv_ref, q_ref, hq_ref, xq_ref, o_ref, lse_ref, norm_ref, mixt_ref, p_all, c_all, *sems,
 ):
+    meet((("batch", nb), ("vocab", nv)))
+    gather = WeightGather(nb, (p_ref, c_ref), (p_all, c_all), *sems)
+    gather.start()
     norm_ref[...] = a_ref[:, 3 * D : 3 * D + 128].astype(FL).T[:8, :]
     gain, bias = norm_ref[0:1, :], norm_ref[3:4, :]
 
@@ -811,7 +839,9 @@
             lse_ref[p, head : head + 1, :] = peak + jnp.log(total)
         o_ref[:, lanes(p * PAIR, PAIR)] = jnp.concatenate(outs, axis=0).T.astype(BF)
 
+    gather.pass_on()
     each(0, NPAIR, attend)
+    gather.finish()
 
 
 def feed_kernel(xq_ref, o_ref, p_ref, u_ref, c_ref, norm_ref, x1_ref, h2_ref, z_ref, act_ref, x2_ref, f_ref):
@@ -870,9 +900,12 @@
 
 
 def attend_back_kernel(
-    pos_ref, do_ref, q_ref, kv_ref, lse_ref, hall_ref, hq_ref, a_ref, x_ref, dx1_ref, mixt_ref, seg_ref, row_ref,
-    norm_ref, dnorm_ref, da_ref, dx_ref, dkv, dq, hallt, dh, dxin, dmem,
+    nb, nv, do_ref, q_ref, kv_ref, lse_ref, hall_ref, hq_ref, a_ref, x_ref, dx1_ref, mixt_ref, seg_ref, row_ref,
+    norm_ref, dnorm_ref, du_ref, da_ref, dx_ref, du_sum, dkv, dq, hallt, dh, dxin, dmem, sel, *refs,
 ):
+    meet((("batch", nb), ("vocab", nv)))
+    layer = GradientSum(nb, nv, (du_ref,), refs, {0: du_sum})
+    layer.start()
     visible = visible_keys(seg_ref, row_ref)
 
     def attend(p):
@@ -899,7 +932,9 @@
         dkv[:, cut] = dk.astype(BF)
         dkv[:, lanes(D + p * PAIR, PAIR)] = dv.astype(BF)
 
-    each(0, NPAIR, attend)
+    each(0, NPAIR // 2, attend)
+    layer.scatter(0)
+    each(NPAIR // 2, NPAIR, attend)
     da_ref[:, :D] = nn(hq_ref[...].T, dq[...]).astype(BF)
 
     def turn(i):
@@ -924,13 +959,21 @@
         dh[cut, :] = nt(dkv[pl.ds(SLOTS * NB + i * BLK, BLK), :], a_ref[:, D : 3 * D]) + nn(mixt_ref[cut, :], dmem[...])
 
     each(0, SEQ_LEN // BLK, local)
-    dxin[:PICKS, :] = nt(dq[...], a_ref[:, :D])
-
-    def scatter_query(k):
-        row = pl.ds(pos_ref[k], 1)
-        dh[row, :] += dxin[pl.ds(k, 1), :]
-
-    each(0, PICKS, scatter_query)
+    put = (row_ref[...] == iota((SEQ_LEN, PICKS), 0)).astype(FL).astype(BF)
+
+    def scatter(target, value):
+        for _ in range(3):
+            part = value.astype(BF)
+            value = value - part.astype(FL)
+
+            def add(i, part=part):
+                cut = pl.ds(i * BLK, BLK)
+                target[cut, :] += nn(sel[cut, :], part)
+
+            each(0, SEQ_LEN // BLK, add)
+
+    sel[...] = put
+    scatter(dh, nt(dq[...], a_ref[:, :D]))
     gain = norm_ref[0:1, :]
     da_rows = [jnp.zeros((1, D), FL), jnp.zeros((1, D), FL)]
 
@@ -943,16 +986,13 @@
 
     dgain, dbias = lax.fori_loop(0, SEQ_LEN // BLK, finish, tuple(da_rows))
 
-    def scatter_rest(k):
-        row = pl.ds(pos_ref[k], 1)
-        dxin[row, :] += dx1_ref[pl.ds(k, 1), :]
-
-    each(0, PICKS, scatter_rest)
+    scatter(dxin, dx1_ref[...])
     dx_ref[...] = dxin[...].astype(BF)
     line = iota((8, D), 0)
     norms = dnorm_ref[...] + jnp.where(line == 0, dgain, jnp.where(line == 3, dbias, 0.0))
     tall = jnp.concatenate([norms, jnp.zeros((EXTRA - 8, D), FL)], axis=0)
     da_ref[:, 3 * D :] = tall.T.astype(BF)
+    layer.gather(0)
 
 
 def head_kernel(
@@ -1202,6 +1242,10 @@
     span = nv * PICKS
     meet((("batch", nb), ("vocab", nv)))
 
+    def column(line):
+        line = jnp.where(line < (v + 1) * block_rows, line - base, -1).astype(FL)
+        return jnp.broadcast_to(line, (128, 2 * PICKS)).T[:, 0:1].astype(I32)
+
     def peer(step):
         return {"vocab": lax.rem(chip + step, chips) * 2 + core}
 
@@ -1245,18 +1289,17 @@
         start = pl.multiple_of(first * PICKS, 2 * PICKS)
         features = fall[pl.ds(first, 2)].reshape(2 * PICKS, D)
         ft[:, pl.ds(start, 2 * PICKS)] = features.T
-        line = target_ref[p, :, pl.ds(pl.multiple_of(c * 2 * PICKS, 2 * PICKS), 2 * PICKS)].astype(FL)
-        target = jnp.broadcast_to(line, (128, 2 * PICKS)).T[:, 0:1].astype(I32) - base
+        line = target_ref[p, :, pl.ds(pl.multiple_of(c * 2 * PICKS, 2 * PICKS), 2 * PICKS)]
+        target = column(line)
         value = nn(features, w_ref[...])
-        peak = jnp.max(jnp.where(live, value, NEG_BIG), axis=1, keepdims=True)
-        hot = target == iota((2 * PICKS, rows), 1)
-        e = jnp.where(live, jnp.exp(value - peak), 0.0)
+        value = jnp.where(live, value, NEG_BIG)
+        peak = jnp.maximum(jnp.max(value, axis=1, keepdims=True), 0.1 * NEG_BIG)
+        e = jnp.exp(value - peak)
         expo[pl.ds(start, 2 * PICKS), :] = e.astype(BF)
         total = jnp.sum(e, axis=1, keepdims=True)
-        picked = jnp.sum(jnp.where(hot, value, 0.0), axis=1, keepdims=True)
-        valid = jnp.sum(jnp.where(hot & live, 1.0, 0.0), axis=1, keepdims=True)
+        picked = jnp.sum(jnp.where(target == iota((2 * PICKS, rows), 1), value, 0.0), axis=1, keepdims=True)
         lane = iota((2 * PICKS, 128), 1)
-        wide = jnp.where(lane == 0, peak, jnp.where(lane == 1, total, jnp.where(lane == 2, picked, valid))).T
+        wide = jnp.where(lane == 0, peak, jnp.where(lane == 1, total, picked)).T
         mine[c * 2, p] = wide[:8, :PICKS]
         mine[c * 2 + 1, p] = wide[:8, PICKS:]
 
@@ -1284,10 +1327,10 @@
 
         def add(u, carry):
             one = read(u)
-            return carry[0] + one[1:2, :] * jnp.exp(one[0:1, :] - peak), carry[1] + one[2:3, :], carry[2] + one[3:4, :]
+            return carry[0] + one[1:2, :] * jnp.exp(one[0:1, :] - peak), carry[1] + one[2:3, :]
 
         zero = jnp.zeros((1, PICKS), FL)
-        return (peak, *lax.fori_loop(0, count, add, (zero, zero, zero)))
+        return (peak, *lax.fori_loop(0, count, add, (zero, zero)))
 
     def tile_of(rows_of):
         line = iota((8, PICKS), 0)
@@ -1312,7 +1355,8 @@
     each(1, nb, lambda t: second_copy(t).start())
     second_got[b] = merged[b]
     each(1, nb, lambda t: second_copy(t).wait())
-    peak, total, picked, valid = merge(lambda u: second_got[u], nb)
+    peak, total, picked = merge(lambda u: second_got[u], nb)
+    valid = (picked > 0.5 * NEG_BIG).astype(FL)
     tile[...] = tile_of((peak + jnp.log(jnp.maximum(total, 1e-37)), picked, valid))
 
     def third_copy(t):
@@ -1368,7 +1412,7 @@
     def exchange(s):
         def add(k):
             pair_copy(s, k).wait()
-            handed[s, k] = (group[shard(k, core), :] + half[s, k].astype(FL)).astype(BF)
+            handed[s, k] = (group[s % 2, shard(k, core), :] + half[s, k].astype(FL)).astype(BF)
 
         each(0, chips, add)
         if s > 0:
@@ -1380,26 +1424,27 @@
         def strip(c, p=p):
             start = pl.multiple_of(p * span + c * 2 * PICKS, 2 * PICKS)
             here = pl.ds(start, 2 * PICKS)
-            line = target_ref[p, :, pl.ds(pl.multiple_of(c * 2 * PICKS, 2 * PICKS), 2 * PICKS)].astype(FL)
-            target = jnp.broadcast_to(line, (128, 2 * PICKS)).T[:, 0:1].astype(I32) - base
+            line = target_ref[p, :, pl.ds(pl.multiple_of(c * 2 * PICKS, 2 * PICKS), 2 * PICKS)]
+            target = column(line)
             two = coef[here, :]
             hot = target == iota((2 * PICKS, rows), 1)
             value = two[:, 0:1] * expo[here, :].astype(FL) - jnp.where(hot, two[:, 1:2], 0.0)
             expo[here, :] = value.astype(BF)
 
         each(0, chips, strip)
-        def features_grad(i, p=p):
+        def features_grad(i, p=p, s=s):
             here = pl.ds(pl.multiple_of(i * 512, 512), 512)
-            group[here, :] = nt(expo[pl.ds(pl.multiple_of(p * span + i * 512, 512), 512), :], w_ref[...])
+            group[s % 2, here, :] = nt(expo[pl.ds(pl.multiple_of(p * span + i * 512, 512), 512), :], w_ref[...])
 
         each(0, span // 512, features_grad)
 
         def swap(k, s=s):
-            handed[s, k] = group[shard(k, 1 - core), :].astype(BF)
+            handed[s, k] = group[s % 2, shard(k, 1 - core), :].astype(BF)
             pair_copy(s, k).start()
 
+        if s != 1:
+            exchange(s - 1 if s > 0 else nb - 1)
         each(0, chips, swap)
-        exchange(s)
 
     words_sum[...] = jnp.zeros_like(words_sum)
 
@@ -1407,7 +1452,9 @@
         cut = lanes(i * 512, 512)
         words_sum[...] += nn(ft[:, cut], expo[cut, :])
 
-    each(0, nb * span // 512, words_grad)
+    each(0, 1, words_grad)
+    exchange(0)
+    each(1, nb * span // 512, words_grad)
     dw_ref[...] = words_sum[...].astype(BF)
 
     for s in range(1, nb):
@@ -1460,7 +1507,7 @@
         pltpu.VMEM((nb, 8, PICKS), FL),
         pltpu.VMEM((nv, nb, 8, PICKS), FL),
         pltpu.VMEM((tokens, 128), FL),
-        pltpu.VMEM((nv * PICKS, D), FL),
+        pltpu.VMEM((2, nv * PICKS, D), FL),
         pltpu.VMEM((nb, chips, PICKS, D), BF),
         pltpu.VMEM((nb, chips, PICKS, D), BF),
         pltpu.VMEM((nb, chips, PICKS, D), BF),
@@ -1579,10 +1626,11 @@
 
     seg_row, pos_row = segments[None, :], counted[None, :]
     tok = tokens.reshape(nv, SEQ_LEN)
-    x, ids, place, most, every, a_all, p_all, u_all, c_all, *rest = embed(
-        nb, nv, cap, rows, jnp.zeros((1,), I32), tok, rounded, pieces, targets[None, :] if split else None
+    x, ids, place, most, every, a_all, u_all, *rest = embed(
+        nb, nv, cap, rows, jnp.zeros((1,), I32), tok, rounded, (pieces[0], pieces[2]),
+        targets[None, :] if split else None,
     )
-    turns = (most[0, 0].astype(I32) + cap - 1) // cap
+    turns = (most[0] + cap - 1) // cap
 
     def more_rows(state):
         turn, total = state
@@ -1590,15 +1638,17 @@
 
     x = lax.while_loop(lambda state: state[0] < turns, more_rows, (jnp.int32(1), x))[1]
 
-    hall, kv, q, hq, xq, mixed, lse, norm_rows, mixing_t = run(
-        attend_kernel,
+    hall, kv, q, hq, xq, mixed, lse, norm_rows, mixing_t, p_all, c_all = run(
+        functools.partial(attend_kernel, nb, nv),
         [
             SD((KEYS, D), BF), SD((KEYS, 2 * D), BF), SD((PICKS, D), BF), SD((PICKS, D), BF), SD((PICKS, D), FL),
             SD((PICKS, D), BF), SD((NPAIR, 2, PICKS), FL), SD((8, D), FL), SD((SEQ_LEN, SLOTS * NB), BF),
+            SD((D, D), BF), SD((FF, D), BF),
         ],
-        [],
-        [x, a_all, seg_row, pos_row],
-        "attend", flops=7 * 10**9, moved=20 * 10**6,
+        weight_semaphores(2),
+        [x, a_all, seg_row, pos_row, pieces[1], pieces[3]],
+        "attend", 6, flops=7 * 10**9, moved=20 * 10**6,
+        in_specs=[VM] * 4 + [HB] * 2, out_specs=[VM] * 9 + [HB] * 2,
     )
     x1, h2, z, act, x2, features = run(
         feed_kernel,
@@ -1626,18 +1676,19 @@
         [df, x2, x1, h2, z, act, mixed, p_all, u_all, c_all, norm_rows],
         "feed_back", flops=4 * 10**9, moved=30 * 10**6,
     )
-    da, dx = run(
-        attend_back_kernel,
-        [SD((D, 3 * D + EXTRA), BF), SD((SEQ_LEN, D), BF)],
+    da, dx, du_sum = run(
+        functools.partial(attend_back_kernel, nb, nv),
+        [SD((D, 3 * D + EXTRA), BF), SD((SEQ_LEN, D), BF), SD((width, FF // 2), BF)],
         [
             pltpu.VMEM((KEYS, 2 * D), BF), pltpu.VMEM((PICKS, D), BF), pltpu.VMEM((D, KEYS), BF),
             pltpu.VMEM((SEQ_LEN, D), FL), pltpu.VMEM((SEQ_LEN, D), FL), pltpu.VMEM((SLOTS * NB, D), BF),
+            pltpu.VMEM((SEQ_LEN, PICKS), BF), *gradient_scratch(nb, nv, [du.shape], (0,), False),
         ],
-        [counted, dmixed, q, kv, lse, hall, hq, a_all, x, dx1, mixing_t, seg_row, pos_row, norm_rows, dnorm],
-        "attend_back", flops=12 * 10**9, moved=25 * 10**6,
-        in_specs=[SM] + [VM] * 14,
+        [dmixed, q, kv, lse, hall, hq, a_all, x, dx1, mixing_t, seg_row, pos_row, norm_rows, dnorm, du],
+        "attend_back", 7, flops=12 * 10**9, moved=25 * 10**6,
+        in_specs=[VM] * 14 + [HB],
     )
-    extra, *sums = unembed(nb, nv, cap, width, rows, dx, ids, place, (da, dp, du, dc), dw if split else None)
+    extra, *sums = unembed(nb, nv, cap, width, rows, dx, ids, place, (da, dp, du_sum, dc), dw if split else None)
     if split:
         dw_sum = sums.pop()
 

time: 613 us -> 597 us (0.974)
  loops' own time: 8.77 us -> 0.44 us
  Pallas kernels: 541 us -> 534 us
    another operation x1, loops' own time: 8.54 us -> 0.18 us  [shards(): lax.while_loop(lambda state: state[0] < turns, more_rows, (jnp.int32(1), x))]
    pallas_call x8, Pallas kernels: 541 us -> 534 us  [run(): pl.pallas_call(kernel, out_shape=outs, in_specs=in_specs if in_specs is n...]
where the time goes in v5:
time: 597 us; the launch traced here: 591 us
  Pallas kernels  534 us (89%)
  other arithmetic  38.1 us (6%)
  local copies, waits for them, and re-layouts  13.3 us (2%)
    pallas_call x8, Pallas kernels, run(): pl.pallas_call(kernel, out_shape=outs, in_specs=in_specs if in_specs is n...  534 us
    sub x6, other arithmetic, adamw(): weight - rate * (fixed_moment / (jnp.sqrt(fixed_square) + ADAM_EPS) + dec...  17 us

profile of v5, /device:TPU:0, one launch (start us, length us, event | category | flops | bytes accessed | tf_op | source)
XLA Modules:
  0.0 591.1 jit_solution(4812125731471627624)
XLA Ops:
  0.7 2.6 bitcast_convert_fusion
  3.3 1.6 pad.8.refs_2_
  5.0 0.7 copy-done.3
  5.7 0.1 convert_bitcast_fusion.3
  5.7 0.0 copy-done.17
  5.8 0.1 copy.164
  6.0 1.1 concatenate.9.refs_3_
  7.1 2.8 convert_bitcast_fusion.2.refs_4_
  10.0 102.5 %embed.1 = (bf16[1024,768]{1,0:T(8,128)(2,1)S(1)}, s32[8,768,1]{2,1,0:T(8,128)}, s32[4,8,1024]{2,1,0:T(8,128)S(1)}, s32[1]{0:T(128)}, s32[4,8,1024]{2,1,0:T(8,12...) custom-call(s32[1]{0:T(128)} %constant.47.clone.1.refs_0_, ...), custom_call_target="tpu_custom_call" | custom-call | tf_op jit(solution)/shard_map/embed/pallas_call | solution.py:68
  113.2 0.2 while.23
  113.4 3.4 convert_bitcast_fusion.1.c_ref
  116.8 0.7 convert_bitcast_fusion.4.p_ref
  117.5 55.5 %attend.1 = (bf16[1536,768]{1,0:T(8,128)(2,1)}, bf16[1536,1536]{1,0:T(8,128)(2,1)}, bf16[128,768]{1,0:T(8,128)(2,1)}, bf16[128,768]{1,0:T(8,128)(2,1)}, f32[128,...) custom-call(bf16[1024,768]{1,0:T(8,128)(2,1)S(1)} %get-tuple-element, ...), custom_call_target="tpu_custom_call" | custom-call | flops 7000000000 | bytes 20000000 | tf_op jit(solution)/shard_map/attend/pallas_call | solution.py:68
  173.0 8.8 %feed.1 = (f32[128,768]{1,0:T(8,128)}, bf16[128,768]{1,0:T(8,128)(2,1)}, f32[128,3072]{1,0:T(8,128)}, bf16[128,3072]{1,0:T(8,128)(2,1)}, f32[128,768]{1,0:T(8,128)}, /*index=5*/bf16[128,768]{1,0:T(8,128)(2,1)}) custom-call(f32[128,768]{1,0:T(8,128)} %get-tuple-element.191.xq_ref, bf16[128,768]{1,0:T(8,128)(2,1)} %get-tuple-element.192.o_ref, ...), custom_call_target="tpu_custom_call" | custom-call | flops 2000000000 | bytes 15000000 | tf_op jit(solution)/shard_map/feed/pallas_call | solution.py:68
  181.8 0.6 broadcast_in_dim.50.live_ref
  182.4 136.9 %wide_head.1 = (f32[128,768]{1,0:T(8,128)}, bf16[768,1664]{1,0:T(8,128)(2,1)}, f32[8,128]{1,0:T(8,128)}) custom-call(bf16[128,768]{1,0:T(8,128)(2,1)} %get-tuple-element.197.f_ref, bf16[768,1664]{1,0:T(8,128)(2,1)} %get-tuple-element.198.w_ref, s32[1,6656]{1,0:T(1,128)} %broadcast_in_dim.50.live_ref, s32[4,1,1024]{2,1,0:T(1,128)} %get-tuple-element.199.target_ref), custom_call_target="tpu_custom_call" | custom-call | tf_op jit(solution)/shard_map/wide_head/pallas_call | solution.py:68
  319.3 15.1 %feed_back.1 = (bf16[3072,768]{1,0:T(8,128)(2,1)}, bf16[768,3072]{1,0:T(8,128)(2,1)}, bf16[768,768]{1,0:T(8,128)(2,1)}, f32[128,768]{1,0:T(8,128)}, bf16[128,768]{1,0:T(8,128)(2,1)}, /*index=5*/f32[8,768]{1,0:T(8,128)}) custom-call(f32[128,768]{1,0:T(8,128)} %get-tuple-element.200.df_ref, f32[128,768]{1,0:T(8,128)} %get-tuple-element.201.x2_ref, ...), custom_call_target="tpu_custom_call" | custom-call | flops 4000000000 | bytes 30000000 | tf_op jit(solution)/shard_map/feed_back/pallas_call | solution.py:68
  334.5 50.9 %attend_back.1 = (bf16[768,2560]{1,0:T(8,128)(2,1)}, bf16[1024,768]{1,0:T(8,128)(2,1)S(1)}, bf16[192,1536]{1,0:T(8,128)(2,1)}) custom-call(bf16[128,768]{1,0:T(8,128)(2,1)} %get-tuple-element.206.do_ref, bf16[128,768]{1,0:T(8,128)(2,1)} %get-tuple-element.207.q_ref, bf16[1536,1536]{1,0:T(8,128)(2,1)} %get-tuple-element.208.kv_ref, ...), custom_call_target="tpu_custom_call" | custom-call | flops 12000000000 | bytes 25000000 | tf_op jit(solution)/shard_map/attend_back/pallas_call | solution.py:68
  385.4 148.3 %unembed.1 = (f32[192,6400]{1,0:T(8,128)}, bf16[192,2560]{1,0:T(8,128)(2,1)}, bf16[192,768]{1,0:T(8,128)(2,1)}, bf16[192,3072]{1,0:T(8,128)(2,1)}, bf16[768,768]{1,0:T(8,128)(2,1)}, /*index=5*/bf16[192,6656]{1,0:T(8,128)(2,1)}) custom-call(bf16[1024,768]{1,0:T(8,128)(2,1)S(1)} %get-tuple-element.522.refs_0_, s32[8,768,1]{2,1,0:T(8,128)} %get-tuple-element.217.refs_1_, ...), custom_call_target="tpu_custom_call" | custom-call | tf_op jit(solution)/shard_map/unembed/pallas_call | solution.py:68
  533.7 0.3 while.24
  534.0 16.4 %norm.1 = f32[8,128]{1,0:T(8,128)} custom-call(f32[192,6400]{1,0:T(8,128)} %get-tuple-element.226.extra_ref, bf16[192,6656]{1,0:T(8,128)(2,1)} %get-tuple-element.227.dw_ref, bf16[192,2560]{1,0:T(8,128)(2,1)} %get-tuple-element.228.a_ref, bf16[192,768]{1,0:T(8,128)(2,1)} %get-tuple-element.229.p_ref, bf16[192,3072]{1,0:T(8,128)(2,1)} %get-tuple-element.230.u_ref, ...), custom_call_target="tpu_custom_call" | custom-call | tf_op jit(solution)/shard_map/norm/pallas_call | solution.py:68
  550.5 1.2 fusion.23
  552.4 0.2 convert_element_type.59
  553.4 0.1 copy.166
  553.6 0.1 copy.167
  553.7 0.1 copy.172
  553.9 0.1 copy.173
  554.0 0.2 multiply_divide_fusion
  554.2 0.1 copy.174
  554.3 0.1 copy.176
  554.4 0.1 copy.175
  554.5 0.7 copy.180
  555.2 0.1 copy.168
  555.3 0.1 copy.170
  555.4 0.1 copy.169
  555.6 0.7 copy.177
  556.3 0.7 copy.178
  556.9 0.7 copy.179
  557.6 0.7 copy.181
  558.3 0.7 copy.182
  559.0 7.7 %multiply_subtract_fusion = (f32[1,768,768]{2,1,0:T(8,128)}, f32[1,768,768]{2,1,0:T(8,128)}, f32[1,768,768]{2,1,0:T(8,128)}) fusion(f32[1,768,768]{2,1,0:T(8,128)} %param.50, f32[]{:T(128)} %bitcast.17, f32[]{:T(128)} %bitcast.15, f32[]{:T(128)S(6)} %min.3, bf16[768,768]{1,0:T(8,128)(2,1)} %get-tuple-element.231.c_ref, f32[1,768,768]{2,1,0:T(8,128)} %param.52, ...), kind=kLoop, calls=%fused_computation.29 | loop fusion | flops 10027008 | bytes 15335436 | tf_op jit(solution)/shard_map/sub | solution.py:1593
  566.8 4.4 multiply_subtract_fusion.1
  571.2 1.5 multiply_subtract_fusion.3
  572.7 1.0 copy-done.4
  573.7 0.5 copy-done.11
  574.3 3.4 multiply_subtract_fusion.2
  577.6 1.0 copy-done.1
  578.6 10.9 %fusion.16 = (f32[6400,192]{0,1:T(8,128)}, f32[6400,192]{0,1:T(8,128)}, f32[6400,192]{0,1:T(8,128)}) fusion(f32[]{:T(128)S(6)} %min.3, f32[192,6400]{1,0:T(8,128)S(1)} %bitcast.98, bf16[192,6656]{1,0:T(8,128)(2,1)S(1)} %copy-done.1, f32[6400,192]{0,1:T(8,128)} %param.40, f32[]{:T(128)} %bitcast.17, f32[]{:T(128)} %bitcast.15, f32[6400,192]{0,1:T(8,128)} %param.39, ...), kind=kLoop, calls=%fused_computation.67 | loop fusion | flops 22118400 | bytes 36864012 | tf_op jit(solution)/shard_map/transpose | solution.py:1717
  (70 shorter events, 0.3 us)
Async XLA Ops:
  3.3 1.7 copy-start.18
  3.3 2.3 copy-start.3
  5.0 0.8 copy-start.17
  5.0 0.8 copy-start.16
  113.4 59.7 %copy-start = (bf16[1024,768]{1,0:T(8,128)(2,1)}, bf16[1024,768]{1,0:T(8,128)(2,1)S(1)}, u32[]{:S(2)}) copy-start(bf16[1024,768]{1,0:T(8,128)(2,1)S(1)} %get-tuple-element.189.x_ref) | copy-start | bytes 4718596
  113.4 3.4 copy-start.9
  173.0 8.8 %copy-start.19 = (s32[6400]{0:T(1024)S(1)}, s32[6400]{0:T(1024)}, u32[]{:S(2)}) copy-start(s32[6400]{0:T(1024)} %param.36) | copy-start | bytes 76804
  385.4 148.3 %copy-start.24 = (s32[8]{0:T(128)S(1)}, s32[8]{0:T(128)}, u32[]{:S(2)}) copy-start(s32[8]{0:T(128)} %constant.129.clone..sunk.2) | copy-start | bytes 100
  533.9 18.5 %copy-start.6 = (bf16[192,2560]{1,0:T(8,128)(2,1)S(1)}, bf16[192,2560]{1,0:T(8,128)(2,1)}, u32[]{:S(2)}) copy-start(bf16[192,2560]{1,0:T(8,128)(2,1)} %get-tuple-element.228.a_ref) | copy-start | bytes 2949124
  550.4 3.0 copy-start.20
  550.4 3.1 copy-start.21
  550.4 3.3 copy-start.22
  550.4 3.4 copy-start.23
  559.0 7.7 %copy-start.2 = (f32[1,192,3072]{2,1,0:T(8,128)S(1)}, f32[1,192,3072]{2,1,0:T(8,128)}, u32[]{:S(2)}) copy-start(f32[1,192,3072]{2,1,0:T(8,128)} %param.47) | copy-start | bytes 7077892
  559.0 7.7 %copy-start.5 = (bf16[192,3072]{1,0:T(8,128)(2,1)S(1)}, bf16[192,3072]{1,0:T(8,128)(2,1)}, u32[]{:S(2)}) copy-start(bf16[192,3072]{1,0:T(8,128)(2,1)} %get-tuple-element.230.u_ref) | copy-start | bytes 3538948
  559.0 7.7 %copy-start.7 = (f32[1,192,3072]{2,1,0:T(8,128)S(1)}, f32[1,192,3072]{2,1,0:T(8,128)}, u32[]{:S(2)}) copy-start(f32[1,192,3072]{2,1,0:T(8,128)} %param.49) | copy-start | bytes 7077892
  559.0 7.7 %copy-start.8 = (f32[1,192,3072]{2,1,0:T(8,128)S(1)}, f32[1,192,3072]{2,1,0:T(8,128)}, u32[]{:S(2)}) copy-start(f32[1,192,3072]{2,1,0:T(8,128)} %param.48) | copy-start | bytes 7077892
  566.7 4.5 copy-start.10
  566.7 4.5 copy-start.13
  566.7 4.5 copy-start.14
  566.7 4.5 copy-start.15
  566.8 6.0 %copy-start.12 = (f32[1,192,2304]{2,1,0:T(8,128)S(1)}, f32[1,192,2304]{2,1,0:T(8,128)}, u32[]{:S(2)}) copy-start(f32[1,192,2304]{2,1,0:T(8,128)} %param.42) | copy-start | bytes 5308420
  566.8 10.8 %slice-start.2 = ((s8[4915200]{0:T(1024)(128)(4,1)}), s8[4194304]{0:T(1024)(128)(4,1)S(1)}, s32[]{:S(2)}) async-start(s8[4915200]{0:T(1024)(128)(4,1)} %bitcast.99), calls=%async_computation.2 | async-start | bytes 8388608
  571.2 2.5 copy-start.4
  571.2 3.1 copy-start.11
  571.2 6.4 %slice-start.3 = ((s8[4915200]{0:T(1024)(128)(4,1)}), s8[720896]{0:T(1024)(128)(4,1)S(1)}, s32[]{:S(2)}) async-start(s8[4915200]{0:T(1024)(128)(4,1)} %bitcast.99), calls=%async_computation.3 | async-start | bytes 1441792
  572.7 4.9 slice-start
  574.3 3.4 slice-start.1
  574.3 4.4 copy-start.1

commit v6 on v5

--- a/solution.py
+++ b/solution.py
@@ -292,12 +292,12 @@
         return (high if bits < 2 else 1 - high) * 2 + (low if bits % 2 == 0 else 1 - low)
 
     def place(self, w, owner, top, size):
-        rows, cols = self.shards[w].shape
-        first = pl.multiple_of(owner * rows + top, 16)
-        return self.wholes[w].at[pl.ds(first, size), lanes(self.core * (cols // 2), cols // 2)]
+        rows = self.shards[w].shape[0]
+        first = pl.multiple_of(owner * rows + self.core * (rows // 2) + top, 16)
+        return self.wholes[w].at[pl.ds(first, size), :]
 
     def routes(self, w):
-        rows = self.shards[w].shape[0]
+        rows = self.shards[w].shape[0] // 2
         if self.nb == 4:
             half = rows // 2
             return [
@@ -317,11 +317,10 @@
 
     def copy(self, w, k):
         owner, top, size, device, _ = self.routes(w)[k]
-        cols = self.shards[w].shape[1]
         if self.nb == 4 and k >= 2:
             source = self.place(w, owner, top, size)
         else:
-            source = self.shards[w].at[:, lanes(self.core * (cols // 2), cols // 2)]
+            source = self.shards[w].at[pl.ds(pl.multiple_of(self.core * size, 16), size), :]
         target = self.place(w, owner, top, size)
         return send(source, target, self.out_sem.at[w, k], self.in_sem.at[w, k], {"batch": device})
 
@@ -395,7 +394,7 @@
         functools.partial(embed_kernel, nb, nv, cap, part, rows, first, split), outs, scratch,
         [turn, tok, table, *shards, *extra],
         "embed" if first else "embed_more", 0 if first else 3,
-        in_specs=[SM, VM, VM] + [HB] * len(shards) + [VM] * len(extra),
+        in_specs=[SM, VM, VM] + [VM] * len(shards) + [VM] * len(extra),
         out_specs=[VM] * 3 + [SM, VM] + [HB] * len(shards) + ([HB, VM] if split else []),
     )
 
@@ -724,7 +723,7 @@
         [grad, ids, place, *grads, *extra],
         "unembed" if first else "unembed_more",
         2 if first else 4,
-        in_specs=[VM] * 3 + ([HB, HB, VM, HB] if first else []) + [HB] * len(extra),
+        in_specs=[VM] * 3 + ([HB, HB, VM, HB] if first else []) + [VM] * len(extra),
         out_specs=[VM] + [HB] * (len(grads) + len(extra)),
     )
 
@@ -1252,15 +1251,24 @@
     def other(step):
         return {"batch": lax.rem(b + step, nb)}
 
+    def flip(s):
+        low, high = lax.rem(b, 2), b // 2
+        return (high if s < 2 else 1 - high) * 2 + (low if s % 2 == 0 else 1 - low)
+
     def slot(s, k):
-        return lax.rem(b - s + nb, nb) * nv + lax.rem(chip - k + chips, chips) * 2 + core
+        return flip(s) * nv + lax.rem(chip - k + chips, chips) * 2 + core
 
     def z_copy(k):
         return send(f_ref, fall.at[b * nv + v], z_out.at[k], z_in.at[k], peer(k))
 
-    def mix_copy(s, k):
-        place = fall.at[slot(0, k)]
-        return send(place, place, mix_out.at[k, s], mix_in.at[k, s], other(s))
+    def mix_copy(s, k, way=0):
+        if s < 3:
+            place, device = fall.at[slot(0, k)], flip(s)
+        else:
+            place, device = fall.at[slot(3 - way, k)], flip(way)
+        return send(place, place, mix_out.at[k, s], mix_in.at[k, s], {"batch": device})
+
+    near = [s for s in (1, 2) if s < nb]
 
     def near_copy(s, k):
         place = fall.at[slot(s, k)]
@@ -1273,9 +1281,16 @@
             def _():
                 z_copy(k).wait_recv()
 
-            each(1, nb, lambda t: mix_copy(t, k).start())
+            for t in near:
+                mix_copy(t, k).start()
         else:
-            mix_copy(s, k).wait_recv()
+            mix_copy(s, k, 1).wait_recv()
+        if nb == 4 and s in (1, 2):
+
+            @pl.when(lax.rem(k, 2) == s - 1)
+            def _():
+                mix_copy(3, k, 3 - s).start()
+
         near_copy(s, k).start()
 
     fall[b * nv + v] = f_ref[...]
@@ -1284,7 +1299,7 @@
 
     def logits(s, k):
         near_copy(s, k).wait_recv()
-        p, c = lax.rem(b - s + nb, nb), lax.rem(chip - k + chips, chips)
+        p, c = flip(s), lax.rem(chip - k + chips, chips)
         first = p * nv + c * 2
         start = pl.multiple_of(first * PICKS, 2 * PICKS)
         features = fall[pl.ds(first, 2)].reshape(2 * PICKS, D)
@@ -1406,20 +1421,32 @@
     def pair_copy(s, k):
         return send(handed.at[s, k], half.at[s, k], pair_out.at[s, k], pair_in.at[s, k], sibling)
 
-    def give_copy(s):
-        return send(handed.at[s], mix_got.at[s], give_out.at[s], give_in.at[s], other(s))
+    def give_copy(s, k):
+        if s < 3:
+            return send(handed.at[s, k], mix_got.at[s, k], give_out.at[s, k], give_in.at[s, k], {"batch": flip(s)})
+        device = jnp.where(lax.rem(k, 2) == 0, flip(1), flip(2))
+        return send(handed.at[3, k], mix_got.at[3, k], give_out.at[3, k], give_in.at[3, k], {"batch": device})
 
     def exchange(s):
         def add(k):
             pair_copy(s, k).wait()
-            handed[s, k] = (group[s % 2, shard(k, core), :] + half[s, k].astype(FL)).astype(BF)
+            value = group[s % 2, shard(k, core), :] + half[s, k].astype(FL)
+            handed[s, k] = value.astype(BF)
+            if nb == 4 and s in (1, 2):
+
+                @pl.when(lax.rem(k, 2) == 2 - s)
+                def _():
+                    give_copy(3, k).wait_recv()
+                    handed[s, k] = (value + mix_got[3, k].astype(FL)).astype(BF)
+
+            if s > 0:
+                give_copy(s, k).start()
 
         each(0, chips, add)
-        if s > 0:
-            give_copy(s).start()
-
-    for s in list(range(1, nb)) + [0]:
-        p = lax.rem(b + s, nb)
+
+    order = [3, 2, 1, 0] if nb == 4 else [1, 0]
+    for turn, s in enumerate(order):
+        p = flip(s)
 
         def strip(c, p=p):
             start = pl.multiple_of(p * span + c * 2 * PICKS, 2 * PICKS)
@@ -1432,6 +1459,9 @@
             expo[here, :] = value.astype(BF)
 
         each(0, chips, strip)
+        if turn > 0:
+            exchange(order[turn - 1])
+
         def features_grad(i, p=p, s=s):
             here = pl.ds(pl.multiple_of(i * 512, 512), 512)
             group[s % 2, here, :] = nt(expo[pl.ds(pl.multiple_of(p * span + i * 512, 512), 512), :], w_ref[...])
@@ -1442,8 +1472,6 @@
             handed[s, k] = group[s % 2, shard(k, 1 - core), :].astype(BF)
             pair_copy(s, k).start()
 
-        if s != 1:
-            exchange(s - 1 if s > 0 else nb - 1)
         each(0, chips, swap)
 
     words_sum[...] = jnp.zeros_like(words_sum)
@@ -1452,17 +1480,15 @@
         cut = lanes(i * 512, 512)
         words_sum[...] += nn(ft[:, cut], expo[cut, :])
 
+    strips = nb * span // 512
     each(0, 1, words_grad)
     exchange(0)
-    each(1, nb * span // 512, words_grad)
-    dw_ref[...] = words_sum[...].astype(BF)
-
-    for s in range(1, nb):
-        give_copy(s).wait()
+    each(1, strips // 2, words_grad)
 
     def total_of(k):
         value = handed[0, k].astype(FL)
-        for s in range(1, nb):
+        for s in near:
+            give_copy(s, k).wait_recv()
             value = value + mix_got[s, k].astype(FL)
         return value
 
@@ -1474,6 +1500,8 @@
         sum_copy(t).start()
 
     each(1, chips, pass_on)
+    each(strips // 2, strips, words_grad)
+    dw_ref[...] = words_sum[...].astype(BF)
     df_ref[...] = total_of(chip)
 
     def collect(t):
@@ -1485,7 +1513,8 @@
     for s in range(nb):
         each(0, chips, lambda k, s=s: near_copy(s, k).wait_send())
         if s > 0:
-            each(0, chips, lambda k, s=s: mix_copy(s, k).wait_send())
+            each(0, chips, lambda k, s=s: mix_copy(s, k, 1).wait_send())
+            each(0, chips, lambda k, s=s: give_copy(s, k).wait_send())
 
 
 def wide_head(nb, nv, block_rows, features, words, live, targets):
@@ -1514,7 +1543,7 @@
         pltpu.VMEM((chips, PICKS, D), BF),
         pltpu.VMEM((chips, PICKS, D), BF),
         dma((chips,)), dma((chips,)), dma((chips, nb)), dma((chips, nb)), dma((chips, nb)), dma((chips, nb)),
-        dma((4, most)), dma((4, most)), dma((nb, chips)), dma((nb, chips)), dma((nb,)), dma((nb,)),
+        dma((4, most)), dma((4, most)), dma((nb, chips)), dma((nb, chips)), dma((nb, chips)), dma((nb, chips)),
         dma((chips,)), dma((chips,)),
     ]
     return run(
@@ -1648,7 +1677,7 @@
         weight_semaphores(2),
         [x, a_all, seg_row, pos_row, pieces[1], pieces[3]],
         "attend", 6, flops=7 * 10**9, moved=20 * 10**6,
-        in_specs=[VM] * 4 + [HB] * 2, out_specs=[VM] * 9 + [HB] * 2,
+        out_specs=[VM] * 9 + [HB] * 2,
     )
     x1, h2, z, act, x2, features = run(
         feed_kernel,

time: 597 us -> 565 us (0.946)
  Pallas kernels: 534 us -> 502 us
    pallas_call x8, Pallas kernels: 534 us -> 502 us  [run(): pl.pallas_call(kernel, out_shape=outs, in_specs=in_specs if in_specs is n...]
where the time goes in v6:
time: 565 us; the launch traced here: 559 us
  Pallas kernels  502 us (89%)
  other arithmetic  38.1 us (7%)
  local copies, waits for them, and re-layouts  13.3 us (2%)
    pallas_call x8, Pallas kernels, run(): pl.pallas_call(kernel, out_shape=outs, in_specs=in_specs if in_specs is n...  502 us
    sub x6, other arithmetic, adamw(): weight - rate * (fixed_moment / (jnp.sqrt(fixed_square) + ADAM_EPS) + dec...  17 us

profile of v6, /device:TPU:0, one launch (start us, length us, event | category | flops | bytes accessed | tf_op | source)
XLA Modules:
  0.0 558.6 jit_solution(2870095740823649668)
XLA Ops:
  0.7 2.6 bitcast_convert_fusion
  3.3 1.6 pad.8.refs_2_
  5.0 0.7 copy-done.3
  5.7 0.1 convert_bitcast_fusion.3
  5.7 0.0 copy-done.17
  5.8 0.1 copy.164
  6.0 1.1 concatenate.9.refs_3_
  7.1 2.8 convert_bitcast_fusion.2.refs_4_
  10.0 103.0 %embed.1 = (bf16[1024,768]{1,0:T(8,128)(2,1)S(1)}, s32[8,768,1]{2,1,0:T(8,128)}, s32[4,8,1024]{2,1,0:T(8,128)S(1)}, s32[1]{0:T(128)}, s32[4,8,1024]{2,1,0:T(8,12...) custom-call(s32[1]{0:T(128)} %constant.47.clone.1.refs_0_, ...), custom_call_target="tpu_custom_call" | custom-call | tf_op jit(solution)/shard_map/embed/pallas_call | solution.py:68
  113.7 0.2 while.23
  113.9 3.4 convert_bitcast_fusion.1.c_ref
  117.3 0.7 convert_bitcast_fusion.4.p_ref
  118.0 41.3 %attend.1 = (bf16[1536,768]{1,0:T(8,128)(2,1)}, bf16[1536,1536]{1,0:T(8,128)(2,1)}, bf16[128,768]{1,0:T(8,128)(2,1)}, bf16[128,768]{1,0:T(8,128)(2,1)}, f32[128,...) custom-call(bf16[1024,768]{1,0:T(8,128)(2,1)S(1)} %get-tuple-element, ...), custom_call_target="tpu_custom_call" | custom-call | flops 7000000000 | bytes 20000000 | tf_op jit(solution)/shard_map/attend/pallas_call | solution.py:68
  159.3 8.8 %feed.1 = (f32[128,768]{1,0:T(8,128)}, bf16[128,768]{1,0:T(8,128)(2,1)}, f32[128,3072]{1,0:T(8,128)}, bf16[128,3072]{1,0:T(8,128)(2,1)}, f32[128,768]{1,0:T(8,128)}, /*index=5*/bf16[128,768]{1,0:T(8,128)(2,1)}) custom-call(f32[128,768]{1,0:T(8,128)} %get-tuple-element.191.xq_ref, bf16[128,768]{1,0:T(8,128)(2,1)} %get-tuple-element.192.o_ref, ...), custom_call_target="tpu_custom_call" | custom-call | flops 2000000000 | bytes 15000000 | tf_op jit(solution)/shard_map/feed/pallas_call | solution.py:68
  168.1 0.6 broadcast_in_dim.50.live_ref
  168.8 121.3 %wide_head.1 = (f32[128,768]{1,0:T(8,128)}, bf16[768,1664]{1,0:T(8,128)(2,1)}, f32[8,128]{1,0:T(8,128)}) custom-call(bf16[128,768]{1,0:T(8,128)(2,1)} %get-tuple-element.197.f_ref, bf16[768,1664]{1,0:T(8,128)(2,1)} %get-tuple-element.198.w_ref, s32[1,6656]{1,0:T(1,128)} %broadcast_in_dim.50.live_ref, s32[4,1,1024]{2,1,0:T(1,128)} %get-tuple-element.199.target_ref), custom_call_target="tpu_custom_call" | custom-call | tf_op jit(solution)/shard_map/wide_head/pallas_call | solution.py:68
  290.1 15.1 %feed_back.1 = (bf16[3072,768]{1,0:T(8,128)(2,1)}, bf16[768,3072]{1,0:T(8,128)(2,1)}, bf16[768,768]{1,0:T(8,128)(2,1)}, f32[128,768]{1,0:T(8,128)}, bf16[128,768]{1,0:T(8,128)(2,1)}, /*index=5*/f32[8,768]{1,0:T(8,128)}) custom-call(f32[128,768]{1,0:T(8,128)} %get-tuple-element.200.df_ref, f32[128,768]{1,0:T(8,128)} %get-tuple-element.201.x2_ref, ...), custom_call_target="tpu_custom_call" | custom-call | flops 4000000000 | bytes 30000000 | tf_op jit(solution)/shard_map/feed_back/pallas_call | solution.py:68
  305.2 47.0 %attend_back.1 = (bf16[768,2560]{1,0:T(8,128)(2,1)}, bf16[1024,768]{1,0:T(8,128)(2,1)S(1)}, bf16[192,1536]{1,0:T(8,128)(2,1)}) custom-call(bf16[128,768]{1,0:T(8,128)(2,1)} %get-tuple-element.206.do_ref, bf16[128,768]{1,0:T(8,128)(2,1)} %get-tuple-element.207.q_ref, bf16[1536,1536]{1,0:T(8,128)(2,1)} %get-tuple-element.208.kv_ref, ...), custom_call_target="tpu_custom_call" | custom-call | flops 12000000000 | bytes 25000000 | tf_op jit(solution)/shard_map/attend_back/pallas_call | solution.py:68
  352.3 150.1 %unembed.1 = (f32[192,6400]{1,0:T(8,128)}, bf16[192,2560]{1,0:T(8,128)(2,1)}, bf16[192,768]{1,0:T(8,128)(2,1)}, bf16[192,3072]{1,0:T(8,128)(2,1)}, bf16[768,768]{1,0:T(8,128)(2,1)}, /*index=5*/bf16[192,6656]{1,0:T(8,128)(2,1)}) custom-call(bf16[1024,768]{1,0:T(8,128)(2,1)S(1)} %get-tuple-element.522.refs_0_, s32[8,768,1]{2,1,0:T(8,128)} %get-tuple-element.217.refs_1_, ...), custom_call_target="tpu_custom_call" | custom-call | tf_op jit(solution)/shard_map/unembed/pallas_call | solution.py:68
  502.3 0.2 while.24
  502.6 15.5 %norm.1 = f32[8,128]{1,0:T(8,128)} custom-call(f32[192,6400]{1,0:T(8,128)} %get-tuple-element.226.extra_ref, bf16[192,6656]{1,0:T(8,128)(2,1)} %get-tuple-element.227.dw_ref, bf16[192,2560]{1,0:T(8,128)(2,1)} %get-tuple-element.228.a_ref, bf16[192,768]{1,0:T(8,128)(2,1)} %get-tuple-element.229.p_ref, bf16[192,3072]{1,0:T(8,128)(2,1)} %get-tuple-element.230.u_ref, ...), custom_call_target="tpu_custom_call" | custom-call | tf_op jit(solution)/shard_map/norm/pallas_call | solution.py:68
  518.1 1.2 fusion.23
  520.1 0.2 convert_element_type.59
  521.1 0.1 copy.166
  521.2 0.1 copy.167
  521.4 0.1 copy.172
  521.5 0.1 copy.173
  521.6 0.2 multiply_divide_fusion
  521.8 0.1 copy.174
  521.9 0.1 copy.176
  522.1 0.1 copy.175
  522.2 0.7 copy.180
  522.9 0.1 copy.168
  523.0 0.1 copy.170
  523.1 0.1 copy.169
  523.2 0.7 copy.177
  523.9 0.7 copy.178
  524.6 0.7 copy.179
  525.3 0.7 copy.181
  525.9 0.7 copy.182
  526.6 7.7 %multiply_subtract_fusion = (f32[1,768,768]{2,1,0:T(8,128)}, f32[1,768,768]{2,1,0:T(8,128)}, f32[1,768,768]{2,1,0:T(8,128)}) fusion(f32[1,768,768]{2,1,0:T(8,128)} %param.50, f32[]{:T(128)} %bitcast.17, f32[]{:T(128)} %bitcast.15, f32[]{:T(128)S(6)} %min.3, bf16[768,768]{1,0:T(8,128)(2,1)} %get-tuple-element.231.c_ref, f32[1,768,768]{2,1,0:T(8,128)} %param.52, ...), kind=kLoop, calls=%fused_computation.29 | loop fusion | flops 10027008 | bytes 15335436 | tf_op jit(solution)/shard_map/sub | solution.py:1622
  534.4 4.4 multiply_subtract_fusion.1
  538.9 1.5 multiply_subtract_fusion.3
  540.4 1.0 copy-done.4
  541.4 0.5 copy-done.11
  541.9 3.4 multiply_subtract_fusion.2
  545.3 1.0 copy-done.1
  546.3 10.9 %fusion.16 = (f32[6400,192]{0,1:T(8,128)}, f32[6400,192]{0,1:T(8,128)}, f32[6400,192]{0,1:T(8,128)}) fusion(f32[]{:T(128)S(6)} %min.3, f32[192,6400]{1,0:T(8,128)S(1)} %bitcast.98, bf16[192,6656]{1,0:T(8,128)(2,1)S(1)} %copy-done.1, f32[6400,192]{0,1:T(8,128)} %param.40, f32[]{:T(128)} %bitcast.17, f32[]{:T(128)} %bitcast.15, f32[6400,192]{0,1:T(8,128)} %param.39, ...), kind=kLoop, calls=%fused_computation.67 | loop fusion | flops 22118400 | bytes 36864012 | tf_op jit(solution)/shard_map/transpose | solution.py:1746
  (70 shorter events, 0.3 us)
Async XLA Ops:
  3.3 1.7 copy-start.18
  3.3 2.3 copy-start.3
  5.0 0.8 copy-start.17
  5.0 0.8 copy-start.16
  113.9 45.4 %copy-start = (bf16[1024,768]{1,0:T(8,128)(2,1)}, bf16[1024,768]{1,0:T(8,128)(2,1)S(1)}, u32[]{:S(2)}) copy-start(bf16[1024,768]{1,0:T(8,128)(2,1)S(1)} %get-tuple-element.189.x_ref) | copy-start | bytes 4718596
  113.9 3.4 copy-start.9
  159.3 8.8 %copy-start.19 = (s32[6400]{0:T(1024)S(1)}, s32[6400]{0:T(1024)}, u32[]{:S(2)}) copy-start(s32[6400]{0:T(1024)} %param.36) | copy-start | bytes 76804
  352.2 150.1 %copy-start.24 = (s32[8]{0:T(128)S(1)}, s32[8]{0:T(128)}, u32[]{:S(2)}) copy-start(s32[8]{0:T(128)} %constant.129.clone..sunk.2) | copy-start | bytes 100
  502.6 17.5 %copy-start.6 = (bf16[192,2560]{1,0:T(8,128)(2,1)S(1)}, bf16[192,2560]{1,0:T(8,128)(2,1)}, u32[]{:S(2)}) copy-start(bf16[192,2560]{1,0:T(8,128)(2,1)} %get-tuple-element.228.a_ref) | copy-start | bytes 2949124
  518.1 3.0 copy-start.20
  518.1 3.1 copy-start.21
  518.1 3.3 copy-start.22
  518.1 3.4 copy-start.23
  526.6 7.7 %copy-start.2 = (f32[1,192,3072]{2,1,0:T(8,128)S(1)}, f32[1,192,3072]{2,1,0:T(8,128)}, u32[]{:S(2)}) copy-start(f32[1,192,3072]{2,1,0:T(8,128)} %param.47) | copy-start | bytes 7077892
  526.6 7.7 %copy-start.5 = (bf16[192,3072]{1,0:T(8,128)(2,1)S(1)}, bf16[192,3072]{1,0:T(8,128)(2,1)}, u32[]{:S(2)}) copy-start(bf16[192,3072]{1,0:T(8,128)(2,1)} %get-tuple-element.230.u_ref) | copy-start | bytes 3538948
  526.6 7.7 %copy-start.7 = (f32[1,192,3072]{2,1,0:T(8,128)S(1)}, f32[1,192,3072]{2,1,0:T(8,128)}, u32[]{:S(2)}) copy-start(f32[1,192,3072]{2,1,0:T(8,128)} %param.49) | copy-start | bytes 7077892
  526.6 7.7 %copy-start.8 = (f32[1,192,3072]{2,1,0:T(8,128)S(1)}, f32[1,192,3072]{2,1,0:T(8,128)}, u32[]{:S(2)}) copy-start(f32[1,192,3072]{2,1,0:T(8,128)} %param.48) | copy-start | bytes 7077892
  534.4 4.5 copy-start.10
  534.4 4.5 copy-start.13
  534.4 4.5 copy-start.14
  534.4 4.5 copy-start.15
  534.4 6.0 %copy-start.12 = (f32[1,192,2304]{2,1,0:T(8,128)S(1)}, f32[1,192,2304]{2,1,0:T(8,128)}, u32[]{:S(2)}) copy-start(f32[1,192,2304]{2,1,0:T(8,128)} %param.42) | copy-start | bytes 5308420
  534.4 10.8 %slice-start.2 = ((s8[4915200]{0:T(1024)(128)(4,1)}), s8[4194304]{0:T(1024)(128)(4,1)S(1)}, s32[]{:S(2)}) async-start(s8[4915200]{0:T(1024)(128)(4,1)} %bitcast.99), calls=%async_computation.2 | async-start | bytes 8388608
  538.8 2.5 copy-start.4
  538.8 3.1 copy-start.11
  538.9 6.4 %slice-start.3 = ((s8[4915200]{0:T(1024)(128)(4,1)}), s8[720896]{0:T(1024)(128)(4,1)S(1)}, s32[]{:S(2)}) async-start(s8[4915200]{0:T(1024)(128)(4,1)} %bitcast.99), calls=%async_computation.3 | async-start | bytes 1441792
  540.4 4.9 slice-start
  541.9 3.4 slice-start.1
  541.9 4.4 copy-start.1

commit v7 on v6

--- a/solution.py
+++ b/solution.py
@@ -576,16 +576,66 @@
     return refs
 
 
+def squares(refs, part):
+    cols = min(ref.shape[1] for ref in refs)
+
+    def add(j, total):
+        value = refs[0][:, lanes(j * part, part)].astype(FL)
+        for ref in refs[1:]:
+            value = value + ref[:, lanes(j * part, part)].astype(FL)
+        return total + jnp.sum(value * value, axis=0, keepdims=True)
+
+    line = lax.fori_loop(0, cols // part, add, jnp.zeros((1, part), FL))
+    return jnp.sum(line, axis=1, keepdims=True)
+
+
+def add_up(nb, nv, own, loss_ref, out_ref, mine, near, lines, vocab_out, vocab_in, batch_out, batch_in):
+    b, v = lax.axis_index("batch"), lax.axis_index("vocab")
+    line = iota((8, 128), 0)
+    mine[...] = jnp.where(line == 0, own, jnp.where((line == 1) & (v == 0), loss_ref[...], 0.0))
+
+    def vocab_copy(step):
+        return send(mine, near.at[v], vocab_out.at[step], vocab_in.at[step], {"vocab": lax.rem(v + step, nv)})
+
+    each(1, nv, lambda step: vocab_copy(step).start())
+    near[v] = mine[...]
+    each(1, nv, lambda step: vocab_copy(step).wait())
+    mine[...] = lax.fori_loop(0, nv, lambda u, total: total + near[u], jnp.zeros((8, 128), FL))
+
+    def batch_copy(step):
+        return send(mine, lines.at[b], batch_out.at[step], batch_in.at[step], {"batch": lax.rem(b + step, nb)})
+
+    each(1, nb, lambda step: batch_copy(step).start())
+    lines[b] = mine[...]
+    each(1, nb, lambda step: batch_copy(step).wait())
+    out_ref[...] = lax.fori_loop(0, nb, lambda u, total: total + lines[u], jnp.zeros((8, 128), FL))
+
+
+def add_up_scratch(nb, nv):
+    dma = pltpu.SemaphoreType.DMA
+    tiles = [pltpu.VMEM((8, 128), FL), pltpu.VMEM((nv, 8, 128), FL), pltpu.VMEM((nb, 8, 128), FL)]
+    return tiles + [dma((nv,)), dma((nv,)), dma((nb,)), dma((nb,))]
+
+
+def norm_kernel(nb, nv, extra_ref, dw_ref, a_ref, p_ref, u_ref, c_ref, loss_ref, out_ref, *scratch):
+    meet((("batch", nb), ("vocab", nv)))
+    own = squares((extra_ref, dw_ref), chunk_of(extra_ref.shape[1], 640))
+    layer = squares((a_ref,), 512) + squares((p_ref,), 384) + squares((u_ref,), 512) + squares((c_ref,), 384)
+    own = own + jnp.where(lax.axis_index("vocab") == 0, layer, jnp.zeros_like(layer))
+    add_up(nb, nv, own, loss_ref, out_ref, *scratch)
+
+
 def unembed_kernel(nb, nv, cap, part, first, split, *refs):
     x_ref, ids_ref, place_ref = refs[:3]
     grads, refs = (refs[3:7], refs[7:]) if first else ((), refs[3:])
     if first:
         totals, grads = {2: grads[2]}, (grads[0], grads[1], None, grads[3])
-    quarter_ref, refs = (refs[0], refs[1:]) if split else (None, refs)
+    (quarter_ref, loss_ref), refs = (refs[:2], refs[2:]) if split else ((None, None), refs)
     out_ref = refs[0]
     sums, refs = (refs[1:5], refs[5:]) if first else ((), refs[1:])
-    dw_ref, refs = (refs[0], refs[1:]) if split else (None, refs)
+    (dw_ref, total_ref, rows_ref), refs = (refs[:3], refs[3:]) if split else ([None] * 3, refs)
     (quarter_out, quarter_in, quarter_own), refs = (refs[:3], refs[3:]) if split else ([None] * 3, refs)
+    (strip, strip_sem, *sum_refs), refs = (refs[:9], refs[9:]) if split else ([None] * 2, refs)
     turned, parts, sent, got, mix_out, mix_in, row_out, row_in = refs[:8]
     layer = GradientSum(nb, nv, grads, refs[8:], totals, sums) if first else None
     b, v = lax.axis_index("batch"), lax.axis_index("vocab")
@@ -691,11 +741,22 @@
             quarter_keep().wait()
             for step in range(1, nb):
                 quarter_copy(step).wait()
+            rows_copy = pltpu.make_async_copy(sums[0].at[:, lanes(3 * D, 128)], strip, strip_sem.at[0])
+            rows_copy.start()
+            layer_squares = jnp.zeros((1, 1), FL)
+            for w in range(4):
+                cols = layer.result[w].shape[1]
+                layer_squares += squares((layer.result[w],), max(n for n in (640, 512, 384, 128) if cols % n == 0))
+            own = squares((out_ref, dw_ref), part)
+            own = own + jnp.where(v < 2, layer_squares, 0.0)
+            add_up(nb, nv, own, loss_ref, total_ref, *sum_refs)
+            rows_copy.wait()
+            rows_ref[...] = strip[...].astype(FL).T[:8, :]
     else:
         each(0, nv, take)
 
 
-def unembed(nb, nv, cap, width, rows, grad, ids, place, grads=(), quarter=None):
+def unembed(nb, nv, cap, width, rows, grad, ids, place, grads=(), quarter=None, loss=None):
     part = chunk_of(rows, 640)
     count = nb * cap
     dma = pltpu.SemaphoreType.DMA
@@ -708,14 +769,15 @@
     ]
     first, split = len(grads) > 0, quarter is not None
     if split:
-        scratch = [dma((nb,)), dma((nb,)), dma((1,))] + scratch
+        strip = [pltpu.VMEM((width, 128), BF), dma((1,))]
+        scratch = [dma((nb,)), dma((nb,)), dma((1,))] + strip + add_up_scratch(nb, nv) + scratch
     if first:
         shapes = [item.shape if w != 2 else (nb * item.shape[0], 2 * item.shape[1]) for w, item in enumerate(grads)]
         scratch += gradient_scratch(nb, nv, shapes, (0, 1, 3))
     outs = [SD((width, rows), FL)] + [SD((item[0] // nb, item[1]), BF) for item in (shapes if first else ())]
-    extra = [quarter] if split else []
+    extra = [quarter, loss] if split else []
     if split:
-        outs.append(SD((width, nb * quarter.shape[1]), BF))
+        outs += [SD((width, nb * quarter.shape[1]), BF), SD((8, 128), FL), SD((8, width), FL)]
     return run(
         functools.partial(unembed_kernel, nb, nv, cap, part, first, split),
         outs,
@@ -724,7 +786,7 @@
         "unembed" if first else "unembed_more",
         2 if first else 4,
         in_specs=[VM] * 3 + ([HB, HB, VM, HB] if first else []) + [VM] * len(extra),
-        out_specs=[VM] + [HB] * (len(grads) + len(extra)),
+        out_specs=[VM] + [HB] * len(grads) + ([VM] * 3 if split else []),
     )
 
 
@@ -1556,60 +1618,10 @@
     )
 
 
-def norm_kernel(
-    nb, nv, extra_ref, dw_ref, a_ref, p_ref, u_ref, c_ref, loss_ref, out_ref,
-    mine, near, lines, vocab_out, vocab_in, batch_out, batch_in,
-):
-    b, v = lax.axis_index("batch"), lax.axis_index("vocab")
-    meet((("batch", nb), ("vocab", nv)))
-
-    def squares(refs, part):
-        cols = refs[0].shape[1]
-
-        def add(j, total):
-            value = refs[0][:, lanes(j * part, part)].astype(FL)
-            for ref in refs[1:]:
-                value = value + ref[:, lanes(j * part, part)].astype(FL)
-            return total + jnp.sum(value * value, axis=0, keepdims=True)
-
-        line = lax.fori_loop(0, cols // part, add, jnp.zeros((1, part), FL))
-        return jnp.sum(line, axis=1, keepdims=True)
-
-    own = squares((extra_ref, dw_ref), chunk_of(extra_ref.shape[1], 640))
-    layer = squares((a_ref,), 512) + squares((p_ref,), 384) + squares((u_ref,), 512) + squares((c_ref,), 384)
-    own = own + jnp.where(v == 0, layer, jnp.zeros_like(layer))
-    line = iota((8, 128), 0)
-    mine[...] = jnp.where(line == 0, own, jnp.where((line == 1) & (v == 0), loss_ref[...], 0.0))
-
-    def vocab_copy(step):
-        return send(mine, near.at[v], vocab_out.at[step], vocab_in.at[step], {"vocab": lax.rem(v + step, nv)})
-
-    each(1, nv, lambda step: vocab_copy(step).start())
-    near[v] = mine[...]
-    each(1, nv, lambda step: vocab_copy(step).wait())
-    mine[...] = lax.fori_loop(0, nv, lambda u, total: total + near[u], jnp.zeros((8, 128), FL))
-
-    def batch_copy(step):
-        return send(mine, lines.at[b], batch_out.at[step], batch_in.at[step], {"batch": lax.rem(b + step, nb)})
-
-    each(1, nb, lambda step: batch_copy(step).start())
-    lines[b] = mine[...]
-    each(1, nb, lambda step: batch_copy(step).wait())
-    out_ref[...] = lax.fori_loop(0, nb, lambda u, total: total + lines[u], jnp.zeros((8, 128), FL))
-
-
 def norm(nb, nv, extra, dw, sums, loss):
-    dma = pltpu.SemaphoreType.DMA
     return run(
-        functools.partial(norm_kernel, nb, nv),
-        [SD((8, 128), FL)],
-        [
-            pltpu.VMEM((8, 128), FL), pltpu.VMEM((nv, 8, 128), FL), pltpu.VMEM((nb, 8, 128), FL),
-            dma((nv,)), dma((nv,)), dma((nb,)), dma((nb,)),
-        ],
-        [extra, dw, *sums, loss],
-        "norm",
-        5,
+        functools.partial(norm_kernel, nb, nv), [SD((8, 128), FL)], add_up_scratch(nb, nv),
+        [extra, dw, *sums, loss], "norm", 5,
     )[0]
 
 
@@ -1717,9 +1729,9 @@
         "attend_back", 7, flops=12 * 10**9, moved=25 * 10**6,
         in_specs=[VM] * 14 + [HB],
     )
-    extra, *sums = unembed(nb, nv, cap, width, rows, dx, ids, place, (da, dp, du_sum, dc), dw if split else None)
+    extra, *sums = unembed(nb, nv, cap, width, rows, dx, ids, place, (da, dp, du_sum, dc), *((dw, loss_block) if split else ()))
     if split:
-        dw_sum = sums.pop()
+        *sums, dw_sum, totals, norm_grads = sums
 
     def more_grads(state):
         turn, total = state
@@ -1730,10 +1742,15 @@
 
     extra = lax.while_loop(lambda state: state[0] < turns, more_grads, (jnp.int32(1), extra))[1]
 
-    totals = norm(nb, nv, extra, dw_sum, sums, loss_block)
+    if split:
+        totals = lax.cond(
+            turns > 1, lambda: norm(nb, nv, extra, dw_sum, sums, loss_block), lambda: totals
+        )
+    else:
+        totals = norm(nb, nv, extra, dw_sum, sums, loss_block)
     grad_table = dw_sum[:, :rows].astype(FL) + extra
     grad_a, grad_p, grad_u, grad_c = (item.astype(FL) for item in sums)
-    grad_norms = grad_a[:, 3 * D : 3 * D + 6].T
+    grad_norms = norm_grads if split else grad_a[:, 3 * D : 3 * D + 6].T
     grad_a = grad_a[:, : 3 * D]
     squares, loss = totals[0, 0], totals[1, 0]
     gradient_norm = jnp.sqrt(squares)
@@ -1749,7 +1766,7 @@
     expand_out = update(expand, expand_moment, expand_square, grad_u[None])
     contract_out = update(contract, contract_moment, contract_square, grad_c[None])
     gain_out = update(gain, gain_moment, gain_square, grad_norms[:3], 0.0, NORM_RATE)
-    shift_out = update(shift, shift_moment, shift_square, grad_norms[3:], 0.0, NORM_RATE)
+    shift_out = update(shift, shift_moment, shift_square, grad_norms[3:6], 0.0, NORM_RATE)
     return (
         loss, gradient_norm, *table_out, *attend_out, *project_out, *expand_out, *contract_out, *gain_out, *shift_out,
     )

time: 565 us -> 552 us (0.977)
  local copies, waits for them, and re-layouts: 13.3 us -> 5.96 us
  Pallas kernels: 502 us -> 495 us
    pallas_call x8 -> x7, Pallas kernels: 502 us -> 495 us  [run(): pl.pallas_call(kernel, out_shape=outs, in_specs=in_specs if in_specs is n...]
    unnamed x66 -> x62, local copies, waits for them, and re-layouts: 7.65 us -> 1.88 us
    sub x6 -> x5, other arithmetic: 17 us -> 20 us  [adamw(): weight - rate * (fixed_moment / (jnp.sqrt(fixed_square) + ADAM_EPS) + dec...]
where the time goes in v7:
time: 552 us; the launch traced here: 546 us
  Pallas kernels  495 us (90%)
  other arithmetic  40.1 us (7%)
  local copies, waits for them, and re-layouts  5.96 us (1%)
    pallas_call x7, Pallas kernels, run(): pl.pallas_call(kernel, out_shape=outs, in_specs=in_specs if in_specs is n...  495 us
    sub x5, other arithmetic, adamw(): weight - rate * (fixed_moment / (jnp.sqrt(fixed_square) + ADAM_EPS) + dec...  20 us

profile of v7, /device:TPU:0, one launch (start us, length us, event | category | flops | bytes accessed | tf_op | source)
XLA Modules:
  0.0 546.3 jit_solution(15521762421720030155)
XLA Ops:
  0.7 2.6 bitcast_convert_fusion
  3.3 0.0 copy-start.15
  3.3 1.6 pad.8.refs_2_
  5.0 0.0 copy-start.2
  5.0 1.7 convert_bitcast_fusion.3
  6.7 0.0 copy-done.17
  6.8 0.1 copy.64
  6.9 1.1 concatenate.9.refs_3_
  8.1 1.2 convert_bitcast_fusion.2.refs_4_
  9.2 103.0 %embed.1 = (bf16[1024,768]{1,0:T(8,128)(2,1)S(1)}, s32[8,768,1]{2,1,0:T(8,128)}, s32[4,8,1024]{2,1,0:T(8,128)S(1)}, s32[1]{0:T(128)}, s32[4,8,1024]{2,1,0:T(8,12...) custom-call(s32[1]{0:T(128)} %constant.55.clone.1.refs_0_, ...), custom_call_target="tpu_custom_call" | custom-call | tf_op jit(solution)/shard_map/embed/pallas_call | solution.py:68
  113.0 0.2 while.23
  113.2 0.0 copy-start
  113.2 0.0 copy-start.9
  113.2 3.4 convert_bitcast_fusion.1.c_ref
  116.6 0.0 copy-done.9
  116.6 0.7 convert_bitcast_fusion.4.p_ref
  117.4 41.3 %attend.1 = (bf16[1536,768]{1,0:T(8,128)(2,1)}, bf16[1536,1536]{1,0:T(8,128)(2,1)}, bf16[128,768]{1,0:T(8,128)(2,1)}, bf16[128,768]{1,0:T(8,128)(2,1)}, f32[128,...) custom-call(bf16[1024,768]{1,0:T(8,128)(2,1)S(1)} %get-tuple-element, ...), custom_call_target="tpu_custom_call" | custom-call | flops 7000000000 | bytes 20000000 | tf_op jit(solution)/shard_map/attend/pallas_call | solution.py:68
  158.7 0.0 copy-start.16
  158.7 8.8 %feed.1 = (f32[128,768]{1,0:T(8,128)}, bf16[128,768]{1,0:T(8,128)(2,1)}, f32[128,3072]{1,0:T(8,128)}, bf16[128,3072]{1,0:T(8,128)(2,1)}, f32[128,768]{1,0:T(8,128)}, /*index=5*/bf16[128,768]{1,0:T(8,128)(2,1)}) custom-call(f32[128,768]{1,0:T(8,128)} %get-tuple-element.255.xq_ref, bf16[128,768]{1,0:T(8,128)(2,1)} %get-tuple-element.256.o_ref, ...), custom_call_target="tpu_custom_call" | custom-call | flops 2000000000 | bytes 15000000 | tf_op jit(solution)/shard_map/feed/pallas_call | solution.py:68
  167.5 0.6 broadcast_in_dim.50.live_ref
  168.1 121.2 %wide_head.1 = (f32[128,768]{1,0:T(8,128)}, bf16[768,1664]{1,0:T(8,128)(2,1)}, f32[8,128]{1,0:T(8,128)S(1)}) custom-call(bf16[128,768]{1,0:T(8,128)(2,1)} %get-tuple-element.261.f_ref, bf16[768,1664]{1,0:T(8,128)(2,1)} %get-tuple-element.262.w_ref, s32[1,6656]{1,0:T(1,128)} %broadcast_in_dim.50.live_ref, s32[4,1,1024]{2,1,0:T(1,128)} %get-tuple-element.263.target_ref), custom_call_target="tpu_custom_call" | custom-call | tf_op jit(solution)/shard_map/wide_head/pallas_call | solution.py:68
  289.3 15.1 %feed_back.1 = (bf16[3072,768]{1,0:T(8,128)(2,1)}, bf16[768,3072]{1,0:T(8,128)(2,1)}, bf16[768,768]{1,0:T(8,128)(2,1)}, f32[128,768]{1,0:T(8,128)}, bf16[128,768]{1,0:T(8,128)(2,1)}, /*index=5*/f32[8,768]{1,0:T(8,128)}) custom-call(f32[128,768]{1,0:T(8,128)} %get-tuple-element.264.df_ref, f32[128,768]{1,0:T(8,128)} %get-tuple-element.265.x2_ref, ...), custom_call_target="tpu_custom_call" | custom-call | flops 4000000000 | bytes 30000000 | tf_op jit(solution)/shard_map/feed_back/pallas_call | solution.py:68
  304.5 47.2 %attend_back.1 = (bf16[768,2560]{1,0:T(8,128)(2,1)}, bf16[1024,768]{1,0:T(8,128)(2,1)S(1)}, bf16[192,1536]{1,0:T(8,128)(2,1)}) custom-call(bf16[128,768]{1,0:T(8,128)(2,1)} %get-tuple-element.270.do_ref, bf16[128,768]{1,0:T(8,128)(2,1)} %get-tuple-element.271.q_ref, bf16[1536,1536]{1,0:T(8,128)(2,1)} %get-tuple-element.272.kv_ref, ...), custom_call_target="tpu_custom_call" | custom-call | flops 12000000000 | bytes 25000000 | tf_op jit(solution)/shard_map/attend_back/pallas_call | solution.py:68
  351.7 0.0 copy-start.24
  351.7 158.5 %unembed.1 = (f32[192,6400]{1,0:T(8,128)}, bf16[192,2560]{1,0:T(8,128)(2,1)}, bf16[192,768]{1,0:T(8,128)(2,1)}, bf16[192,3072]{1,0:T(8,128)(2,1)}, bf16[768,768]...) custom-call(bf16[1024,768]{1,0:T(8,128)(2,1)S(1)} %get-tuple-element.491.refs_0_, ...), custom_call_target="tpu_custom_call" | custom-call | tf_op jit(solution)/shard_map/unembed/pallas_call | solution.py:68
  510.2 0.2 while.24
  510.5 0.0 copy-start.20
  510.5 0.0 copy-start.21
  510.5 0.0 copy-start.22
  510.5 0.0 copy-start.23
  510.5 0.5 fusion.23
  512.6 0.6 multiply_subtract_fusion.4
  513.2 0.0 copy-start.8
  513.2 0.0 slice-start.4
  513.2 7.9 %multiply_subtract_fusion = (f32[1,768,768]{2,1,0:T(8,128)}, f32[1,768,768]{2,1,0:T(8,128)}, f32[1,768,768]{2,1,0:T(8,128)}) fusion(f32[1,768,768]{2,1,0:T(8,128)} %param.52, f32[]{:T(128)} %bitcast.17, f32[]{:T(128)} %bitcast.15, f32[]{:T(128)S(6)} %min.14, bf16[768,768]{1,0:T(8,128)(2,1)} %get-tuple-element.297, f32[1,768,768]{2,1,0:T(8,128)} %param.54, ...), kind=kLoop, calls=%fused_computation.29 | loop fusion | flops 10027008 | bytes 15335436 | tf_op jit(solution)/shard_map/sub | solution.py:1634
  521.2 0.0 copy-start.10
  521.2 0.0 copy-start.13
  521.2 0.0 copy-start.14
  521.2 0.0 copy-start.11
  521.2 0.0 slice-start.2
  521.3 0.0 slice-start.5
  521.3 4.4 multiply_subtract_fusion.1
  525.7 0.0 slice-start.3
  525.7 1.5 multiply_subtract_fusion.3
  527.2 1.5 copy-done.4
  528.7 0.3 copy-done.6
  528.9 5.6 %multiply_subtract_fusion.2 = (f32[1,192,2304]{2,1,0:T(8,128)}, f32[1,192,2304]{2,1,0:T(8,128)}, f32[1,192,2304]{2,1,0:T(8,128)}) fusion(f32[1,192,2304]{2,1,0:T(8,128)S(1)} %copy-done.4, f32[]{:T(128)} %bitcast.17, f32[]{:T(128)} %bitcast.15, f32[]{:T(128)S(6)} %min.14, bf16[192,2560]{1,0:T(8,128)(2,1)S(1)} %copy-done.6, f32[1,192,2304]{2,1,0:T(8,128)S(1)} %copy-done.11, ...), kind=kLoop, calls=%fused_computation.36 | loop fusion | flops 7520256 | bytes 11501580 | tf_op jit(solution)/shard_map/sub | solution.py:1634
  534.6 10.3 %fusion.16 = (f32[6400,192]{0,1:T(8,128)}, f32[6400,192]{0,1:T(8,128)}, f32[6400,192]{0,1:T(8,128)}) fusion(f32[]{:T(128)S(6)} %min.14, f32[192,6400]{1,0:T(8,128)S(1)} %bitcast.96, bf16[192,6656]{1,0:T(8,128)(2,1)S(1)} %copy-done.1, f32[6400,192]{0,1:T(8,128)S(1)} %bitcast.100, f32[]{:T(128)} %bitcast.17, f32[]{:T(128)} %bitcast.15, f32[6400,192]{0,1:T(8,128)} %param.41, ...), kind=kLoop, calls=%fused_computation.60 | loop fusion | flops 22118400 | bytes 36864012 | tf_op jit(solution)/shard_map/transpose | solution.py:1763
  (49 shorter events, 0.1 us)
Async XLA Ops:
  3.3 1.7 copy-start.15
  5.0 1.8 copy-start.18
  5.0 1.8 copy-start.17
  5.0 3.1 copy-start.2
  113.2 45.4 %copy-start = (bf16[1024,768]{1,0:T(8,128)(2,1)}, bf16[1024,768]{1,0:T(8,128)(2,1)S(1)}, u32[]{:S(2)}) copy-start(bf16[1024,768]{1,0:T(8,128)(2,1)S(1)} %get-tuple-element.253.x_ref) | copy-start | bytes 4718596
  113.2 3.4 copy-start.9
  158.7 8.8 %copy-start.16 = (s32[6400]{0:T(1024)S(1)}, s32[6400]{0:T(1024)}, u32[]{:S(2)}) copy-start(s32[6400]{0:T(1024)} %param.38) | copy-start | bytes 76804
  351.7 158.5 %copy-start.24 = (s32[8]{0:T(128)S(1)}, s32[8]{0:T(128)}, u32[]{:S(2)}) copy-start(s32[8]{0:T(128)} %constant.132.clone..sunk.2) | copy-start | bytes 100
  510.4 2.1 copy-start.19
  510.5 2.1 copy-start.20
  510.5 2.1 copy-start.21
  510.5 2.1 copy-start.22
  510.5 2.1 copy-start.23
  513.2 8.0 %copy-start.3 = (f32[1,192,3072]{2,1,0:T(8,128)S(1)}, f32[1,192,3072]{2,1,0:T(8,128)}, u32[]{:S(2)}) copy-start(f32[1,192,3072]{2,1,0:T(8,128)} %param.49) | copy-start | bytes 7077892
  513.2 8.0 %copy-start.5 = (bf16[192,3072]{1,0:T(8,128)(2,1)S(1)}, bf16[192,3072]{1,0:T(8,128)(2,1)}, u32[]{:S(2)}) copy-start(bf16[192,3072]{1,0:T(8,128)(2,1)} %get-tuple-element.296) | copy-start | bytes 3538948
  513.2 8.0 %copy-start.7 = (f32[1,192,3072]{2,1,0:T(8,128)S(1)}, f32[1,192,3072]{2,1,0:T(8,128)}, u32[]{:S(2)}) copy-start(f32[1,192,3072]{2,1,0:T(8,128)} %param.51) | copy-start | bytes 7077892
  513.2 8.0 %copy-start.8 = (f32[1,192,3072]{2,1,0:T(8,128)S(1)}, f32[1,192,3072]{2,1,0:T(8,128)}, u32[]{:S(2)}) copy-start(f32[1,192,3072]{2,1,0:T(8,128)} %param.50) | copy-start | bytes 7077892
  513.2 21.3 %slice-start.4 = ((s8[4915200]{0:T(1024)(128)(4,1)}), s8[4194304]{0:T(1024)(128)(4,1)S(1)}, s32[]{:S(2)}) async-start(s8[4915200]{0:T(1024)(128)(4,1)} %bitcast.99), calls=%async_computation.4 | async-start | bytes 8388608
  521.2 4.5 copy-start.10
  521.2 4.5 copy-start.12
  521.2 4.5 copy-start.13
  521.2 4.5 copy-start.14
  521.2 6.0 %copy-start.11 = (f32[1,192,2304]{2,1,0:T(8,128)S(1)}, f32[1,192,2304]{2,1,0:T(8,128)}, u32[]{:S(2)}) copy-start(f32[1,192,2304]{2,1,0:T(8,128)} %param.45) | copy-start | bytes 5308420
  521.2 13.3 %slice-start.2 = ((s8[4915200]{0:T(1024)(128)(4,1)}), s8[4194304]{0:T(1024)(128)(4,1)S(1)}, s32[]{:S(2)}) async-start(s8[4915200]{0:T(1024)(128)(4,1)} %bitcast.97), calls=%async_computation.2 | async-start | bytes 8388608
  521.3 13.3 %slice-start.5 = ((s8[4915200]{0:T(1024)(128)(4,1)}), s8[720896]{0:T(1024)(128)(4,1)S(1)}, s32[]{:S(2)}) async-start(s8[4915200]{0:T(1024)(128)(4,1)} %bitcast.99), calls=%async_computation.5 | async-start | bytes 1441792
  525.6 3.0 copy-start.4
  525.6 3.3 copy-start.6
  525.7 8.8 %slice-start.3 = ((s8[4915200]{0:T(1024)(128)(4,1)}), s8[720896]{0:T(1024)(128)(4,1)S(1)}, s32[]{:S(2)}) async-start(s8[4915200]{0:T(1024)(128)(4,1)} %bitcast.97), calls=%async_computation.3 | async-start | bytes 1441792
  527.2 7.3 %slice-start = ((s8[4915200]{0:T(1024)(128)(4,1)}), s8[4194304]{0:T(1024)(128)(4,1)S(1)}, s32[]{:S(2)}) async-start(s8[4915200]{0:T(1024)(128)(4,1)} %bitcast.95), calls=%async_computation | async-start | bytes 8388608
  528.9 5.6 %slice-start.1 = ((s8[4915200]{0:T(1024)(128)(4,1)}), s8[720896]{0:T(1024)(128)(4,1)S(1)}, s32[]{:S(2)}) async-start(s8[4915200]{0:T(1024)(128)(4,1)} %bitcast.95), calls=%async_computation.1 | async-start | bytes 1441792
  528.9 5.6 %copy-start.1 = (bf16[192,6656]{1,0:T(8,128)(2,1)S(1)}, bf16[192,6656]{1,0:T(8,128)(2,1)}, u32[]{:S(2)}) copy-start(bf16[192,6656]{1,0:T(8,128)(2,1)} %get-tuple-element.293) | copy-start | bytes 7667716

commit v8 on v7

--- a/solution.py
+++ b/solution.py
@@ -266,7 +266,9 @@
         mix_copy(step).wait()
     x_ref[...] = turned[...].reshape(nb * width, SEQ_LEN).T
     if first:
-        gather.finish()
+        gather.last_hop()
+        for w in range(len(shards)):
+            gather.finish(w)
     if split:
         quarter_keep().wait()
         for step in range(1, nb):
@@ -345,16 +347,17 @@
                 self.copy(w, k + 2).start()
                 self.pair(w, k).start()
 
-    def finish(self):
+    def last_hop(self):
         for w in range(len(self.shards)):
             for k in range(2 if self.nb == 4 else 0, len(self.routes(w))):
                 self.copy(w, k).wait_recv()
                 self.pair(w, k).start()
-        for w in range(len(self.shards)):
-            self.own_copy(w).wait()
-            for k in range(len(self.routes(w))):
-                self.copy(w, k).wait_send()
-                self.pair(w, k).wait()
+
+    def finish(self, w):
+        self.own_copy(w).wait()
+        for k in range(len(self.routes(w))):
+            self.copy(w, k).wait_send()
+            self.pair(w, k).wait()
 
 
 def embed(nb, nv, cap, rows, turn, tok, table, shards=(), targets=None):
@@ -437,11 +440,43 @@
             self.pair(w).start()
             self.load(w).start()
 
+    def flip(self, bits):
+        low, high = lax.rem(self.b, 2), self.b // 2
+        return (high if bits < 2 else 1 - high) * 2 + (low if bits % 2 == 0 else 1 - low)
+
+    def rows_of(self, w, owner, top, size):
+        rows = self.own[w].shape[0] // self.nb
+        return pl.ds(pl.multiple_of(owner * rows + top, 16), size)
+
     def mix(self, w, step):
-        other = lax.rem(self.b + step, self.nb)
         rows = self.own[w].shape[0] // self.nb
-        source = self.own[w].at[pl.ds(pl.multiple_of(other * rows, 16), rows), :]
+        other = self.flip(step) if self.nb == 4 else lax.rem(self.b + step, self.nb)
+        source = self.own[w].at[self.rows_of(w, other, 0, rows), :]
         return send(source, self.shard[w].at[step], self.mix_out.at[w, step], self.mix_in.at[w, step], {"batch": other})
+
+    def corner(self, w, way):
+        half = self.own[w].shape[0] // self.nb // 2
+        cut = pl.ds((way - 1) * half, half)
+        source = self.own[w].at[self.rows_of(w, self.flip(3), (way - 1) * half, half), :]
+        at = 3 * (way - 1)
+        return send(
+            source, self.shard[w].at[3, cut, :], self.mix_out.at[w, at], self.mix_in.at[w, at], {"batch": self.flip(way)}
+        )
+
+    def relay(self, w):
+        if self.nb != 4:
+            return
+        half = self.own[w].shape[0] // self.nb // 2
+        for way in (1, 2):
+            self.corner(w, way).wait()
+            cut = pl.ds((way - 1) * half, half)
+            here = self.rows_of(w, self.flip(3 - way), (way - 1) * half, half)
+            self.own[w][here, :] = (self.own[w][here, :].astype(FL) + self.shard[w][3, cut, :].astype(FL)).astype(BF)
+        for step in (1, 2):
+            self.mix(w, step).start()
+
+    def steps(self):
+        return (1, 2) if self.nb == 4 else range(1, self.nb)
 
     def scatter(self, w):
         self.load(w).wait()
@@ -453,8 +488,12 @@
             self.own[w][cut, :] = (self.own[w][cut, :].astype(FL) + self.near[w][cut, :].astype(FL)).astype(BF)
 
         each(0, self.nb, add)
-        for step in range(1, self.nb):
-            self.mix(w, step).start()
+        if self.nb == 4:
+            for way in (1, 2):
+                self.corner(w, way).start()
+        else:
+            for step in self.steps():
+                self.mix(w, step).start()
 
     def pieces(self, w):
         rows = self.total[w].shape[0]
@@ -484,11 +523,11 @@
 
     def gather(self, w):
         rows = self.total[w].shape[0]
-        for step in range(1, self.nb):
+        for step in self.steps():
             self.mix(w, step).wait()
         here = pl.ds(pl.multiple_of(self.b * rows, 16), rows)
         value = self.own[w][here, :].astype(FL)
-        for step in range(1, self.nb):
+        for step in self.steps():
             value = value + self.shard[w][step].astype(FL)
         self.total[w][...] = value.astype(BF)
 
@@ -697,6 +736,7 @@
         layer.scatter(3)
     each(1, nv // 2 + 1, build)
     if first:
+        layer.relay(3)
         layer.collect(2)
     each(nv // 2 + 1, nv + 1, build)
     if first:
@@ -723,12 +763,14 @@
     if first:
         quarter = nv // 4
         each(0, quarter, take)
+        layer.relay(0)
         layer.reduce(3)
         layer.scatter(1)
         if split:
             for step in range(1, nb):
                 quarter_copy(step).start()
         each(quarter, 2 * quarter, take)
+        layer.relay(1)
         layer.reduce(0)
         each(2 * quarter, 3 * quarter, take)
         layer.collect(3)
@@ -855,8 +897,9 @@
 
 
 def attend_kernel(
-    nb, nv, x_ref, a_ref, seg_ref, pos_ref, p_ref, c_ref,
-    hall_ref, kv_ref, q_ref, hq_ref, xq_ref, o_ref, lse_ref, norm_ref, mixt_ref, p_all, c_all, *sems,
+    nb, nv, x_ref, a_ref, seg_ref, pos_ref, p_ref, c_ref, u_ref,
+    hall_ref, kv_ref, q_ref, hq_ref, o_ref, lse_ref, norm_ref, mixt_ref, p_all, c_all,
+    x1_ref, h2_ref, z_ref, act_ref, x2_ref, f_ref, *sems,
 ):
     meet((("batch", nb), ("vocab", nv)))
     gather = WeightGather(nb, (p_ref, c_ref), (p_all, c_all), *sems)
@@ -881,7 +924,7 @@
     each(0, KEYS // BLK, project)
     pick = (pos_ref[...] == iota((SEQ_LEN, PICKS), 0)).astype(FL).astype(BF).T
     hq_ref[...] = nn(pick, normed).astype(BF)
-    xq_ref[...] = nn(pick, x_ref[...])
+    x1_ref[...] = nn(pick, x_ref[...])
     q_ref[...] = nn(hq_ref[...], a_ref[:, :D]).astype(BF)
     visible = visible_keys(seg_ref, pos_ref)
 
@@ -902,26 +945,28 @@
 
     gather.pass_on()
     each(0, NPAIR, attend)
-    gather.finish()
-
-
-def feed_kernel(xq_ref, o_ref, p_ref, u_ref, c_ref, norm_ref, x1_ref, h2_ref, z_ref, act_ref, x2_ref, f_ref):
-    x1 = xq_ref[...] + nn(o_ref[...], p_ref[...])
+    gather.last_hop()
+    gather.finish(0)
+    x1 = x1_ref[...] + nn(o_ref[...], p_all[...])
     x1_ref[...] = x1
     unit, _ = standard(x1)
     h2 = (unit * norm_ref[1:2, :] + norm_ref[4:5, :]).astype(BF)
     h2_ref[...] = h2
     x2_ref[...] = x1
 
-    def piece(j):
+    def expand(j):
         cut = lanes(j * D, D)
         z = nn(h2, u_ref[:, cut])
         z_ref[:, cut] = z
-        act = jax.nn.gelu(z, approximate=True).astype(BF)
-        act_ref[:, cut] = act
-        x2_ref[...] += nn(act, c_ref[pl.ds(j * D, D), :])
-
-    each(0, FF // D, piece)
+        act_ref[:, cut] = jax.nn.gelu(z, approximate=True).astype(BF)
+
+    each(0, FF // D, expand)
+    gather.finish(1)
+
+    def contract(j):
+        x2_ref[...] += nn(act_ref[:, lanes(j * D, D)], c_all[pl.ds(j * D, D), :])
+
+    each(0, FF // D, contract)
     unit, _ = standard(x2_ref[...])
     f_ref[...] = (unit * norm_ref[2:3, :] + norm_ref[5:6, :]).astype(BF)
 
@@ -996,6 +1041,7 @@
     each(0, NPAIR // 2, attend)
     layer.scatter(0)
     each(NPAIR // 2, NPAIR, attend)
+    layer.relay(0)
     da_ref[:, :D] = nn(hq_ref[...].T, dq[...]).astype(BF)
 
     def turn(i):
@@ -1679,27 +1725,18 @@
 
     x = lax.while_loop(lambda state: state[0] < turns, more_rows, (jnp.int32(1), x))[1]
 
-    hall, kv, q, hq, xq, mixed, lse, norm_rows, mixing_t, p_all, c_all = run(
+    hall, kv, q, hq, mixed, lse, norm_rows, mixing_t, p_all, c_all, x1, h2, z, act, x2, features = run(
         functools.partial(attend_kernel, nb, nv),
         [
-            SD((KEYS, D), BF), SD((KEYS, 2 * D), BF), SD((PICKS, D), BF), SD((PICKS, D), BF), SD((PICKS, D), FL),
+            SD((KEYS, D), BF), SD((KEYS, 2 * D), BF), SD((PICKS, D), BF), SD((PICKS, D), BF),
             SD((PICKS, D), BF), SD((NPAIR, 2, PICKS), FL), SD((8, D), FL), SD((SEQ_LEN, SLOTS * NB), BF),
             SD((D, D), BF), SD((FF, D), BF),
-        ],
-        weight_semaphores(2),
-        [x, a_all, seg_row, pos_row, pieces[1], pieces[3]],
-        "attend", 6, flops=7 * 10**9, moved=20 * 10**6,
-        out_specs=[VM] * 9 + [HB] * 2,
-    )
-    x1, h2, z, act, x2, features = run(
-        feed_kernel,
-        [
             SD((PICKS, D), FL), SD((PICKS, D), BF), SD((PICKS, FF), FL), SD((PICKS, FF), BF), SD((PICKS, D), FL),
             SD((PICKS, D), BF),
         ],
-        [],
-        [xq, mixed, p_all, u_all, c_all, norm_rows],
-        "feed", flops=2 * 10**9, moved=15 * 10**6,
+        weight_semaphores(2),
+        [x, a_all, seg_row, pos_row, pieces[1], pieces[3], u_all],
+        "attend", 6, flops=9 * 10**9, moved=30 * 10**6,
     )
     if split:
         live = jnp.pad(vocab_mask, (0, nb * quarter - rows))[None, :]

time: 552 us -> 558 us (1.011)
  loops' own time: 0.45 us -> 9.1 us
    another operation x1, loops' own time: 0.22 us -> 8.87 us  [shards(): lax.while_loop(lambda state: state[0] < turns, more_rows, (jnp.int32(1), x))]
    pallas_call x7 -> x6, Pallas kernels: 495 us -> 493 us  [run(): pl.pallas_call(kernel, out_shape=outs, in_specs=in_specs if in_specs is n...]
where the time goes in v8:
time: 558 us; the launch traced here: 553 us
  Pallas kernels  493 us (88%)
  other arithmetic  40.1 us (7%)
  loops' own time  9.1 us (2%)
  local copies, waits for them, and re-layouts  5.96 us (1%)
    pallas_call x6, Pallas kernels, run(): pl.pallas_call(kernel, out_shape=outs, in_specs=in_specs if in_specs is n...  493 us
    sub x5, other arithmetic, adamw(): weight - rate * (fixed_moment / (jnp.sqrt(fixed_square) + ADAM_EPS) + dec...  20 us

profile of v8, /device:TPU:0, one launch (start us, length us, event | category | flops | bytes accessed | tf_op | source)
XLA Modules:
  0.0 552.7 jit_solution(5717764615854068115)
XLA Ops:
  0.7 2.6 bitcast_convert_fusion
  3.3 0.0 copy-start.15
  3.3 1.6 pad.8.refs_2_
  5.0 0.0 copy-done.15
  5.0 0.0 copy-start.2
  5.0 1.7 convert_bitcast_fusion.3
  6.8 0.1 copy.64
  6.9 1.1 concatenate.9.refs_3_
  8.1 0.0 copy-done.2
  8.1 1.2 convert_bitcast_fusion.2.refs_4_
  9.2 103.1 %embed.1 = (bf16[1024,768]{1,0:T(8,128)(2,1)S(1)}, s32[8,768,1]{2,1,0:T(8,128)}, s32[4,8,1024]{2,1,0:T(8,128)S(1)}, s32[1]{0:T(128)}, s32[4,8,1024]{2,1,0:T(8,12...) custom-call(s32[1]{0:T(128)} %constant.55.clone.1.refs_0_, ...), custom_call_target="tpu_custom_call" | custom-call | tf_op jit(solution)/shard_map/embed/pallas_call | solution.py:68
  113.0 8.9 %while.23 = (s32[]{:T(128)}, bf16[1024,768]{1,0:T(8,128)(2,1)S(1)}, s32[]{:T(128)}, s32[8,1024]{1,0:T(8,128)S(1)}, bf16[192,6656]{1,0:T(8,128)(2,1)}, /*index=5*/s32[]{:T(128)}) while((s32[]{:T(128)}, bf16[1024,768]{1,0:T(8,128)(2,1)S(1)}, s32[]{:T(128)}, s32[8,1024]{1,0:T(8,128)S(1)}, bf16[192,6656]{1,0:T(8,128)(2,1)}, ...), condition=%wide.region_1.2_spmd, body=%wide.region_0.1_spmd.sunk | while | flops 786434 | bytes 4718661 | solution.py:1726
  121.8 0.0 copy-start
  121.9 0.0 copy-start.9
  121.9 3.4 convert_bitcast_fusion.1.c_ref
  125.3 0.7 convert_bitcast_fusion.4.p_ref
  126.0 45.5 %attend.1 = (bf16[1536,768]{1,0:T(8,128)(2,1)}, bf16[1536,1536]{1,0:T(8,128)(2,1)}, bf16[128,768]{1,0:T(8,128)(2,1)}, bf16[128,768]{1,0:T(8,128)(2,1)}, bf16[128...) custom-call(bf16[1024,768]{1,0:T(8,128)(2,1)S(1)} %get-tuple-element, ...), custom_call_target="tpu_custom_call" | custom-call | flops 8999999488 | bytes 30000000 | tf_op jit(solution)/shard_map/attend/pallas_call | solution.py:68
  171.5 0.0 copy-done
  171.6 0.0 copy-done.16
  171.6 0.6 broadcast_in_dim.50.live_ref
  172.2 121.2 %wide_head.1 = (f32[128,768]{1,0:T(8,128)}, bf16[768,1664]{1,0:T(8,128)(2,1)}, f32[8,128]{1,0:T(8,128)S(1)}) custom-call(bf16[128,768]{1,0:T(8,128)(2,1)} %get-tuple-element.255.f_ref, bf16[768,1664]{1,0:T(8,128)(2,1)} %get-tuple-element.256.w_ref, s32[1,6656]{1,0:T(1,128)} %broadcast_in_dim.50.live_ref, s32[4,1,1024]{2,1,0:T(1,128)} %get-tuple-element.257.target_ref), custom_call_target="tpu_custom_call" | custom-call | tf_op jit(solution)/shard_map/wide_head/pallas_call | solution.py:68
  293.4 15.6 %feed_back.1 = (bf16[3072,768]{1,0:T(8,128)(2,1)}, bf16[768,3072]{1,0:T(8,128)(2,1)}, bf16[768,768]{1,0:T(8,128)(2,1)}, f32[128,768]{1,0:T(8,128)}, bf16[128,768]{1,0:T(8,128)(2,1)}, /*index=5*/f32[8,768]{1,0:T(8,128)}) custom-call(f32[128,768]{1,0:T(8,128)} %get-tuple-element.258.df_ref, f32[128,768]{1,0:T(8,128)} %get-tuple-element.259.x2_ref, ...), custom_call_target="tpu_custom_call" | custom-call | flops 4000000000 | bytes 30000000 | tf_op jit(solution)/shard_map/feed_back/pallas_call | solution.py:68
  309.0 49.0 %attend_back.1 = (bf16[768,2560]{1,0:T(8,128)(2,1)}, bf16[1024,768]{1,0:T(8,128)(2,1)S(1)}, bf16[192,1536]{1,0:T(8,128)(2,1)}) custom-call(bf16[128,768]{1,0:T(8,128)(2,1)} %get-tuple-element.268.do_ref, bf16[128,768]{1,0:T(8,128)(2,1)} %get-tuple-element.269.q_ref, bf16[1536,1536]{1,0:T(8,128)(2,1)} %get-tuple-element.270.kv_ref, ...), custom_call_target="tpu_custom_call" | custom-call | flops 12000000000 | bytes 25000000 | tf_op jit(solution)/shard_map/attend_back/pallas_call | solution.py:68
  358.0 0.0 copy-start.24
  358.0 158.6 %unembed.1 = (f32[192,6400]{1,0:T(8,128)}, bf16[192,2560]{1,0:T(8,128)(2,1)}, bf16[192,768]{1,0:T(8,128)(2,1)}, bf16[192,3072]{1,0:T(8,128)(2,1)}, bf16[768,768]...) custom-call(bf16[1024,768]{1,0:T(8,128)(2,1)S(1)} %get-tuple-element.489.refs_0_, ...), custom_call_target="tpu_custom_call" | custom-call | tf_op jit(solution)/shard_map/unembed/pallas_call | solution.py:68
  516.6 0.2 while.24
  516.9 0.0 copy-start.20
  516.9 0.0 copy-start.21
  516.9 0.0 copy-start.22
  516.9 0.0 copy-start.23
  516.9 0.5 fusion.23
  519.0 0.6 multiply_subtract_fusion.4
  519.6 0.0 copy-start.8
  519.6 0.0 slice-start.4
  519.6 7.9 %multiply_subtract_fusion = (f32[1,768,768]{2,1,0:T(8,128)}, f32[1,768,768]{2,1,0:T(8,128)}, f32[1,768,768]{2,1,0:T(8,128)}) fusion(f32[1,768,768]{2,1,0:T(8,128)} %param.52, f32[]{:T(128)} %bitcast.17, f32[]{:T(128)} %bitcast.15, f32[]{:T(128)S(6)} %min.14, bf16[768,768]{1,0:T(8,128)(2,1)} %get-tuple-element.295, f32[1,768,768]{2,1,0:T(8,128)} %param.54, ...), kind=kLoop, calls=%fused_computation.29 | loop fusion | flops 10027008 | bytes 15335436 | tf_op jit(solution)/shard_map/sub | solution.py:1680
  527.6 0.0 copy-start.10
  527.6 0.0 copy-start.13
  527.6 0.0 copy-start.14
  527.7 0.0 copy-start.11
  527.7 0.0 slice-start.2
  527.7 0.0 slice-start.5
  527.7 4.4 multiply_subtract_fusion.1
  532.1 0.0 slice-start.3
  532.1 1.5 multiply_subtract_fusion.3
  533.6 1.5 copy-done.4
  535.1 0.3 copy-done.6
  535.3 5.6 %multiply_subtract_fusion.2 = (f32[1,192,2304]{2,1,0:T(8,128)}, f32[1,192,2304]{2,1,0:T(8,128)}, f32[1,192,2304]{2,1,0:T(8,128)}) fusion(f32[1,192,2304]{2,1,0:T(8,128)S(1)} %copy-done.4, f32[]{:T(128)} %bitcast.17, f32[]{:T(128)} %bitcast.15, f32[]{:T(128)S(6)} %min.14, bf16[192,2560]{1,0:T(8,128)(2,1)S(1)} %copy-done.6, f32[1,192,2304]{2,1,0:T(8,128)S(1)} %copy-done.11, ...), kind=kLoop, calls=%fused_computation.36 | loop fusion | flops 7520256 | bytes 11501580 | tf_op jit(solution)/shard_map/sub | solution.py:1680
  541.0 10.3 %fusion.16 = (f32[6400,192]{0,1:T(8,128)}, f32[6400,192]{0,1:T(8,128)}, f32[6400,192]{0,1:T(8,128)}) fusion(f32[]{:T(128)S(6)} %min.14, f32[192,6400]{1,0:T(8,128)S(1)} %bitcast.96, bf16[192,6656]{1,0:T(8,128)(2,1)S(1)} %copy-done.1, f32[6400,192]{0,1:T(8,128)S(1)} %bitcast.100, f32[]{:T(128)} %bitcast.17, f32[]{:T(128)} %bitcast.15, f32[6400,192]{0,1:T(8,128)} %param.41, ...), kind=kLoop, calls=%fused_computation.60 | loop fusion | flops 22118400 | bytes 36864012 | tf_op jit(solution)/shard_map/transpose | solution.py:1800
  (48 shorter events, 0.1 us)
Async XLA Ops:
  3.3 1.7 copy-start.15
  5.0 1.8 copy-start.18
  5.0 1.8 copy-start.17
  5.0 3.1 copy-start.2
  121.8 49.7 %copy-start = (bf16[1024,768]{1,0:T(8,128)(2,1)}, bf16[1024,768]{1,0:T(8,128)(2,1)S(1)}, u32[]{:S(2)}) copy-start(bf16[1024,768]{1,0:T(8,128)(2,1)S(1)} %get-tuple-element.252.x_ref) | copy-start | bytes 4718596
  121.9 3.4 copy-start.9
  126.0 45.6 %copy-start.16 = (s32[6400]{0:T(1024)S(1)}, s32[6400]{0:T(1024)}, u32[]{:S(2)}) copy-start(s32[6400]{0:T(1024)} %param.38) | copy-start | bytes 76804
  358.0 158.6 %copy-start.24 = (s32[8]{0:T(128)S(1)}, s32[8]{0:T(128)}, u32[]{:S(2)}) copy-start(s32[8]{0:T(128)} %constant.132.clone..sunk.2) | copy-start | bytes 100
  516.9 2.1 copy-start.19
  516.9 2.1 copy-start.20
  516.9 2.1 copy-start.21
  516.9 2.1 copy-start.22
  516.9 2.1 copy-start.23
  519.6 8.0 %copy-start.3 = (f32[1,192,3072]{2,1,0:T(8,128)S(1)}, f32[1,192,3072]{2,1,0:T(8,128)}, u32[]{:S(2)}) copy-start(f32[1,192,3072]{2,1,0:T(8,128)} %param.49) | copy-start | bytes 7077892
  519.6 8.0 %copy-start.5 = (bf16[192,3072]{1,0:T(8,128)(2,1)S(1)}, bf16[192,3072]{1,0:T(8,128)(2,1)}, u32[]{:S(2)}) copy-start(bf16[192,3072]{1,0:T(8,128)(2,1)} %get-tuple-element.294) | copy-start | bytes 3538948
  519.6 8.0 %copy-start.7 = (f32[1,192,3072]{2,1,0:T(8,128)S(1)}, f32[1,192,3072]{2,1,0:T(8,128)}, u32[]{:S(2)}) copy-start(f32[1,192,3072]{2,1,0:T(8,128)} %param.51) | copy-start | bytes 7077892
  519.6 8.0 %copy-start.8 = (f32[1,192,3072]{2,1,0:T(8,128)S(1)}, f32[1,192,3072]{2,1,0:T(8,128)}, u32[]{:S(2)}) copy-start(f32[1,192,3072]{2,1,0:T(8,128)} %param.50) | copy-start | bytes 7077892
  519.6 21.3 %slice-start.4 = ((s8[4915200]{0:T(1024)(128)(4,1)}), s8[4194304]{0:T(1024)(128)(4,1)S(1)}, s32[]{:S(2)}) async-start(s8[4915200]{0:T(1024)(128)(4,1)} %bitcast.99), calls=%async_computation.4 | async-start | bytes 8388608
  527.6 4.5 copy-start.10
  527.6 4.5 copy-start.12
  527.6 4.5 copy-start.13
  527.6 4.5 copy-start.14
  527.7 6.0 %copy-start.11 = (f32[1,192,2304]{2,1,0:T(8,128)S(1)}, f32[1,192,2304]{2,1,0:T(8,128)}, u32[]{:S(2)}) copy-start(f32[1,192,2304]{2,1,0:T(8,128)} %param.45) | copy-start | bytes 5308420
  527.7 13.3 %slice-start.2 = ((s8[4915200]{0:T(1024)(128)(4,1)}), s8[4194304]{0:T(1024)(128)(4,1)S(1)}, s32[]{:S(2)}) async-start(s8[4915200]{0:T(1024)(128)(4,1)} %bitcast.97), calls=%async_computation.2 | async-start | bytes 8388608
  527.7 13.3 %slice-start.5 = ((s8[4915200]{0:T(1024)(128)(4,1)}), s8[720896]{0:T(1024)(128)(4,1)S(1)}, s32[]{:S(2)}) async-start(s8[4915200]{0:T(1024)(128)(4,1)} %bitcast.99), calls=%async_computation.5 | async-start | bytes 1441792
  532.1 3.0 copy-start.4
  532.1 3.3 copy-start.6
  532.1 8.8 %slice-start.3 = ((s8[4915200]{0:T(1024)(128)(4,1)}), s8[720896]{0:T(1024)(128)(4,1)S(1)}, s32[]{:S(2)}) async-start(s8[4915200]{0:T(1024)(128)(4,1)} %bitcast.97), calls=%async_computation.3 | async-start | bytes 1441792
  533.6 7.3 %slice-start = ((s8[4915200]{0:T(1024)(128)(4,1)}), s8[4194304]{0:T(1024)(128)(4,1)S(1)}, s32[]{:S(2)}) async-start(s8[4915200]{0:T(1024)(128)(4,1)} %bitcast.95), calls=%async_computation | async-start | bytes 8388608
  535.3 5.6 %slice-start.1 = ((s8[4915200]{0:T(1024)(128)(4,1)}), s8[720896]{0:T(1024)(128)(4,1)S(1)}, s32[]{:S(2)}) async-start(s8[4915200]{0:T(1024)(128)(4,1)} %bitcast.95), calls=%async_computation.1 | async-start | bytes 1441792
  535.3 5.6 %copy-start.1 = (bf16[192,6656]{1,0:T(8,128)(2,1)S(1)}, bf16[192,6656]{1,0:T(8,128)(2,1)}, u32[]{:S(2)}) copy-start(bf16[192,6656]{1,0:T(8,128)(2,1)} %get-tuple-element.291) | copy-start | bytes 7667716

commit v9 on v8

--- a/solution.py
+++ b/solution.py
@@ -440,43 +440,11 @@
             self.pair(w).start()
             self.load(w).start()
 
-    def flip(self, bits):
-        low, high = lax.rem(self.b, 2), self.b // 2
-        return (high if bits < 2 else 1 - high) * 2 + (low if bits % 2 == 0 else 1 - low)
-
-    def rows_of(self, w, owner, top, size):
+    def mix(self, w, step):
+        other = lax.rem(self.b + step, self.nb)
         rows = self.own[w].shape[0] // self.nb
-        return pl.ds(pl.multiple_of(owner * rows + top, 16), size)
-
-    def mix(self, w, step):
-        rows = self.own[w].shape[0] // self.nb
-        other = self.flip(step) if self.nb == 4 else lax.rem(self.b + step, self.nb)
-        source = self.own[w].at[self.rows_of(w, other, 0, rows), :]
+        source = self.own[w].at[pl.ds(pl.multiple_of(other * rows, 16), rows), :]
         return send(source, self.shard[w].at[step], self.mix_out.at[w, step], self.mix_in.at[w, step], {"batch": other})
-
-    def corner(self, w, way):
-        half = self.own[w].shape[0] // self.nb // 2
-        cut = pl.ds((way - 1) * half, half)
-        source = self.own[w].at[self.rows_of(w, self.flip(3), (way - 1) * half, half), :]
-        at = 3 * (way - 1)
-        return send(
-            source, self.shard[w].at[3, cut, :], self.mix_out.at[w, at], self.mix_in.at[w, at], {"batch": self.flip(way)}
-        )
-
-    def relay(self, w):
-        if self.nb != 4:
-            return
-        half = self.own[w].shape[0] // self.nb // 2
-        for way in (1, 2):
-            self.corner(w, way).wait()
-            cut = pl.ds((way - 1) * half, half)
-            here = self.rows_of(w, self.flip(3 - way), (way - 1) * half, half)
-            self.own[w][here, :] = (self.own[w][here, :].astype(FL) + self.shard[w][3, cut, :].astype(FL)).astype(BF)
-        for step in (1, 2):
-            self.mix(w, step).start()
-
-    def steps(self):
-        return (1, 2) if self.nb == 4 else range(1, self.nb)
 
     def scatter(self, w):
         self.load(w).wait()
@@ -488,12 +456,8 @@
             self.own[w][cut, :] = (self.own[w][cut, :].astype(FL) + self.near[w][cut, :].astype(FL)).astype(BF)
 
         each(0, self.nb, add)
-        if self.nb == 4:
-            for way in (1, 2):
-                self.corner(w, way).start()
-        else:
-            for step in self.steps():
-                self.mix(w, step).start()
+        for step in range(1, self.nb):
+            self.mix(w, step).start()
 
     def pieces(self, w):
         rows = self.total[w].shape[0]
@@ -523,11 +487,11 @@
 
     def gather(self, w):
         rows = self.total[w].shape[0]
-        for step in self.steps():
+        for step in range(1, self.nb):
             self.mix(w, step).wait()
         here = pl.ds(pl.multiple_of(self.b * rows, 16), rows)
         value = self.own[w][here, :].astype(FL)
-        for step in self.steps():
+        for step in range(1, self.nb):
             value = value + self.shard[w][step].astype(FL)
         self.total[w][...] = value.astype(BF)
 
@@ -736,7 +700,6 @@
         layer.scatter(3)
     each(1, nv // 2 + 1, build)
     if first:
-        layer.relay(3)
         layer.collect(2)
     each(nv // 2 + 1, nv + 1, build)
     if first:
@@ -763,14 +726,12 @@
     if first:
         quarter = nv // 4
         each(0, quarter, take)
-        layer.relay(0)
         layer.reduce(3)
         layer.scatter(1)
         if split:
             for step in range(1, nb):
                 quarter_copy(step).start()
         each(quarter, 2 * quarter, take)
-        layer.relay(1)
         layer.reduce(0)
         each(2 * quarter, 3 * quarter, take)
         layer.collect(3)
@@ -1041,7 +1002,6 @@
     each(0, NPAIR // 2, attend)
     layer.scatter(0)
     each(NPAIR // 2, NPAIR, attend)
-    layer.relay(0)
     da_ref[:, :D] = nn(hq_ref[...].T, dq[...]).astype(BF)
 
     def turn(i):

time: 558 us -> 557 us (level)
  no operation moved by 1% of the time
where the time goes in v9:
time: 557 us; the launch traced here: 551 us
  Pallas kernels  491 us (88%)
  other arithmetic  40.1 us (7%)
  loops' own time  9.1 us (2%)
  local copies, waits for them, and re-layouts  5.96 us (1%)
    pallas_call x6, Pallas kernels, run(): pl.pallas_call(kernel, out_shape=outs, in_specs=in_specs if in_specs is n...  491 us
    sub x5, other arithmetic, adamw(): weight - rate * (fixed_moment / (jnp.sqrt(fixed_square) + ADAM_EPS) + dec...  20 us

profile of v9, /device:TPU:0, one launch (start us, length us, event | category | flops | bytes accessed | tf_op | source)
XLA Modules:
  0.0 550.7 jit_solution(18281396095551994825)
XLA Ops:
  0.7 2.6 bitcast_convert_fusion
  3.3 0.0 copy-start.15
  3.3 1.6 pad.8.refs_2_
  5.0 0.0 copy-start.2
  5.0 1.7 convert_bitcast_fusion.3
  6.8 0.1 copy.64
  6.9 1.1 concatenate.9.refs_3_
  8.1 1.2 convert_bitcast_fusion.2.refs_4_
  9.2 103.1 %embed.1 = (bf16[1024,768]{1,0:T(8,128)(2,1)S(1)}, s32[8,768,1]{2,1,0:T(8,128)}, s32[4,8,1024]{2,1,0:T(8,128)S(1)}, s32[1]{0:T(128)}, s32[4,8,1024]{2,1,0:T(8,12...) custom-call(s32[1]{0:T(128)} %constant.55.clone.1.refs_0_, ...), custom_call_target="tpu_custom_call" | custom-call | tf_op jit(solution)/shard_map/embed/pallas_call | solution.py:68
  113.0 8.9 %while.23 = (s32[]{:T(128)}, bf16[1024,768]{1,0:T(8,128)(2,1)S(1)}, s32[]{:T(128)}, s32[8,1024]{1,0:T(8,128)S(1)}, bf16[192,6656]{1,0:T(8,128)(2,1)}, /*index=5*/s32[]{:T(128)}) while((s32[]{:T(128)}, bf16[1024,768]{1,0:T(8,128)(2,1)S(1)}, s32[]{:T(128)}, s32[8,1024]{1,0:T(8,128)S(1)}, bf16[192,6656]{1,0:T(8,128)(2,1)}, ...), condition=%wide.region_1.2_spmd, body=%wide.region_0.1_spmd.sunk | while | flops 786434 | bytes 4718661 | solution.py:1686
  121.8 0.0 copy-start
  121.9 0.0 copy-start.9
  121.9 3.4 convert_bitcast_fusion.1.c_ref
  125.3 0.7 convert_bitcast_fusion.4.p_ref
  126.0 45.5 %attend.1 = (bf16[1536,768]{1,0:T(8,128)(2,1)}, bf16[1536,1536]{1,0:T(8,128)(2,1)}, bf16[128,768]{1,0:T(8,128)(2,1)}, bf16[128,768]{1,0:T(8,128)(2,1)}, bf16[128...) custom-call(bf16[1024,768]{1,0:T(8,128)(2,1)S(1)} %get-tuple-element, ...), custom_call_target="tpu_custom_call" | custom-call | flops 8999999488 | bytes 30000000 | tf_op jit(solution)/shard_map/attend/pallas_call | solution.py:68
  171.6 0.6 broadcast_in_dim.50.live_ref
  172.2 121.2 %wide_head.1 = (f32[128,768]{1,0:T(8,128)}, bf16[768,1664]{1,0:T(8,128)(2,1)}, f32[8,128]{1,0:T(8,128)S(1)}) custom-call(bf16[128,768]{1,0:T(8,128)(2,1)} %get-tuple-element.255.f_ref, bf16[768,1664]{1,0:T(8,128)(2,1)} %get-tuple-element.256.w_ref, s32[1,6656]{1,0:T(1,128)} %broadcast_in_dim.50.live_ref, s32[4,1,1024]{2,1,0:T(1,128)} %get-tuple-element.257.target_ref), custom_call_target="tpu_custom_call" | custom-call | tf_op jit(solution)/shard_map/wide_head/pallas_call | solution.py:68
  293.4 15.6 %feed_back.1 = (bf16[3072,768]{1,0:T(8,128)(2,1)}, bf16[768,3072]{1,0:T(8,128)(2,1)}, bf16[768,768]{1,0:T(8,128)(2,1)}, f32[128,768]{1,0:T(8,128)}, bf16[128,768]{1,0:T(8,128)(2,1)}, /*index=5*/f32[8,768]{1,0:T(8,128)}) custom-call(f32[128,768]{1,0:T(8,128)} %get-tuple-element.258.df_ref, f32[128,768]{1,0:T(8,128)} %get-tuple-element.259.x2_ref, ...), custom_call_target="tpu_custom_call" | custom-call | flops 4000000000 | bytes 30000000 | tf_op jit(solution)/shard_map/feed_back/pallas_call | solution.py:68
  309.0 47.1 %attend_back.1 = (bf16[768,2560]{1,0:T(8,128)(2,1)}, bf16[1024,768]{1,0:T(8,128)(2,1)S(1)}, bf16[192,1536]{1,0:T(8,128)(2,1)}) custom-call(bf16[128,768]{1,0:T(8,128)(2,1)} %get-tuple-element.268.do_ref, bf16[128,768]{1,0:T(8,128)(2,1)} %get-tuple-element.269.q_ref, bf16[1536,1536]{1,0:T(8,128)(2,1)} %get-tuple-element.270.kv_ref, ...), custom_call_target="tpu_custom_call" | custom-call | flops 12000000000 | bytes 25000000 | tf_op jit(solution)/shard_map/attend_back/pallas_call | solution.py:68
  356.1 0.0 copy-start.24
  356.1 158.5 %unembed.1 = (f32[192,6400]{1,0:T(8,128)}, bf16[192,2560]{1,0:T(8,128)(2,1)}, bf16[192,768]{1,0:T(8,128)(2,1)}, bf16[192,3072]{1,0:T(8,128)(2,1)}, bf16[768,768]...) custom-call(bf16[1024,768]{1,0:T(8,128)(2,1)S(1)} %get-tuple-element.489.refs_0_, ...), custom_call_target="tpu_custom_call" | custom-call | tf_op jit(solution)/shard_map/unembed/pallas_call | solution.py:68
  514.6 0.2 while.24
  514.9 0.0 copy-start.20
  514.9 0.0 copy-start.21
  514.9 0.0 copy-start.22
  514.9 0.0 copy-start.23
  514.9 0.5 fusion.23
  517.0 0.6 multiply_subtract_fusion.4
  517.6 0.0 copy-start.8
  517.6 0.0 slice-start.4
  517.7 7.9 %multiply_subtract_fusion = (f32[1,768,768]{2,1,0:T(8,128)}, f32[1,768,768]{2,1,0:T(8,128)}, f32[1,768,768]{2,1,0:T(8,128)}) fusion(f32[1,768,768]{2,1,0:T(8,128)} %param.52, f32[]{:T(128)} %bitcast.17, f32[]{:T(128)} %bitcast.15, f32[]{:T(128)S(6)} %min.14, bf16[768,768]{1,0:T(8,128)(2,1)} %get-tuple-element.295, f32[1,768,768]{2,1,0:T(8,128)} %param.54, ...), kind=kLoop, calls=%fused_computation.29 | loop fusion | flops 10027008 | bytes 15335436 | tf_op jit(solution)/shard_map/sub | solution.py:1640
  525.6 0.0 copy-done.3
  525.6 0.0 copy-start.10
  525.6 0.0 copy-start.13
  525.6 0.0 copy-start.14
  525.7 0.0 copy-start.11
  525.7 0.0 slice-start.2
  525.7 0.0 slice-start.5
  525.7 4.4 multiply_subtract_fusion.1
  530.1 0.0 copy-done.12
  530.1 0.0 slice-start.3
  530.1 1.5 multiply_subtract_fusion.3
  531.6 1.5 copy-done.4
  533.1 0.3 copy-done.6
  533.3 5.6 %multiply_subtract_fusion.2 = (f32[1,192,2304]{2,1,0:T(8,128)}, f32[1,192,2304]{2,1,0:T(8,128)}, f32[1,192,2304]{2,1,0:T(8,128)}) fusion(f32[1,192,2304]{2,1,0:T(8,128)S(1)} %copy-done.4, f32[]{:T(128)} %bitcast.17, f32[]{:T(128)} %bitcast.15, f32[]{:T(128)S(6)} %min.14, bf16[192,2560]{1,0:T(8,128)(2,1)S(1)} %copy-done.6, f32[1,192,2304]{2,1,0:T(8,128)S(1)} %copy-done.11, ...), kind=kLoop, calls=%fused_computation.36 | loop fusion | flops 7520256 | bytes 11501580 | tf_op jit(solution)/shard_map/sub | solution.py:1640
  539.0 0.0 slice-done.3
  539.0 0.0 slice-done
  539.0 10.3 %fusion.16 = (f32[6400,192]{0,1:T(8,128)}, f32[6400,192]{0,1:T(8,128)}, f32[6400,192]{0,1:T(8,128)}) fusion(f32[]{:T(128)S(6)} %min.14, f32[192,6400]{1,0:T(8,128)S(1)} %bitcast.96, bf16[192,6656]{1,0:T(8,128)(2,1)S(1)} %copy-done.1, f32[6400,192]{0,1:T(8,128)S(1)} %bitcast.100, f32[]{:T(128)} %bitcast.17, f32[]{:T(128)} %bitcast.15, f32[6400,192]{0,1:T(8,128)} %param.41, ...), kind=kLoop, calls=%fused_computation.60 | loop fusion | flops 22118400 | bytes 36864012 | tf_op jit(solution)/shard_map/transpose | solution.py:1760
  (48 shorter events, 0.1 us)
Async XLA Ops:
  3.3 1.7 copy-start.15
  5.0 1.8 copy-start.18
  5.0 1.8 copy-start.17
  5.0 3.1 copy-start.2
  121.8 49.7 %copy-start = (bf16[1024,768]{1,0:T(8,128)(2,1)}, bf16[1024,768]{1,0:T(8,128)(2,1)S(1)}, u32[]{:S(2)}) copy-start(bf16[1024,768]{1,0:T(8,128)(2,1)S(1)} %get-tuple-element.252.x_ref) | copy-start | bytes 4718596
  121.9 3.4 copy-start.9
  126.0 45.6 %copy-start.16 = (s32[6400]{0:T(1024)S(1)}, s32[6400]{0:T(1024)}, u32[]{:S(2)}) copy-start(s32[6400]{0:T(1024)} %param.38) | copy-start | bytes 76804
  356.1 158.5 %copy-start.24 = (s32[8]{0:T(128)S(1)}, s32[8]{0:T(128)}, u32[]{:S(2)}) copy-start(s32[8]{0:T(128)} %constant.132.clone..sunk.2) | copy-start | bytes 100
  514.9 2.1 copy-start.19
  514.9 2.1 copy-start.20
  514.9 2.1 copy-start.21
  514.9 2.1 copy-start.22
  514.9 2.1 copy-start.23
  517.6 8.0 %copy-start.3 = (f32[1,192,3072]{2,1,0:T(8,128)S(1)}, f32[1,192,3072]{2,1,0:T(8,128)}, u32[]{:S(2)}) copy-start(f32[1,192,3072]{2,1,0:T(8,128)} %param.49) | copy-start | bytes 7077892
  517.6 8.0 %copy-start.5 = (bf16[192,3072]{1,0:T(8,128)(2,1)S(1)}, bf16[192,3072]{1,0:T(8,128)(2,1)}, u32[]{:S(2)}) copy-start(bf16[192,3072]{1,0:T(8,128)(2,1)} %get-tuple-element.294) | copy-start | bytes 3538948
  517.6 8.0 %copy-start.7 = (f32[1,192,3072]{2,1,0:T(8,128)S(1)}, f32[1,192,3072]{2,1,0:T(8,128)}, u32[]{:S(2)}) copy-start(f32[1,192,3072]{2,1,0:T(8,128)} %param.51) | copy-start | bytes 7077892
  517.6 8.0 %copy-start.8 = (f32[1,192,3072]{2,1,0:T(8,128)S(1)}, f32[1,192,3072]{2,1,0:T(8,128)}, u32[]{:S(2)}) copy-start(f32[1,192,3072]{2,1,0:T(8,128)} %param.50) | copy-start | bytes 7077892
  517.6 21.3 %slice-start.4 = ((s8[4915200]{0:T(1024)(128)(4,1)}), s8[4194304]{0:T(1024)(128)(4,1)S(1)}, s32[]{:S(2)}) async-start(s8[4915200]{0:T(1024)(128)(4,1)} %bitcast.99), calls=%async_computation.4 | async-start | bytes 8388608
  525.6 4.5 copy-start.10
  525.6 4.5 copy-start.12
  525.6 4.5 copy-start.13
  525.6 4.5 copy-start.14
  525.7 6.0 %copy-start.11 = (f32[1,192,2304]{2,1,0:T(8,128)S(1)}, f32[1,192,2304]{2,1,0:T(8,128)}, u32[]{:S(2)}) copy-start(f32[1,192,2304]{2,1,0:T(8,128)} %param.45) | copy-start | bytes 5308420
  525.7 13.3 %slice-start.2 = ((s8[4915200]{0:T(1024)(128)(4,1)}), s8[4194304]{0:T(1024)(128)(4,1)S(1)}, s32[]{:S(2)}) async-start(s8[4915200]{0:T(1024)(128)(4,1)} %bitcast.97), calls=%async_computation.2 | async-start | bytes 8388608
  525.7 13.3 %slice-start.5 = ((s8[4915200]{0:T(1024)(128)(4,1)}), s8[720896]{0:T(1024)(128)(4,1)S(1)}, s32[]{:S(2)}) async-start(s8[4915200]{0:T(1024)(128)(4,1)} %bitcast.99), calls=%async_computation.5 | async-start | bytes 1441792
  530.1 3.0 copy-start.4
  530.1 3.3 copy-start.6
  530.1 8.8 %slice-start.3 = ((s8[4915200]{0:T(1024)(128)(4,1)}), s8[720896]{0:T(1024)(128)(4,1)S(1)}, s32[]{:S(2)}) async-start(s8[4915200]{0:T(1024)(128)(4,1)} %bitcast.97), calls=%async_computation.3 | async-start | bytes 1441792
  531.6 7.3 %slice-start = ((s8[4915200]{0:T(1024)(128)(4,1)}), s8[4194304]{0:T(1024)(128)(4,1)S(1)}, s32[]{:S(2)}) async-start(s8[4915200]{0:T(1024)(128)(4,1)} %bitcast.95), calls=%async_computation | async-start | bytes 8388608
  533.3 5.6 %slice-start.1 = ((s8[4915200]{0:T(1024)(128)(4,1)}), s8[720896]{0:T(1024)(128)(4,1)S(1)}, s32[]{:S(2)}) async-start(s8[4915200]{0:T(1024)(128)(4,1)} %bitcast.95), calls=%async_computation.1 | async-start | bytes 1441792
  533.3 5.6 %copy-start.1 = (bf16[192,6656]{1,0:T(8,128)(2,1)S(1)}, bf16[192,6656]{1,0:T(8,128)(2,1)}, u32[]{:S(2)}) copy-start(bf16[192,6656]{1,0:T(8,128)(2,1)} %get-tuple-element.291) | copy-start | bytes 7667716
